TPU v7x, 128 devices: a whole 4x4x4 slice. The times are simulated.
128 devices in a mesh: req: 4 (over z), exp: 32 (over x, y, core).
Axes of the slice: x: 4, y: 4, z: 4, core: 2. Of those that a mesh axis runs over, the one named last changes fastest.
Arguments:
- attn_out: bfloat16 [16384, 2048], P(('req', 'exp')), may hold values from -6 to 6
- residual: bfloat16 [16384, 2048], P(('req', 'exp')), may hold values from -6 to 6
- out_weight: bfloat16 [2048, 2048], P('exp'), may hold values from -0.125 to 0.125
- norm_gain: float32 [2048], replicated, may hold values from 0.25 to 1.75
- expert_ids: int32 [16384, 6], P(('req', 'exp')), may hold values from 0 to 31, all different within a row; in each aligned block of 128 rows (0 to 127, 128 to 255, ...) at most 36 rows name the same one
- gate_weights: float32 [16384, 6], P(('req', 'exp')), may hold values from 0.05 to 0.5
- expert_gate: bfloat16 [32, 2048, 1408], P('exp'), may hold values from -0.125 to 0.125
- expert_up: bfloat16 [32, 2048, 1408], P('exp'), may hold values from -0.125 to 0.125
- expert_down: bfloat16 [32, 1408, 2048], P('exp'), may hold values from -0.15625 to 0.15625
- shared_gate: bfloat16 [2048, 1408], P(None, 'req'), may hold values from -0.125 to 0.125
- shared_up: bfloat16 [2048, 1408], P(None, 'req'), may hold values from -0.125 to 0.125
- shared_down: bfloat16 [2048, 1408], P(None, 'req'), may hold values from -0.15625 to 0.15625
Outputs:
- mixed: bfloat16 [16384, 2048], P(('req', 'exp'))
Inputs may be any that keep to these rules, and one draw needn't show every extreme that they name: `expert_ids`: within the rows of one device no expert is named by more than 36 rows, and each row names 6 different experts.
All inputs are finite; a program needn't handle non-finite values.
Results may differ from a plain program's by a relative error of at most 0.012.
Values may be sent and summed in bfloat16 or wider, within the bound.
A program may use at most 192 MiB of HBM per device.

v0:
```python
import jax
import jax.numpy as jnp
from jax import lax
from jax.sharding import PartitionSpec as P


def shared_block(rows, w_gate, w_up, w_down):
    gate_part = jnp.dot(rows, w_gate, preferred_element_type=jnp.float32)
    up_part = jnp.dot(rows, w_up, preferred_element_type=jnp.float32)
    hidden = (jax.nn.silu(gate_part) * up_part).astype(jnp.bfloat16)
    return lax.dot_general(
        hidden, w_down, (((1,), (1,)), ((), ())), preferred_element_type=jnp.float32
    )


def body(
    attn_out,
    residual,
    out_weight,
    norm_gain,
    expert_ids,
    gate_weights,
    expert_gate,
    expert_up,
    expert_down,
    shared_gate,
    shared_up,
    shared_down,
):
    row_count, width = attn_out.shape
    topk = expert_ids.shape[1]
    experts = lax.axis_size("exp")
    capacity = min(row_count, 3 * row_count * topk // (2 * experts))
    proj = jnp.dot(
        attn_out,
        lax.all_gather(out_weight, "exp", axis=0, tiled=True),
        preferred_element_type=jnp.float32,
    )
    stream = (residual.astype(jnp.float32) + proj).astype(jnp.bfloat16)
    stream_f = stream.astype(jnp.float32)
    scale = lax.rsqrt(jnp.mean(stream_f * stream_f, axis=1, keepdims=True) + 1e-06)
    normed = (stream_f * scale * norm_gain).astype(jnp.bfloat16)
    flat_ids = expert_ids.reshape(-1)
    onehot = (flat_ids[:, None] == jnp.arange(experts, dtype=jnp.int32)[None, :]).astype(jnp.int32)
    position = jnp.sum(jnp.cumsum(onehot, axis=0) * onehot, axis=1) - 1
    slot = flat_ids * capacity + position
    source_row = jnp.arange(row_count * topk, dtype=jnp.int32) // topk
    table = jnp.full((experts * capacity,), row_count, jnp.int32).at[slot].set(source_row)
    padded = jnp.concatenate([normed, jnp.zeros((1, width), jnp.bfloat16)], axis=0)
    outgoing = padded[table].reshape(experts, capacity, width)
    received = lax.all_to_all(outgoing, "exp", split_axis=0, concat_axis=0, tiled=True)
    sources, items, depth = received.shape
    joined = received.reshape(sources * items, depth)
    gate_part = jnp.dot(joined, expert_gate[0], preferred_element_type=jnp.float32)
    up_part = jnp.dot(joined, expert_up[0], preferred_element_type=jnp.float32)
    hidden = (jax.nn.silu(gate_part) * up_part).astype(jnp.bfloat16)
    result = jnp.dot(hidden, expert_down[0], preferred_element_type=jnp.float32).astype(
        jnp.bfloat16
    )
    returned = lax.all_to_all(
        result.reshape(sources, items, depth), "exp", split_axis=0, concat_axis=0, tiled=True
    )
    picked = returned.reshape(experts * capacity, width)[slot]
    routed = jnp.sum(
        picked.astype(jnp.float32).reshape(row_count, topk, width) * gate_weights[:, :, None],
        axis=1,
    )
    shared = shared_block(
        normed,
        lax.all_gather(shared_gate, "req", axis=1, tiled=True),
        lax.all_gather(shared_up, "req", axis=1, tiled=True),
        lax.all_gather(shared_down, "req", axis=1, tiled=True),
    )
    return (stream_f + routed + shared).astype(jnp.bfloat16)


def solution(mesh):
    return jax.shard_map(
        body,
        mesh=mesh,
        in_specs=(
            P(("req", "exp"), None),
            P(("req", "exp"), None),
            P("exp", None),
            P(),
            P(("req", "exp"), None),
            P(("req", "exp"), None),
            P("exp", None, None),
            P("exp", None, None),
            P("exp", None, None),
            P(None, "req"),
            P(None, "req"),
            P(None, "req"),
        ),
        out_specs=P(("req", "exp"), None),
        check_vma=False,
    )
```

profile of v0, /device:TPU:1, one launch (start us, length us, event | category | flops | bytes accessed | tf_op | source)
XLA Modules:
  0.0 325.8 jit_solution(5530081147603296855)
XLA Ops:
  6.5 0.7 all-gather.5.cloned.1.call-update
  7.3 0.7 all-gather.7.cloned.1.call-update
  8.1 0.7 all-gather.11.cloned.1.call-update
  8.7 0.8 copy.15
  9.5 0.1 eq.29
  9.7 0.1 eq.25
  9.8 1.7 reduce-window.6
  11.6 0.3 slice_reduce_fusion
  11.9 0.7 broadcast_multiply_fusion
  12.7 0.1 mul.67
  13.0 3.4 %scatter_custom_fusion = s32[1152]{0:T(1024)S(1)} fusion(s32[768]{0:T(1024)S(1)} %fusion.20, s32[768]{0:T(1024)S(1)} %add_select_fusion, s32[]{:T(128)} %constant.12.clone.1), kind=kCustom, calls=%fused_computation.39 | custom fusion | bytes 4612 | tf_op jit(solution)/shard_map/scatter | solution.py:48
  16.4 49.6 %all-gather.5.cloned.1.call-done = bf16[2048,2048]{1,0:T(8,128)(2,1)} async-done(((bf16[64,2048]{1,0:T(8,128)(2,1)}), bf16[2048,2048]{1,0:T(8,128)(2,1)}) %all-gather.5.cloned.1.call-update) | async-done | bytes 8388624 | tf_op jit(solution)/shard_map/all_gather | solution.py:36
  66.1 4.8 %multiply_reduce_fusion.1 = (f32[128]{0:T(128)S(1)}, f32[128,2048]{1,0:T(8,128)S(1)}) fusion(bf16[128,2048]{1,0:T(8,128)(2,1)S(1)} %copy-done, bf16[2048,2048]{1,0:T(8,128)(2,1)} %all-gather.5.cloned.1.call-done, bf16[128,2048]{1,0:T(8,128)(2,1)} %param.13), kind=kOutput, calls=%fused_computation.19 | convolution fusion | flops 1075314560 | bytes 10486272 | tf_op jit(solution)/shard_map/dot_general | solution.py:34
  70.9 0.2 multiply_convert_fusion
  71.1 6.0 %gather_fusion = bf16[1152,2048]{1,0:T(8,128)(2,1)} fusion(bf16[129,2048]{1,0:T(8,128)(2,1)S(1)} %concatenate.3, s32[2048]{0:T(1024)S(1)} %pad_clamp_fusion), kind=kCustom, calls=%fused_computation | custom fusion | bytes 9441792 | tf_op jit(solution)/shard_map/gather | solution.py:50
  77.1 7.4 %reshape.78 = bf16[32,36,2048]{2,1,0:T(8,128)(2,1)} reshape(bf16[1152,2048]{1,0:T(8,128)(2,1)} %gather_fusion) | data formatting | bytes 9437184 | tf_op jit(solution)/shard_map/reshape | solution.py:50
  84.5 5.6 %all-to-all-start = ((bf16[32,36,2048]{2,1,0:T(8,128)(2,1)}), bf16[32,36,2048]{2,1,0:T(8,128)(2,1)}, u32[]{:S(2)}, u32[]{:S(2)}) async-start(bf16[32,36,2048]{2,1,0:T(8,128)(2,1)} %reshape.78), calls=%async_computation | async-start | bytes 10485760 | tf_op jit(solution)/shard_map/all_to_all | solution.py:51
  90.2 0.2 all-gather.9.cloned.1.call-start
  90.4 0.3 all-gather.9.cloned.1.call-update
  90.7 64.0 %all-to-all-done = bf16[32,36,2048]{2,1,0:T(8,128)(2,1)} async-done(((bf16[32,36,2048]{2,1,0:T(8,128)(2,1)}), bf16[32,36,2048]{2,1,0:T(8,128)(2,1)}, u32[]{:S(2)}, u32[]{:S(2)}) %all-to-all-start) | async-done | bytes 4718624 | tf_op jit(solution)/shard_map/all_to_all | solution.py:51
  154.7 7.3 %reshape.79 = bf16[1152,2048]{1,0:T(8,128)(2,1)} reshape(bf16[32,36,2048]{2,1,0:T(8,128)(2,1)} %all-to-all-done) | data formatting | bytes 9437184 | tf_op jit(solution)/shard_map/reshape | solution.py:53
  162.0 12.7 %fusion.3 = f32[1152,1408]{1,0:T(8,128)} fusion(bf16[1152,2048]{1,0:T(8,128)(2,1)} %reshape.79, bf16[1,2048,1408]{2,1,0:T(8,128)(2,1)} %param.18), kind=kOutput, calls=%fused_computation.9 | convolution fusion | flops 6643777536 | bytes 16973824 | tf_op jit(solution)/shard_map/dot_general | solution.py:54
  174.7 22.8 %convolution_convert_fusion = bf16[1152,2048]{1,0:T(8,128)(2,1)} fusion(bf16[1,1408,2048]{2,1,0:T(8,128)(2,1)} %param.20, bf16[1152,2048]{1,0:T(8,128)(2,1)} %reshape.79, f32[1152,1408]{1,0:T(8,128)} %fusion.3, bf16[1,2048,1408]{2,1,0:T(8,128)(2,1)} %param.19), kind=kOutput, calls=%fused_computation.6 | convolution fusion | flops 13299646464 | bytes 27459584 | tf_op jit(solution)/shard_map/dot_general | solution.py:57
  197.5 7.3 %reshape.80 = bf16[32,36,2048]{2,1,0:T(8,128)(2,1)} reshape(bf16[1152,2048]{1,0:T(8,128)(2,1)} %convolution_convert_fusion) | data formatting | bytes 9437184 | tf_op jit(solution)/shard_map/reshape | solution.py:61
  204.8 10.0 %all-to-all-start.1 = ((bf16[32,36,2048]{2,1,0:T(8,128)(2,1)}), bf16[32,36,2048]{2,1,0:T(8,128)(2,1)}, u32[]{:S(2)}, u32[]{:S(2)}) async-start(bf16[32,36,2048]{2,1,0:T(8,128)(2,1)} %reshape.80), calls=%async_computation.1 | async-start | bytes 10485760 | tf_op jit(solution)/shard_map/all_to_all | solution.py:60
  215.0 4.6 %fusion.23 = f32[128,1408]{1,0:T(8,128)S(1)} fusion(bf16[128,2048]{1,0:T(8,128)(2,1)S(1)} %multiply_convert_fusion, bf16[2048,1408]{0,1:T(8,128)(2,1)} %all-gather.7.cloned.1.call-done), kind=kOutput, calls=%fused_computation.48 | convolution fusion | flops 738197504 | bytes 7012352 | tf_op jit(solution)/shard_map/dot_general | solution.py:8
  219.6 59.8 %all-to-all-done.1 = bf16[32,36,2048]{2,1,0:T(8,128)(2,1)} async-done(((bf16[32,36,2048]{2,1,0:T(8,128)(2,1)}), bf16[32,36,2048]{2,1,0:T(8,128)(2,1)}, u32[]{:S(2)}, u32[]{:S(2)}) %all-to-all-start.1) | async-done | bytes 4718624 | tf_op jit(solution)/shard_map/all_to_all | solution.py:60
  279.4 7.2 %reshape.81 = bf16[1152,2048]{1,0:T(8,128)(2,1)} reshape(bf16[32,36,2048]{2,1,0:T(8,128)(2,1)} %all-to-all-done.1) | data formatting | bytes 9437184 | tf_op jit(solution)/shard_map/reshape | solution.py:63
  286.7 10.1 %gather_fusion.1 = bf16[768,2048]{1,0:T(8,128)(2,1)} fusion(bf16[1152,2048]{1,0:T(8,128)(2,1)} %reshape.81, s32[1024]{0:T(1024)S(1)} %pad_clamp_fusion.1), kind=kCustom, calls=%fused_computation.1 | custom fusion | bytes 6294528 | tf_op jit(solution)/shard_map/gather | solution.py:63
  296.7 6.5 %reshape.82 = f32[128,6,2048]{2,1,0:T(8,128)} reshape(bf16[768,2048]{1,0:T(8,128)(2,1)} %gather_fusion.1) | data formatting | bytes 9437184 | tf_op jit(solution)/shard_map/convert_element_type | solution.py:65
  303.3 7.6 %multiply_reduce_fusion = f32[128,2048]{1,0:T(8,128)} fusion(f32[128,6,2048]{2,1,0:T(8,128)} %reshape.82, f32[128,6]{1,0:T(8,128)S(1)} %copy.18), kind=kLoop, calls=%fused_computation.4 | loop fusion | flops 2883584 | bytes 7343104 | tf_op jit(solution)/shard_map/reduce_sum | solution.py:64
  310.9 8.4 %fusion.7 = bf16[128,2048]{1,0:T(8,128)(2,1)} fusion(bf16[2048,1408]{0,1:T(8,128)(2,1)} %all-gather.11.cloned.1.call-done, f32[128,2048]{1,0:T(8,128)S(1)} %get-tuple-element.6, f32[128,2048]{1,0:T(8,128)} %multiply_reduce_fusion, bf16[128,2048]{1,0:T(8,128)(2,1)S(1)} %multiply_convert_fusion, bf16[2048,1408]{0,1:T(8,128)(2,1)} %all-gather.9.cloned.1.call-done, ...), kind=kOutput, calls=%fused_computation.16 | convolution fusion | flops 1478262784 | bytes 15400960 | tf_op jit(solution)/shard_map/dot_general | solution.py:11
  (27 shorter events, 0.6 us)
Async XLA Ops:
  6.5 59.5 %copy-start = (bf16[128,2048]{1,0:T(8,128)(2,1)S(1)}, bf16[128,2048]{1,0:T(8,128)(2,1)}, u32[]{:S(2)}) copy-start(bf16[128,2048]{1,0:T(8,128)(2,1)} %param.12) | copy-start | bytes 1572868
  6.5 59.5 %all-gather.5.cloned.1.call-start = ((), (), s32[]{:S(2)}) async-start(), calls=%async_computation.2 | async-start | bytes 8650752 | tf_op jit(solution)/shard_map/all_gather | solution.py:36
  7.3 207.8 %all-gather.7.cloned.1.call-start = ((), (), s32[]{:S(2)}) async-start(), calls=%async_computation.3 | async-start | bytes 7208960 | tf_op jit(solution)/shard_map/all_gather | solution.py:70
  8.0 302.8 %all-gather.11.cloned.1.call-start = ((), (), s32[]{:S(2)}) async-start(), calls=%async_computation.5 | async-start | bytes 7208960 | tf_op jit(solution)/shard_map/all_gather | solution.py:72
  16.4 54.5 %copy-start.2 = (f32[2048]{0:T(1024)S(1)}, f32[2048]{0:T(1024)}, u32[]{:S(2)}) copy-start(f32[2048]{0:T(1024)} %param.15) | copy-start | bytes 24580
  84.5 70.2 %all-to-all-start = ((bf16[32,36,2048]{2,1,0:T(8,128)(2,1)}), bf16[32,36,2048]{2,1,0:T(8,128)(2,1)}, u32[]{:S(2)}, u32[]{:S(2)}) async-start(bf16[32,36,2048]{2,1,0:T(8,128)(2,1)} %reshape.78), calls=%async_computation | async-start | bytes 10485760 | tf_op jit(solution)/shard_map/all_to_all | solution.py:51
  90.2 220.7 %all-gather.9.cloned.1.call-start = ((), (), s32[]{:S(2)}) async-start(), calls=%async_computation.4 | async-start | bytes 7208960 | tf_op jit(solution)/shard_map/all_gather | solution.py:71
  204.8 10.1 %copy-start.3 = (f32[128,6]{0,1:T(8,128)S(1)}, f32[128,6]{0,1:T(8,128)}, u32[]{:S(2)}) copy-start(f32[128,6]{0,1:T(8,128)} %param.17) | copy-start | bytes 9220
  204.8 74.6 %all-to-all-start.1 = ((bf16[32,36,2048]{2,1,0:T(8,128)(2,1)}), bf16[32,36,2048]{2,1,0:T(8,128)(2,1)}, u32[]{:S(2)}, u32[]{:S(2)}) async-start(bf16[32,36,2048]{2,1,0:T(8,128)(2,1)} %reshape.80), calls=%async_computation.1 | async-start | bytes 10485760 | tf_op jit(solution)/shard_map/all_to_all | solution.py:60
  303.3 16.0 %copy-start.1 = (bf16[128,2048]{1,0:T(8,128)(2,1)S(1)}, bf16[128,2048]{1,0:T(8,128)(2,1)}, u32[]{:S(2)}) copy-start(bf16[128,2048]{1,0:T(8,128)(2,1)} %param.12) | copy-start | bytes 1572868
Sparse Core Ops, SparseCore 0:
  9.6 56.3 all-gather.4
  67.7 60.7 all-gather.6
  130.2 61.9 all-gather.10
  193.7 61.9 all-gather.8
where the time goes:
time: 330 us; the launch traced here: 326 us
  waiting for transfers between devices  176 us (53%)
  local copies, waits for them, and re-layouts  57 us (17%)
  matrix products  53.3 us (16%)
  starting transfers between devices  16 us (5%)
  between operations  13.3 us (4%)
  other arithmetic  10.3 us (3%)
    all_to_all x1, waiting for transfers between devices, body(): lax.all_to_all(outgoing, 'exp', split_axis=0, concat_axis=0, tiled=True)  64 us
    all_to_all x1, waiting for transfers between devices, body(): lax.all_to_all(result.reshape(sources, items, depth), 'exp', split_axis=0...  59.8 us
    all_gather x1, waiting for transfers between devices, body(): lax.all_gather(out_weight, 'exp', axis=0, tiled=True)  49.6 us
    dot_general x1, matrix products, body(): jnp.dot(hidden, expert_down[0], preferred_element_type=jnp.float32)  22.8 us
    dot_general x1, matrix products, body(): jnp.dot(joined, expert_gate[0], preferred_element_type=jnp.float32)  12.7 us
    gather x1, local copies, waits for them, and re-layouts, body(): picked = returned.reshape(experts * capacity, width)[slot]  10.1 us
    all_to_all x1, starting transfers between devices, body(): lax.all_to_all(result.reshape(sources, items, depth), 'exp', split_axis=0...  10 us
    dot_general x1, matrix products, shared_block(): lax.dot_general(hidden, w_down, (((1,), (1,)), ((), ())), preferred_eleme...  8.44 us
  transfers between devices with their start and end apart: 6, of which 3 were waited for; matrix products, arithmetic and copies ran while one was open for 34% of the time, Pallas kernels for 0%

commit v1 on v0

v1 whole, which is shorter than its diff:
```python
import jax
import jax.numpy as jnp
from jax import lax
from jax.sharding import PartitionSpec as P


def body(
    attn_out,
    residual,
    out_weight,
    norm_gain,
    expert_ids,
    gate_weights,
    expert_gate,
    expert_up,
    expert_down,
    shared_gate,
    shared_up,
    shared_down,
):
    row_count, width = attn_out.shape
    topk = expert_ids.shape[1]
    experts = lax.axis_size("exp")
    capacity = min(row_count, 3 * row_count * topk // (2 * experts))
    proj = jnp.dot(
        attn_out,
        lax.all_gather(out_weight, "exp", axis=0, tiled=True),
        preferred_element_type=jnp.float32,
    )
    stream = (residual.astype(jnp.float32) + proj).astype(jnp.bfloat16)
    stream_f = stream.astype(jnp.float32)
    scale = lax.rsqrt(jnp.mean(stream_f * stream_f, axis=1, keepdims=True) + 1e-06)
    normed = (stream_f * scale * norm_gain).astype(jnp.bfloat16)

    flat_ids = expert_ids.reshape(-1)
    onehot = (flat_ids[:, None] == jnp.arange(experts, dtype=jnp.int32)[None, :]).astype(jnp.int32)
    position = jnp.sum(jnp.cumsum(onehot, axis=0) * onehot, axis=1) - 1
    slot = flat_ids * capacity + position
    source_row = jnp.arange(row_count * topk, dtype=jnp.int32) // topk
    table = jnp.full((experts * capacity,), row_count, jnp.int32).at[slot].set(source_row)
    rows = jnp.arange(row_count, dtype=jnp.int32)
    pick = (table.reshape(experts, capacity)[:, :, None] == rows[None, None, :]).astype(jnp.bfloat16)
    outgoing = jnp.einsum(
        "ecr,rd->ecd", pick, normed, preferred_element_type=jnp.float32
    ).astype(jnp.bfloat16)
    joined = lax.all_to_all(outgoing, "exp", split_axis=0, concat_axis=0, tiled=True)
    gate_part = jnp.einsum("scd,df->scf", joined, expert_gate[0], preferred_element_type=jnp.float32)
    up_part = jnp.einsum("scd,df->scf", joined, expert_up[0], preferred_element_type=jnp.float32)
    hidden = (jax.nn.silu(gate_part) * up_part).astype(jnp.bfloat16)
    hidden = lax.optimization_barrier(hidden)
    result = jnp.einsum(
        "scf,fd->scd", hidden, expert_down[0], preferred_element_type=jnp.float32
    ).astype(jnp.bfloat16)
    returned = lax.all_to_all(result, "exp", split_axis=0, concat_axis=0, tiled=True)
    slot_weight = jnp.zeros((experts * capacity,), jnp.float32).at[slot].set(gate_weights.reshape(-1))
    combine = jnp.where(
        table.reshape(experts, capacity)[None, :, :] == rows[:, None, None],
        slot_weight.reshape(experts, capacity)[None, :, :],
        0.0,
    )
    routed = jnp.einsum(
        "rec,ecd->rd",
        combine,
        returned.astype(jnp.float32),
        precision=lax.Precision.HIGHEST,
        preferred_element_type=jnp.float32,
    )

    group_rows = lax.all_gather(normed, "req", axis=0, tiled=True)
    s_gate = jnp.dot(group_rows, shared_gate, preferred_element_type=jnp.float32)
    s_up = jnp.dot(group_rows, shared_up, preferred_element_type=jnp.float32)
    s_hidden = (jax.nn.silu(s_gate) * s_up).astype(jnp.bfloat16)
    s_partial = lax.dot_general(
        s_hidden, shared_down, (((1,), (1,)), ((), ())), preferred_element_type=jnp.float32
    )
    shared = lax.psum_scatter(s_partial, "req", scatter_dimension=0, tiled=True)
    return (stream_f + routed + shared).astype(jnp.bfloat16)


def solution(mesh):
    return jax.shard_map(
        body,
        mesh=mesh,
        in_specs=(
            P(("req", "exp"), None),
            P(("req", "exp"), None),
            P("exp", None),
            P(),
            P(("req", "exp"), None),
            P(("req", "exp"), None),
            P("exp", None, None),
            P("exp", None, None),
            P("exp", None, None),
            P(None, "req"),
            P(None, "req"),
            P(None, "req"),
        ),
        out_specs=P(("req", "exp"), None),
        check_vma=False,
    )
```

time: 330 us -> 271 us (0.82)
  local copies, waits for them, and re-layouts: 57 us -> 8.82 us
  waiting for transfers between devices: 176 us -> 167 us
  other arithmetic: 10.3 us -> 2.77 us
  matrix products: 53.3 us -> 60.6 us
    all_to_all x1, waiting for transfers between devices: 64 us -> 19.6 us  [body(): lax.all_to_all(outgoing, 'exp', split_axis=0, concat_axis=0, tiled=True)]
    all_gather x3 -> x1, waiting for transfers between devices: 0.02 us -> 33.7 us  [body(): group_rows = lax.all_gather(normed, 'req', axis=0, tiled=True)]
    reshape x4 -> x1, local copies, waits for them, and re-layouts: 29.3 us -> 0.13 us  [body(): gate_weights.reshape(-1)]
    gather x2 -> x0, local copies, waits for them, and re-layouts: 16 us -> none  [the longest x1 10.1 us: body(): picked = returned.reshape(experts * capacity, width)[slot]]
    reduce_sum x1 -> x0, other arithmetic: 7.56 us -> none  [body(): jnp.sum(picked.astype(jnp.float32).reshape(row_count, topk, width) * gate...]
    dot_general x4 -> x7, matrix products: 48.5 us -> 55.6 us  [the longest x1 12.9 us: body(): jnp.einsum('scd,df->scf', joined, expert_gate[0], preferred_element_type=...]
    convert_element_type x1 -> x0, local copies, waits for them, and re-layouts: 6.55 us -> none  [body(): picked.astype(jnp.float32).reshape(row_count, topk, width)]
    scatter x0 -> x1, local copies, waits for them, and re-layouts: none -> 3.38 us  [body(): jnp.zeros((experts * capacity,), jnp.float32).at[slot]]
  transfers between devices with their start and end apart: 6 -> 5, of which waited for: 3 -> 4; matrix products, arithmetic and copies ran while one was open for 34% -> 21% of each run, Pallas kernels for 0% -> 0%
where the time goes in v1:
time: 271 us; the launch traced here: 268 us
  waiting for transfers between devices  167 us (62%)
  matrix products  60.6 us (22%)
  starting transfers between devices  15.7 us (6%)
  between operations  13.3 us (5%)
  local copies, waits for them, and re-layouts  8.82 us (3%)
  other arithmetic  2.77 us (1%)
    all_to_all x1, waiting for transfers between devices, body(): lax.all_to_all(result, 'exp', split_axis=0, concat_axis=0, tiled=True)  60.9 us
    all_gather x1, waiting for transfers between devices, body(): lax.all_gather(out_weight, 'exp', axis=0, tiled=True)  51.1 us
    all_gather x1, waiting for transfers between devices, body(): group_rows = lax.all_gather(normed, 'req', axis=0, tiled=True)  33.7 us
    all_to_all x1, waiting for transfers between devices, body(): lax.all_to_all(outgoing, 'exp', split_axis=0, concat_axis=0, tiled=True)  19.6 us
    dot_general x1, matrix products, body(): jnp.einsum('scd,df->scf', joined, expert_gate[0], preferred_element_type=...  12.9 us
    dot_general x1, matrix products, body(): jnp.einsum('scd,df->scf', joined, expert_up[0], preferred_element_type=jn...  12.2 us
    dot_general x1, matrix products, body(): jnp.einsum('scf,fd->scd', hidden, expert_down[0], preferred_element_type=...  10.2 us
    all_to_all x1, starting transfers between devices, body(): lax.all_to_all(result, 'exp', split_axis=0, concat_axis=0, tiled=True)  9.95 us
  transfers between devices with their start and end apart: 5, of which 4 were waited for; matrix products, arithmetic and copies ran while one was open for 21% of the time, Pallas kernels for 0%

profile of v1, /device:TPU:1, one launch (start us, length us, event | category | flops | bytes accessed | tf_op | source)
XLA Modules:
  0.0 268.0 jit_solution(15319625592396566629)
XLA Ops:
  6.5 0.7 all-gather.3.cloned.1.call-update
  7.3 0.8 copy.14
  8.1 0.1 eq.57
  8.2 0.1 eq.53
  8.3 1.7 reduce-window.6
  10.1 0.3 slice_reduce_fusion
  10.4 0.7 broadcast_multiply_fusion
  11.1 0.1 copy.13
  11.2 0.1 mul.54
  11.4 0.1 fusion.28
  11.5 3.4 %scatter_custom_fusion = s32[1152]{0:T(1024)S(1)} fusion(s32[768]{0:T(1024)S(1)} %fusion.37, s32[768]{0:T(1024)S(1)} %add_select_fusion, s32[]{:T(128)} %constant.11.clone.1), kind=kCustom, calls=%fused_computation.53 | custom fusion | bytes 4612 | tf_op jit(solution)/shard_map/scatter | solution.py:40
  14.9 0.1 eq.61
  15.0 51.1 %all-gather.3.cloned.1.call-done = bf16[2048,2048]{1,0:T(8,128)(2,1)} async-done(((bf16[64,2048]{1,0:T(8,128)(2,1)}), bf16[2048,2048]{1,0:T(8,128)(2,1)}) %all-gather.3.cloned.1.call-update) | async-done | bytes 8388624 | tf_op jit(solution)/shard_map/all_gather | solution.py:27
  66.1 5.0 %multiply_reduce_fusion = (f32[128]{0:T(128)S(1)}, f32[128,2048]{1,0:T(8,128)S(1)}) fusion(bf16[128,2048]{1,0:T(8,128)(2,1)} %param.12, bf16[2048,2048]{1,0:T(8,128)(2,1)} %all-gather.3.cloned.1.call-done, bf16[128,2048]{1,0:T(8,128)(2,1)} %param.13), kind=kOutput, calls=%fused_computation.21 | convolution fusion | flops 1075314560 | bytes 10486272 | tf_op jit(solution)/shard_map/dot_general | solution.py:25
  71.0 0.2 multiply_convert_fusion.1
  71.2 3.9 %convolution_convert_fusion = bf16[32,36,2048]{2,1,0:T(8,128)(2,1)} fusion(bf16[128,2048]{1,0:T(8,128)(2,1)S(1)} %multiply_convert_fusion.1, s32[32,36]{1,0:T(8,128)S(1)} %eq.61), kind=kOutput, calls=%fused_computation.8 | convolution fusion | flops 606486528 | bytes 5247488 | tf_op jit(solution)/shard_map/ecr,rd->ecd/dot_general | solution.py:43
  75.1 5.5 %all-to-all-start = ((bf16[32,36,2048]{2,1,0:T(8,128)(2,1)}), bf16[32,36,2048]{2,1,0:T(8,128)(2,1)}, u32[]{:S(2)}, u32[]{:S(2)}) async-start(bf16[32,36,2048]{2,1,0:T(8,128)(2,1)} %convolution_convert_fusion), calls=%async_computation | async-start | bytes 10485760 | tf_op jit(solution)/shard_map/all_to_all | solution.py:46
  80.7 0.7 all-gather.5.cloned.1.call-update
  81.4 0.2 reduce-scatter.2.cloned.1.call-start
  81.6 33.7 %all-gather.5.cloned.1.call-done = bf16[512,2048]{1,0:T(8,128)(2,1)} async-done(((bf16[128,2048]{1,0:T(8,128)(2,1)}), bf16[512,2048]{1,0:T(8,128)(2,1)}) %all-gather.5.cloned.1.call-update) | async-done | bytes 2097168 | tf_op jit(solution)/shard_map/all_gather | solution.py:69
  115.4 3.8 %fusion.40 = f32[512,352]{0,1:T(8,128)} fusion(bf16[512,2048]{1,0:T(8,128)(2,1)} %all-gather.5.cloned.1.call-done, bf16[2048,352]{0,1:T(8,128)(2,1)} %param.21), kind=kOutput, calls=%fused_computation.62 | convolution fusion | flops 738197504 | bytes 4259840 | tf_op jit(solution)/shard_map/dot_general | solution.py:70
  119.2 6.4 %fusion.14 = f32[512,2048]{1,0:T(8,128)} fusion(bf16[2048,352]{0,1:T(8,128)(2,1)S(1)} %copy-done, bf16[512,2048]{1,0:T(8,128)(2,1)} %all-gather.5.cloned.1.call-done, bf16[2048,352]{0,1:T(8,128)(2,1)} %param.22, f32[512,352]{0,1:T(8,128)} %fusion.40), kind=kOutput, calls=%fused_computation.19 | convolution fusion | flops 1477476352 | bytes 9895936 | tf_op jit(solution)/shard_map/dot_general | solution.py:73
  125.7 19.6 %all-to-all-done = bf16[32,36,2048]{2,1,0:T(8,128)(2,1)} async-done(((bf16[32,36,2048]{2,1,0:T(8,128)(2,1)}), bf16[32,36,2048]{2,1,0:T(8,128)(2,1)}, u32[]{:S(2)}, u32[]{:S(2)}) %all-to-all-start) | async-done | bytes 4718624 | tf_op jit(solution)/shard_map/all_to_all | solution.py:46
  145.2 12.2 %fusion.2 = f32[32,36,1408]{2,1,0:T(8,128)S(1)} fusion(bf16[32,36,2048]{2,1,0:T(8,128)(2,1)} %all-to-all-done, bf16[1,2048,1408]{2,1,0:T(8,128)(2,1)} %param.19), kind=kOutput, calls=%fused_computation.5 | convolution fusion | flops 6643777536 | bytes 16973824 | tf_op jit(solution)/shard_map/scd,df->scf/dot_general | solution.py:48
  157.4 12.9 %multiply_convert_fusion = bf16[32,36,1408]{2,1,0:T(8,128)(2,1)S(1)} fusion(f32[32,36,1408]{2,1,0:T(8,128)S(1)} %fusion.2, bf16[32,36,2048]{2,1,0:T(8,128)(2,1)} %all-to-all-done, bf16[1,2048,1408]{2,1,0:T(8,128)(2,1)} %param.18), kind=kOutput, calls=%fused_computation.2 | convolution fusion | flops 6653509632 | bytes 20217856 | tf_op jit(solution)/shard_map/scd,df->scf/dot_general | solution.py:47
  170.4 10.2 %fusion.5 = bf16[32,36,2048]{2,1,0:T(8,128)(2,1)} fusion(bf16[32,36,1408]{2,1,0:T(8,128)(2,1)S(1)} %multiply_convert_fusion, bf16[1,1408,2048]{2,1,0:T(8,128)(2,1)S(1)} %bitcast.54), kind=kOutput, calls=%fused_computation.9 | convolution fusion | flops 6646136832 | bytes 13729792 | tf_op jit(solution)/shard_map/scf,fd->scd/dot_general | solution.py:51
  180.6 9.9 %all-to-all-start.1 = ((bf16[32,36,2048]{2,1,0:T(8,128)(2,1)}), bf16[32,36,2048]{2,1,0:T(8,128)(2,1)}, u32[]{:S(2)}, u32[]{:S(2)}) async-start(bf16[32,36,2048]{2,1,0:T(8,128)(2,1)} %fusion.5), calls=%async_computation.1 | async-start | bytes 10485760 | tf_op jit(solution)/shard_map/all_to_all | solution.py:54
  190.6 0.1 copy.17
  190.7 0.1 reshape.80
  190.8 3.4 %scatter_custom_fusion.1 = f32[1152]{0:T(1024)S(1)} fusion(s32[768]{0:T(1024)S(1)} %fusion.37, f32[768]{0:T(1024)S(1)} %reshape.80, f32[]{:T(128)} %constant.34.clone.1), kind=kCustom, calls=%fused_computation.51 | custom fusion | bytes 4612 | tf_op jit(solution)/shard_map/scatter | solution.py:55
  194.3 60.9 %all-to-all-done.1 = bf16[32,36,2048]{2,1,0:T(8,128)(2,1)} async-done(((bf16[32,36,2048]{2,1,0:T(8,128)(2,1)}), bf16[32,36,2048]{2,1,0:T(8,128)(2,1)}, u32[]{:S(2)}, u32[]{:S(2)}) %all-to-all-start.1) | async-done | bytes 4718624 | tf_op jit(solution)/shard_map/all_to_all | solution.py:54
  255.3 6.2 %fusion.10 = bf16[128,2048]{1,0:T(8,128)(2,1)} fusion(f32[128,2048]{1,0:T(8,128)} %reduce-scatter.2.cloned.1.call-done, f32[128,2048]{1,0:T(8,128)S(1)} %get-tuple-element.6, bf16[32,36,2048]{2,1,0:T(8,128)(2,1)} %all-to-all-done.1, f32[32,36]{1,0:T(8,128)S(1)} %broadcast_in_dim.29, s32[32,36]{1,0:T(8,128)S(1)} %eq.61), kind=kOutput, calls=%fused_computation.14 | convolution fusion | flops 3624960000 | bytes 7349248 | tf_op jit(solution)/shard_map/rec,ecd->rd/dot_general | solution.py:61
  (26 shorter events, 0.3 us)
Async XLA Ops:
  6.5 112.7 %copy-start = (bf16[2048,352]{0,1:T(8,128)(2,1)S(1)}, bf16[2048,352]{0,1:T(8,128)(2,1)}, u32[]{:S(2)}) copy-start(bf16[2048,352]{0,1:T(8,128)(2,1)} %param.23) | copy-start | bytes 4325380
  6.5 59.5 %all-gather.3.cloned.1.call-start = ((), (), s32[]{:S(2)}) async-start(), calls=%async_computation.3 | async-start | bytes 8650752 | tf_op jit(solution)/shard_map/all_gather | solution.py:27
  15.0 56.1 %copy-start.3 = (f32[2048]{0:T(1024)S(1)}, f32[2048]{0:T(1024)}, u32[]{:S(2)}) copy-start(f32[2048]{0:T(1024)} %param.15) | copy-start | bytes 24580
  71.2 3.9 %copy-start.2 = (bf16[128,2048]{1,0:T(8,128)(2,1)}, bf16[128,2048]{1,0:T(8,128)(2,1)S(1)}, u32[]{:S(2)}) copy-start(bf16[128,2048]{1,0:T(8,128)(2,1)S(1)} %multiply_convert_fusion.1) | copy-start | bytes 1572868
  75.1 70.1 %all-to-all-start = ((bf16[32,36,2048]{2,1,0:T(8,128)(2,1)}), bf16[32,36,2048]{2,1,0:T(8,128)(2,1)}, u32[]{:S(2)}, u32[]{:S(2)}) async-start(bf16[32,36,2048]{2,1,0:T(8,128)(2,1)} %convolution_convert_fusion), calls=%async_computation | async-start | bytes 10485760 | tf_op jit(solution)/shard_map/all_to_all | solution.py:46
  80.7 34.7 %all-gather.5.cloned.1.call-start = ((), (), s32[]{:S(2)}) async-start(), calls=%async_computation.4 | async-start | bytes 2621440 | tf_op jit(solution)/shard_map/all_gather | solution.py:69
  81.4 173.9 %reduce-scatter.2.cloned.1.call-start = ((), (), s32[]{:S(2)}) async-start(), calls=%async_computation.5 | async-start | bytes 5242880 | tf_op jit(solution)/shard_map/reduce_scatter | solution.py:76
  145.2 25.1 %slice-start = ((s8[5767168]{0:T(1024)(128)(4,1)}), s8[4194304]{0:T(1024)(128)(4,1)S(1)}, s32[]{:S(2)}) async-start(s8[5767168]{0:T(1024)(128)(4,1)} %bitcast.53), calls=%async_computation.6 | async-start | bytes 8388608
  157.4 12.9 %slice-start.1 = ((s8[5767168]{0:T(1024)(128)(4,1)}), s8[1572864]{0:T(1024)(128)(4,1)S(1)}, s32[]{:S(2)}) async-start(s8[5767168]{0:T(1024)(128)(4,1)} %bitcast.53), calls=%async_computation.7 | async-start | bytes 3145728
  180.6 10.0 %copy-start.4 = (f32[128,6]{0,1:T(8,128)S(1)}, f32[128,6]{0,1:T(8,128)}, u32[]{:S(2)}) copy-start(f32[128,6]{0,1:T(8,128)} %param.17) | copy-start | bytes 9220
  180.6 74.7 %all-to-all-start.1 = ((bf16[32,36,2048]{2,1,0:T(8,128)(2,1)}), bf16[32,36,2048]{2,1,0:T(8,128)(2,1)}, u32[]{:S(2)}, u32[]{:S(2)}) async-start(bf16[32,36,2048]{2,1,0:T(8,128)(2,1)} %fusion.5), calls=%async_computation.1 | async-start | bytes 10485760 | tf_op jit(solution)/shard_map/all_to_all | solution.py:54
  190.6 70.9 %copy-start.1 = (bf16[2048,352]{0,1:T(8,128)(2,1)S(1)}, bf16[2048,352]{0,1:T(8,128)(2,1)}, u32[]{:S(2)}) copy-start(bf16[2048,352]{0,1:T(8,128)(2,1)} %param.23) | copy-start | bytes 4325380
Sparse Core Ops, SparseCore 0:
  9.6 56.3 all-gather.2
  83.2 32.1 all-gather.4
  125.8 46.9 reduce-scatter.1

commit v2 on v1

--- a/solution.py
+++ b/solution.py
@@ -40,18 +40,30 @@
     table = jnp.full((experts * capacity,), row_count, jnp.int32).at[slot].set(source_row)
     rows = jnp.arange(row_count, dtype=jnp.int32)
     pick = (table.reshape(experts, capacity)[:, :, None] == rows[None, None, :]).astype(jnp.bfloat16)
+    lanes = 128
+    blocks = width // lanes
     outgoing = jnp.einsum(
-        "ecr,rd->ecd", pick, normed, preferred_element_type=jnp.float32
+        "ecr,rjk->ecjk", pick, normed.reshape(row_count, blocks, lanes),
+        preferred_element_type=jnp.float32,
     ).astype(jnp.bfloat16)
-    joined = lax.all_to_all(outgoing, "exp", split_axis=0, concat_axis=0, tiled=True)
-    gate_part = jnp.einsum("scd,df->scf", joined, expert_gate[0], preferred_element_type=jnp.float32)
-    up_part = jnp.einsum("scd,df->scf", joined, expert_up[0], preferred_element_type=jnp.float32)
+    joined = lax.all_to_all(
+        outgoing.reshape(experts, capacity * blocks, lanes), "exp",
+        split_axis=0, concat_axis=0, tiled=True,
+    ).reshape(experts, capacity, blocks, lanes)
+    gate_w = expert_gate[0].reshape(blocks, lanes, -1)
+    up_w = expert_up[0].reshape(blocks, lanes, -1)
+    gate_part = jnp.einsum("scjk,jkf->scf", joined, gate_w, preferred_element_type=jnp.float32)
+    up_part = jnp.einsum("scjk,jkf->scf", joined, up_w, preferred_element_type=jnp.float32)
     hidden = (jax.nn.silu(gate_part) * up_part).astype(jnp.bfloat16)
     hidden = lax.optimization_barrier(hidden)
     result = jnp.einsum(
-        "scf,fd->scd", hidden, expert_down[0], preferred_element_type=jnp.float32
+        "scf,fjk->scjk", hidden, expert_down[0].reshape(-1, blocks, lanes),
+        preferred_element_type=jnp.float32,
     ).astype(jnp.bfloat16)
-    returned = lax.all_to_all(result, "exp", split_axis=0, concat_axis=0, tiled=True)
+    returned = lax.all_to_all(
+        result.reshape(experts, capacity * blocks, lanes), "exp",
+        split_axis=0, concat_axis=0, tiled=True,
+    ).reshape(experts, capacity, blocks, lanes)
     slot_weight = jnp.zeros((experts * capacity,), jnp.float32).at[slot].set(gate_weights.reshape(-1))
     combine = jnp.where(
         table.reshape(experts, capacity)[None, :, :] == rows[:, None, None],
@@ -59,12 +71,12 @@
         0.0,
     )
     routed = jnp.einsum(
-        "rec,ecd->rd",
+        "rec,ecjk->rjk",
         combine,
         returned.astype(jnp.float32),
         precision=lax.Precision.HIGHEST,
         preferred_element_type=jnp.float32,
-    )
+    ).reshape(row_count, width)
 
     group_rows = lax.all_gather(normed, "req", axis=0, tiled=True)
     s_gate = jnp.dot(group_rows, shared_gate, preferred_element_type=jnp.float32)

time: 271 us -> 275 us (1.015)
  local copies, waits for them, and re-layouts: 8.82 us -> 36.6 us
  waiting for transfers between devices: 167 us -> 147 us
    all_to_all x2, waiting for transfers between devices: 80.5 us -> 69.2 us  [the longest x1 54.6 us: body(): lax.all_to_all(result.reshape(experts, capacity * blocks, lanes), 'exp',...]
    dot_general x0 -> x1, local copies, waits for them, and re-layouts: none -> 8.28 us  [body(): jnp.einsum('rec,ecjk->rjk', combine, returned.astype(jnp.float32), precis...]
    all_gather x1, waiting for transfers between devices: 33.7 us -> 26.4 us  [body(): group_rows = lax.all_gather(normed, 'req', axis=0, tiled=True)]
    unnamed x16 -> x15, local copies, waits for them, and re-layouts: 0.95 us -> 8.2 us
    convert_element_type x0 -> x2, local copies, waits for them, and re-layouts: none -> 6.34 us  [the longest x1 3.19 us: body(): outgoing = jnp.einsum('ecr,rjk->ecjk', pick, normed.reshape(row_count, bl...]
    reshape x0 -> x1, local copies, waits for them, and re-layouts: none -> 5.86 us  [body(): returned = lax.all_to_all(result.reshape(experts, capacity * blocks, lane...]
  transfers between devices with their start and end apart: 5 -> 5, of which waited for: 4 -> 4; matrix products, arithmetic and copies ran while one was open for 21% -> 29% of each run, Pallas kernels for 0% -> 0%
where the time goes in v2:
time: 275 us; the launch traced here: 273 us
  waiting for transfers between devices  147 us (53%)
  matrix products  58.4 us (21%)
  local copies, waits for them, and re-layouts  36.6 us (13%)
  starting transfers between devices  13.5 us (5%)
  between operations  13.3 us (5%)
  other arithmetic  3.56 us (1%)
    all_to_all x1, waiting for transfers between devices, body(): lax.all_to_all(result.reshape(experts, capacity * blocks, lanes), 'exp',...  54.6 us
    all_gather x1, waiting for transfers between devices, body(): lax.all_gather(out_weight, 'exp', axis=0, tiled=True)  51.1 us
    all_gather x1, waiting for transfers between devices, body(): group_rows = lax.all_gather(normed, 'req', axis=0, tiled=True)  26.4 us
    all_to_all x1, waiting for transfers between devices, body(): lax.all_to_all(outgoing.reshape(experts, capacity * blocks, lanes), 'exp'...  14.5 us
    dot_general x1, matrix products, body(): jnp.einsum('scjk,jkf->scf', joined, gate_w, preferred_element_type=jnp.fl...  12.8 us
    dot_general x1, matrix products, body(): jnp.einsum('scjk,jkf->scf', joined, up_w, preferred_element_type=jnp.floa...  12.1 us
    dot_general x1, matrix products, body(): jnp.einsum('scf,fjk->scjk', hidden, expert_down[0].reshape(-1, blocks, la...  9.08 us
    dot_general x1, matrix products, body(): jnp.einsum('rec,ecjk->rjk', combine, returned.astype(jnp.float32), precis...  8.65 us
  transfers between devices with their start and end apart: 5, of which 4 were waited for; matrix products, arithmetic and copies ran while one was open for 29% of the time, Pallas kernels for 0%

profile of v2, /device:TPU:1, one launch (start us, length us, event | category | flops | bytes accessed | tf_op | source)
XLA Modules:
  0.0 272.6 jit_solution(3965826598224297137)
XLA Ops:
  6.5 0.7 all-gather.3.cloned.1.call-update
  7.3 0.8 copy.16
  8.1 0.1 eq.57
  8.2 0.1 eq.53
  8.3 1.7 reduce-window.6
  10.1 0.3 slice_reduce_fusion
  10.4 0.7 broadcast_multiply_fusion
  11.1 0.1 copy.15
  11.2 0.1 mul.54
  11.5 3.4 %scatter_custom_fusion = s32[1152]{0:T(1024)S(1)} fusion(s32[768]{0:T(1024)S(1)} %fusion.58, s32[768]{0:T(1024)S(1)} %add_select_fusion, s32[]{:T(128)} %constant.11.clone.1), kind=kCustom, calls=%fused_computation.66 | custom fusion | bytes 4612 | tf_op jit(solution)/shard_map/scatter | solution.py:40
  15.0 51.1 %all-gather.3.cloned.1.call-done = bf16[2048,2048]{1,0:T(8,128)(2,1)} async-done(((bf16[64,2048]{1,0:T(8,128)(2,1)}), bf16[2048,2048]{1,0:T(8,128)(2,1)}) %all-gather.3.cloned.1.call-update) | async-done | bytes 8388624 | tf_op jit(solution)/shard_map/all_gather | solution.py:27
  66.1 5.0 %multiply_reduce_fusion = (f32[128]{0:T(128)S(1)}, f32[128,2048]{1,0:T(8,128)S(1)}) fusion(bf16[128,2048]{1,0:T(8,128)(2,1)} %param.12, bf16[2048,2048]{1,0:T(8,128)(2,1)} %all-gather.3.cloned.1.call-done, bf16[128,2048]{1,0:T(8,128)(2,1)} %param.13), kind=kOutput, calls=%fused_computation.32 | convolution fusion | flops 1075314560 | bytes 10486272 | tf_op jit(solution)/shard_map/dot_general | solution.py:25
  71.0 1.6 convolution_convert_fusion
  72.7 3.2 %copy.21 = bf16[32,36,16,128]{3,2,1,0:T(8,128)(2,1)} copy(bf16[32,36,16,128]{3,1,2,0:T(8,128)(2,1)S(1)} %convolution_convert_fusion) | data formatting | bytes 9437184 | tf_op jit(solution)/shard_map/convert_element_type | solution.py:48
  75.9 5.5 %all-to-all-start = ((bf16[32,576,128]{2,1,0:T(8,128)(2,1)}), bf16[32,576,128]{2,1,0:T(8,128)(2,1)}, u32[]{:S(2)}, u32[]{:S(2)}) async-start(bf16[32,576,128]{2,1,0:T(8,128)(2,1)} %bitcast.99), calls=%async_computation | async-start | bytes 9437184 | tf_op jit(solution)/shard_map/all_to_all | solution.py:49
  81.4 0.9 multiply_convert_fusion
  82.5 7.3 %copy.33 = bf16[176,8,16,128]{3,2,1,0:T(8,128)(2,1)} copy(bf16[176,8,16,128]{3,1,2,0:T(8,128)(2,1)} %bitcast.102) | data formatting | bytes 11534336
  89.7 26.4 %all-gather.5.cloned.1.call-done = bf16[512,2048]{1,0:T(8,128)(2,1)} async-done(((bf16[128,2048]{1,0:T(8,128)(2,1)}), bf16[512,2048]{1,0:T(8,128)(2,1)}) %all-gather.5.cloned.1.call-update) | async-done | bytes 2097168 | tf_op jit(solution)/shard_map/all_gather | solution.py:81
  116.1 2.9 %fusion.61 = f32[512,352]{0,1:T(8,128)S(1)} fusion(bf16[512,2048]{1,0:T(8,128)(2,1)} %all-gather.5.cloned.1.call-done, bf16[2048,352]{0,1:T(8,128)(2,1)} %param.21), kind=kOutput, calls=%fused_computation.75 | convolution fusion | flops 738197504 | bytes 4259840 | tf_op jit(solution)/shard_map/dot_general | solution.py:82
  119.0 6.2 %fusion.33 = f32[512,2048]{1,0:T(8,128)} fusion(bf16[2048,352]{0,1:T(8,128)(2,1)S(1)} %copy-done, bf16[512,2048]{1,0:T(8,128)(2,1)} %all-gather.5.cloned.1.call-done, bf16[2048,352]{0,1:T(8,128)(2,1)} %param.22, f32[512,352]{0,1:T(8,128)S(1)} %fusion.61), kind=kOutput, calls=%fused_computation.30 | convolution fusion | flops 1477476352 | bytes 9895936 | tf_op jit(solution)/shard_map/dot_general | solution.py:85
  125.3 14.5 %all-to-all-done = bf16[32,576,128]{2,1,0:T(8,128)(2,1)} async-done(((bf16[32,576,128]{2,1,0:T(8,128)(2,1)}), bf16[32,576,128]{2,1,0:T(8,128)(2,1)}, u32[]{:S(2)}, u32[]{:S(2)}) %all-to-all-start) | async-done | bytes 4718624 | tf_op jit(solution)/shard_map/all_to_all | solution.py:49
  139.8 12.1 %fusion.9 = f32[32,36,1408,1]{2,1,3,0:T(8,128)S(1)} fusion(bf16[16,128,1408,1]{2,1,0,3:T(8,128)(2,1)} %bitcast.107, bf16[32,36,16,128]{3,2,1,0:T(8,128)(2,1)} %bitcast.5), kind=kOutput, calls=%fused_computation.14 | convolution fusion | flops 6643777536 | bytes 16973824 | tf_op jit(solution)/shard_map/scjk,jkf->scf/dot_general | solution.py:56
  151.9 12.8 %fusion = bf16[32,36,1408]{2,1,0:T(8,128)(2,1)S(1)} fusion(f32[32,36,1408,1]{2,1,3,0:T(8,128)S(1)} %fusion.9, bf16[16,128,1408,1]{2,1,0,3:T(8,128)(2,1)} %bitcast.108, bf16[32,36,16,128]{3,2,1,0:T(8,128)(2,1)} %bitcast.5), kind=kOutput, calls=%fused_computation.3 | convolution fusion | flops 6653509632 | bytes 20217856 | tf_op jit(solution)/shard_map/scjk,jkf->scf/dot_general | solution.py:55
  164.8 9.1 %fusion.13 = bf16[32,36,16,128]{3,1,2,0:T(8,128)(2,1)S(1)} fusion(bf16[1408,16,128]{2,1,0:T(8,128)(2,1)S(1)} %bitcast.105, bf16[32,36,1408]{2,1,0:T(8,128)(2,1)S(1)} %fusion), kind=kOutput, calls=%fused_computation.20 | convolution fusion | flops 6646136832 | bytes 13729792 | tf_op jit(solution)/shard_map/scf,fjk->scjk/dot_general | solution.py:59
  173.9 3.1 %copy.24 = bf16[32,36,16,128]{3,2,1,0:T(8,128)(2,1)} copy(bf16[32,36,16,128]{3,1,2,0:T(8,128)(2,1)S(1)} %fusion.13) | data formatting | bytes 9437184 | tf_op jit(solution)/shard_map/convert_element_type | solution.py:62
  177.0 7.9 %all-to-all-start.1 = ((bf16[32,576,128]{2,1,0:T(8,128)(2,1)}), bf16[32,576,128]{2,1,0:T(8,128)(2,1)}, u32[]{:S(2)}, u32[]{:S(2)}) async-start(bf16[32,576,128]{2,1,0:T(8,128)(2,1)} %bitcast.100), calls=%async_computation.1 | async-start | bytes 9437184 | tf_op jit(solution)/shard_map/all_to_all | solution.py:63
  185.0 0.1 reshape.102
  185.2 3.4 %scatter_custom_fusion.1 = f32[1152]{0:T(1024)S(1)} fusion(s32[768]{0:T(1024)S(1)} %fusion.58, f32[768]{0:T(1024)S(1)} %reshape.102, f32[]{:T(128)} %constant.34.clone.1), kind=kCustom, calls=%fused_computation.64 | custom fusion | bytes 4612 | tf_op jit(solution)/shard_map/scatter | solution.py:67
  188.7 54.6 %all-to-all-done.1 = bf16[32,576,128]{2,1,0:T(8,128)(2,1)} async-done(((bf16[32,576,128]{2,1,0:T(8,128)(2,1)}), bf16[32,576,128]{2,1,0:T(8,128)(2,1)}, u32[]{:S(2)}, u32[]{:S(2)}) %all-to-all-start.1) | async-done | bytes 4718624 | tf_op jit(solution)/shard_map/all_to_all | solution.py:63
  243.3 5.9 %copy.60 = bf16[32,36,16,128]{3,2,0,1:T(8,128)(2,1)} copy(bf16[32,36,16,128]{3,2,1,0:T(8,128)(2,1)} %bitcast.18) | data formatting | bytes 9437184 | tf_op jit(solution)/shard_map/reshape | solution.py:66
  249.2 8.3 %dot_general.37 = bf16[2048,36,32]{0,2,1:T(8,128)(2,1)} reshape(bf16[16,128,36,32]{1,0,3,2:T(8,128)(2,1)} %bitcast.101) | data formatting | bytes 9437184 | tf_op jit(solution)/shard_map/rec,ecjk->rjk/dot_general | solution.py:73
  257.5 8.6 %fusion.29 = bf16[128,2048]{1,0:T(8,128)(2,1)} fusion(f32[128,2048]{1,0:T(8,128)} %reduce-scatter.2.cloned.1.call-done, f32[128,2048]{1,0:T(8,128)S(1)} %get-tuple-element.6, bf16[2048,36,32]{0,2,1:T(8,128)(2,1)} %dot_general.37, f32[32,36]{1,0:T(8,128)S(1)} %broadcast_in_dim.29, s32[32,36]{1,0:T(8,128)S(1)} %eq.61), kind=kOutput, calls=%fused_computation.27 | convolution fusion | flops 3624960000 | bytes 7349248 | tf_op jit(solution)/shard_map/rec,ecjk->rjk/dot_general | solution.py:73
  (29 shorter events, 0.6 us)
Async XLA Ops:
  6.5 112.5 %copy-start = (bf16[2048,352]{0,1:T(8,128)(2,1)S(1)}, bf16[2048,352]{0,1:T(8,128)(2,1)}, u32[]{:S(2)}) copy-start(bf16[2048,352]{0,1:T(8,128)(2,1)} %param.23) | copy-start | bytes 4325380
  6.5 59.5 %all-gather.3.cloned.1.call-start = ((), (), s32[]{:S(2)}) async-start(), calls=%async_computation.3 | async-start | bytes 8650752 | tf_op jit(solution)/shard_map/all_gather | solution.py:27
  15.0 56.1 %copy-start.2 = (f32[2048]{0:T(1024)S(1)}, f32[2048]{0:T(1024)}, u32[]{:S(2)}) copy-start(f32[2048]{0:T(1024)} %param.15) | copy-start | bytes 24580
  75.9 63.9 %all-to-all-start = ((bf16[32,576,128]{2,1,0:T(8,128)(2,1)}), bf16[32,576,128]{2,1,0:T(8,128)(2,1)}, u32[]{:S(2)}, u32[]{:S(2)}) async-start(bf16[32,576,128]{2,1,0:T(8,128)(2,1)} %bitcast.99), calls=%async_computation | async-start | bytes 9437184 | tf_op jit(solution)/shard_map/all_to_all | solution.py:49
  81.4 34.7 %all-gather.5.cloned.1.call-start = ((), (), s32[]{:S(2)}) async-start(), calls=%async_computation.4 | async-start | bytes 2621440 | tf_op jit(solution)/shard_map/all_gather | solution.py:81
  82.4 175.1 %reduce-scatter.2.cloned.1.call-start = ((), (), s32[]{:S(2)}) async-start(), calls=%async_computation.5 | async-start | bytes 5242880 | tf_op jit(solution)/shard_map/reduce_scatter | solution.py:88
  139.8 25.0 %slice-start = ((s8[5767168]{0:T(1024)(128)(4,1)}), s8[4194304]{0:T(1024)(128)(4,1)S(1)}, s32[]{:S(2)}) async-start(s8[5767168]{0:T(1024)(128)(4,1)} %bitcast.103), calls=%async_computation.6 | async-start | bytes 8388608
  151.9 12.9 %slice-start.1 = ((s8[5767168]{0:T(1024)(128)(4,1)}), s8[1572864]{0:T(1024)(128)(4,1)S(1)}, s32[]{:S(2)}) async-start(s8[5767168]{0:T(1024)(128)(4,1)} %bitcast.103), calls=%async_computation.7 | async-start | bytes 3145728
  177.0 7.9 %copy-start.3 = (f32[128,6]{0,1:T(8,128)S(1)}, f32[128,6]{0,1:T(8,128)}, u32[]{:S(2)}) copy-start(f32[128,6]{0,1:T(8,128)} %param.17) | copy-start | bytes 9220
  177.0 66.3 %all-to-all-start.1 = ((bf16[32,576,128]{2,1,0:T(8,128)(2,1)}), bf16[32,576,128]{2,1,0:T(8,128)(2,1)}, u32[]{:S(2)}, u32[]{:S(2)}) async-start(bf16[32,576,128]{2,1,0:T(8,128)(2,1)} %bitcast.100), calls=%async_computation.1 | async-start | bytes 9437184 | tf_op jit(solution)/shard_map/all_to_all | solution.py:63
  249.2 16.9 %copy-start.1 = (bf16[2048,352]{0,1:T(8,128)(2,1)S(1)}, bf16[2048,352]{0,1:T(8,128)(2,1)}, u32[]{:S(2)}) copy-start(bf16[2048,352]{0,1:T(8,128)(2,1)} %param.23) | copy-start | bytes 4325380
Sparse Core Ops, SparseCore 0:
  9.6 56.3 all-gather.2
  83.9 32.1 all-gather.4
  125.4 46.9 reduce-scatter.1

commit v3 on v1

--- a/solution.py
+++ b/solution.py
@@ -22,9 +22,12 @@
     topk = expert_ids.shape[1]
     experts = lax.axis_size("exp")
     capacity = min(row_count, 3 * row_count * topk // (2 * experts))
+    req = lax.axis_size("req")
+    quarter = out_weight.shape[0] // req
+    piece = lax.dynamic_slice_in_dim(out_weight, lax.axis_index("req") * quarter, quarter, 0)
     proj = jnp.dot(
         attn_out,
-        lax.all_gather(out_weight, "exp", axis=0, tiled=True),
+        lax.all_gather(piece, ("exp", "req"), axis=0, tiled=True),
         preferred_element_type=jnp.float32,
     )
     stream = (residual.astype(jnp.float32) + proj).astype(jnp.bfloat16)

time: 271 us -> 292 us (1.077)
  waiting for transfers between devices: 167 us -> 183 us
  local copies, waits for them, and re-layouts: 8.82 us -> 12.8 us
    all_gather x1, waiting for transfers between devices: 51.1 us -> 67.1 us  [body(): lax.all_gather(piece, ('exp', 'req'), axis=0, tiled=True)]
  transfers between devices with their start and end apart: 5 -> 5, of which waited for: 4 -> 4; matrix products, arithmetic and copies ran while one was open for 21% -> 20% of each run, Pallas kernels for 0% -> 0%
where the time goes in v3:
time: 292 us; the launch traced here: 289 us
  waiting for transfers between devices  183 us (63%)
  matrix products  62.9 us (22%)
  starting transfers between devices  14 us (5%)
  between operations  13.3 us (5%)
  local copies, waits for them, and re-layouts  12.8 us (4%)
  other arithmetic  2.96 us (1%)
    all_gather x1, waiting for transfers between devices, body(): lax.all_gather(piece, ('exp', 'req'), axis=0, tiled=True)  67.1 us
    all_to_all x1, waiting for transfers between devices, body(): lax.all_to_all(result, 'exp', split_axis=0, concat_axis=0, tiled=True)  60.8 us
    all_gather x1, waiting for transfers between devices, body(): group_rows = lax.all_gather(normed, 'req', axis=0, tiled=True)  35.2 us
    all_to_all x1, waiting for transfers between devices, body(): lax.all_to_all(outgoing, 'exp', split_axis=0, concat_axis=0, tiled=True)  19.3 us
    dot_general x1, matrix products, body(): jnp.einsum('scd,df->scf', joined, expert_gate[0], preferred_element_type=...  12.9 us
    dot_general x1, matrix products, body(): jnp.einsum('scd,df->scf', joined, expert_up[0], preferred_element_type=jn...  12.2 us
    dot_general x1, matrix products, body(): jnp.einsum('scf,fd->scd', hidden, expert_down[0], preferred_element_type=...  10.2 us
    all_to_all x1, starting transfers between devices, body(): lax.all_to_all(result, 'exp', split_axis=0, concat_axis=0, tiled=True)  9.04 us
  transfers between devices with their start and end apart: 5, of which 4 were waited for; matrix products, arithmetic and copies ran while one was open for 20% of the time, Pallas kernels for 0%

profile of v3, /device:TPU:1, one launch (start us, length us, event | category | flops | bytes accessed | tf_op | source)
XLA Modules:
  0.0 289.1 jit_solution(8442988998689780267)
XLA Ops:
  6.5 1.6 constant_dynamic-slice_fusion
  8.1 0.8 copy.20
  8.9 0.1 eq.57
  9.1 0.1 eq.53
  9.2 1.4 copy.18
  10.6 1.7 reduce-window.6
  12.3 0.3 slice_reduce_fusion
  12.6 0.7 broadcast_multiply_fusion
  13.3 0.1 copy.19
  13.4 0.1 mul.58
  13.8 3.4 %scatter_custom_fusion = s32[1152]{0:T(1024)S(1)} fusion(s32[768]{0:T(1024)S(1)} %fusion.38, s32[768]{0:T(1024)S(1)} %add_select_fusion, s32[]{:T(128)} %constant.21.clone.1), kind=kCustom, calls=%fused_computation.54 | custom fusion | bytes 4612 | tf_op jit(solution)/shard_map/scatter | solution.py:43
  17.3 67.1 %all-gather.3.cloned.1.call-done = bf16[2048,2048]{1,0:T(8,128)(2,1)} async-done(((bf16[16,2048]{1,0:T(8,128)(2,1)}), bf16[2048,2048]{1,0:T(8,128)(2,1)}) %all-gather.3.cloned.1.call-update) | async-done | bytes 8388624 | tf_op jit(solution)/shard_map/all_gather | solution.py:30
  84.4 5.8 %multiply_reduce_fusion = (f32[128]{0:T(128)S(1)}, f32[128,2048]{0,1:T(8,128)S(1)}) fusion(bf16[2048,2048]{1,0:T(8,128)(2,1)} %all-gather.3.cloned.1.call-done, bf16[128,2048]{1,0:T(8,128)(2,1)} %param.12, bf16[128,2048]{0,1:T(8,128)(2,1)S(1)} %copy.18), kind=kOutput, calls=%fused_computation.22 | convolution fusion | flops 1075314560 | bytes 10486272 | tf_op jit(solution)/shard_map/dot_general | solution.py:28
  90.2 0.3 multiply_convert_fusion.1
  90.6 3.9 %convolution_convert_fusion = bf16[32,36,2048]{2,1,0:T(8,128)(2,1)} fusion(bf16[128,2048]{0,1:T(8,128)(2,1)S(1)} %multiply_convert_fusion.1, s32[32,36]{1,0:T(8,128)S(1)} %eq.61), kind=kOutput, calls=%fused_computation.8 | convolution fusion | flops 606486528 | bytes 5247488 | tf_op jit(solution)/shard_map/ecr,rd->ecd/dot_general | solution.py:46
  94.5 4.7 %all-to-all-start = ((bf16[32,36,2048]{2,1,0:T(8,128)(2,1)}), bf16[32,36,2048]{2,1,0:T(8,128)(2,1)}, u32[]{:S(2)}, u32[]{:S(2)}) async-start(bf16[32,36,2048]{2,1,0:T(8,128)(2,1)} %convolution_convert_fusion), calls=%async_computation | async-start | bytes 10485760 | tf_op jit(solution)/shard_map/all_to_all | solution.py:49
  99.3 0.7 all-gather.5.cloned.1.call-update
  100.0 0.2 reduce-scatter.2.cloned.1.call-start
  100.2 35.2 %all-gather.5.cloned.1.call-done = bf16[512,2048]{0,1:T(8,128)(2,1)} async-done(((bf16[128,2048]{0,1:T(8,128)(2,1)}), bf16[512,2048]{0,1:T(8,128)(2,1)}) %all-gather.5.cloned.1.call-update) | async-done | bytes 2097168 | tf_op jit(solution)/shard_map/all_gather | solution.py:72
  135.4 2.9 %fusion.41 = f32[512,352]{0,1:T(8,128)S(1)} fusion(bf16[2048,352]{0,1:T(8,128)(2,1)} %param.21, bf16[512,2048]{0,1:T(8,128)(2,1)} %all-gather.5.cloned.1.call-done), kind=kOutput, calls=%fused_computation.64 | convolution fusion | flops 738197504 | bytes 4259840 | tf_op jit(solution)/shard_map/dot_general | solution.py:73
  138.3 6.2 %fusion.15 = f32[512,2048]{0,1:T(8,128)} fusion(bf16[2048,352]{0,1:T(8,128)(2,1)S(1)} %copy-done, bf16[2048,352]{0,1:T(8,128)(2,1)} %param.22, bf16[512,2048]{0,1:T(8,128)(2,1)} %all-gather.5.cloned.1.call-done, f32[512,352]{0,1:T(8,128)S(1)} %fusion.41), kind=kOutput, calls=%fused_computation.20 | convolution fusion | flops 1477476352 | bytes 9895936 | tf_op jit(solution)/shard_map/dot_general | solution.py:76
  144.6 19.3 %all-to-all-done = bf16[32,36,2048]{2,1,0:T(8,128)(2,1)} async-done(((bf16[32,36,2048]{2,1,0:T(8,128)(2,1)}), bf16[32,36,2048]{2,1,0:T(8,128)(2,1)}, u32[]{:S(2)}, u32[]{:S(2)}) %all-to-all-start) | async-done | bytes 4718624 | tf_op jit(solution)/shard_map/all_to_all | solution.py:49
  163.9 12.2 %fusion.2 = f32[32,36,1408]{2,1,0:T(8,128)S(1)} fusion(bf16[32,36,2048]{2,1,0:T(8,128)(2,1)} %all-to-all-done, bf16[1,2048,1408]{2,1,0:T(8,128)(2,1)} %param.19), kind=kOutput, calls=%fused_computation.5 | convolution fusion | flops 6643777536 | bytes 16973824 | tf_op jit(solution)/shard_map/scd,df->scf/dot_general | solution.py:51
  176.1 12.9 %multiply_convert_fusion = bf16[32,36,1408]{2,1,0:T(8,128)(2,1)S(1)} fusion(f32[32,36,1408]{2,1,0:T(8,128)S(1)} %fusion.2, bf16[32,36,2048]{2,1,0:T(8,128)(2,1)} %all-to-all-done, bf16[1,2048,1408]{2,1,0:T(8,128)(2,1)} %param.18), kind=kOutput, calls=%fused_computation.2 | convolution fusion | flops 6653509632 | bytes 20217856 | tf_op jit(solution)/shard_map/scd,df->scf/dot_general | solution.py:50
  189.0 10.2 %fusion.5 = bf16[32,36,2048]{2,1,0:T(8,128)(2,1)} fusion(bf16[32,36,1408]{2,1,0:T(8,128)(2,1)S(1)} %multiply_convert_fusion, bf16[1,1408,2048]{2,1,0:T(8,128)(2,1)S(1)} %bitcast.62), kind=kOutput, calls=%fused_computation.9 | convolution fusion | flops 6646136832 | bytes 13729792 | tf_op jit(solution)/shard_map/scf,fd->scd/dot_general | solution.py:54
  199.2 9.0 %all-to-all-start.1 = ((bf16[32,36,2048]{2,1,0:T(8,128)(2,1)}), bf16[32,36,2048]{2,1,0:T(8,128)(2,1)}, u32[]{:S(2)}, u32[]{:S(2)}) async-start(bf16[32,36,2048]{2,1,0:T(8,128)(2,1)} %fusion.5), calls=%async_computation.1 | async-start | bytes 10485760 | tf_op jit(solution)/shard_map/all_to_all | solution.py:57
  208.3 0.1 copy.23
  208.4 0.1 reshape.80
  208.5 3.4 %scatter_custom_fusion.1 = f32[1152]{0:T(1024)S(1)} fusion(s32[768]{0:T(1024)S(1)} %fusion.38, f32[768]{0:T(1024)S(1)} %reshape.80, f32[]{:T(128)} %constant.44.clone.1), kind=kCustom, calls=%fused_computation.52 | custom fusion | bytes 4612 | tf_op jit(solution)/shard_map/scatter | solution.py:58
  212.0 60.8 %all-to-all-done.1 = bf16[32,36,2048]{2,1,0:T(8,128)(2,1)} async-done(((bf16[32,36,2048]{2,1,0:T(8,128)(2,1)}), bf16[32,36,2048]{2,1,0:T(8,128)(2,1)}, u32[]{:S(2)}, u32[]{:S(2)}) %all-to-all-start.1) | async-done | bytes 4718624 | tf_op jit(solution)/shard_map/all_to_all | solution.py:57
  272.8 8.7 %fusion.11 = bf16[128,2048]{0,1:T(8,128)(2,1)S(1)} fusion(f32[128,2048]{0,1:T(8,128)} %reduce-scatter.2.cloned.1.call-done, f32[128,2048]{0,1:T(8,128)S(1)} %get-tuple-element.6, bf16[32,36,2048]{2,1,0:T(8,128)(2,1)} %all-to-all-done.1, f32[32,36]{1,0:T(8,128)S(1)} %broadcast_in_dim.29, s32[32,36]{1,0:T(8,128)S(1)} %eq.61), kind=kOutput, calls=%fused_computation.15 | convolution fusion | flops 3624960000 | bytes 7349248 | tf_op jit(solution)/shard_map/rec,ecd->rd/dot_general | solution.py:64
  281.6 1.0 copy.27
  (29 shorter events, 0.5 us)
Async XLA Ops:
  6.5 131.8 %copy-start = (bf16[2048,352]{0,1:T(8,128)(2,1)S(1)}, bf16[2048,352]{0,1:T(8,128)(2,1)}, u32[]{:S(2)}) copy-start(bf16[2048,352]{0,1:T(8,128)(2,1)} %param.23) | copy-start | bytes 4325380
  6.5 77.8 %all-gather.3.cloned.1.call-start = ((), (), s32[]{:S(2)}) async-start(), calls=%async_computation.3 | async-start | bytes 8454144 | tf_op jit(solution)/shard_map/all_gather | solution.py:30
  17.2 73.0 %copy-start.3 = (f32[2048]{0:T(1024)S(1)}, f32[2048]{0:T(1024)}, u32[]{:S(2)}) copy-start(f32[2048]{0:T(1024)} %param.15) | copy-start | bytes 24580
  90.6 3.9 %copy-start.2 = (bf16[128,2048]{0,1:T(8,128)(2,1)}, bf16[128,2048]{0,1:T(8,128)(2,1)S(1)}, u32[]{:S(2)}) copy-start(bf16[128,2048]{0,1:T(8,128)(2,1)S(1)} %multiply_convert_fusion.1) | copy-start | bytes 1572868
  94.5 69.4 %all-to-all-start = ((bf16[32,36,2048]{2,1,0:T(8,128)(2,1)}), bf16[32,36,2048]{2,1,0:T(8,128)(2,1)}, u32[]{:S(2)}, u32[]{:S(2)}) async-start(bf16[32,36,2048]{2,1,0:T(8,128)(2,1)} %convolution_convert_fusion), calls=%async_computation | async-start | bytes 10485760 | tf_op jit(solution)/shard_map/all_to_all | solution.py:49
  99.2 36.2 %all-gather.5.cloned.1.call-start = ((), (), s32[]{:S(2)}) async-start(), calls=%async_computation.4 | async-start | bytes 2621440 | tf_op jit(solution)/shard_map/all_gather | solution.py:72
  100.0 172.9 %reduce-scatter.2.cloned.1.call-start = ((), (), s32[]{:S(2)}) async-start(), calls=%async_computation.5 | async-start | bytes 5242880 | tf_op jit(solution)/shard_map/reduce_scatter | solution.py:79
  163.9 25.1 %slice-start = ((s8[5767168]{0:T(1024)(128)(4,1)}), s8[4194304]{0:T(1024)(128)(4,1)S(1)}, s32[]{:S(2)}) async-start(s8[5767168]{0:T(1024)(128)(4,1)} %bitcast.61), calls=%async_computation.6 | async-start | bytes 8388608
  176.0 12.9 %slice-start.1 = ((s8[5767168]{0:T(1024)(128)(4,1)}), s8[1572864]{0:T(1024)(128)(4,1)S(1)}, s32[]{:S(2)}) async-start(s8[5767168]{0:T(1024)(128)(4,1)} %bitcast.61), calls=%async_computation.7 | async-start | bytes 3145728
  199.2 9.1 %copy-start.4 = (f32[128,6]{0,1:T(8,128)S(1)}, f32[128,6]{0,1:T(8,128)}, u32[]{:S(2)}) copy-start(f32[128,6]{0,1:T(8,128)} %param.17) | copy-start | bytes 9220
  199.2 73.6 %all-to-all-start.1 = ((bf16[32,36,2048]{2,1,0:T(8,128)(2,1)}), bf16[32,36,2048]{2,1,0:T(8,128)(2,1)}, u32[]{:S(2)}, u32[]{:S(2)}) async-start(bf16[32,36,2048]{2,1,0:T(8,128)(2,1)} %fusion.5), calls=%async_computation.1 | async-start | bytes 10485760 | tf_op jit(solution)/shard_map/all_to_all | solution.py:57
  208.3 74.3 %copy-start.1 = (bf16[2048,352]{0,1:T(8,128)(2,1)S(1)}, bf16[2048,352]{0,1:T(8,128)(2,1)}, u32[]{:S(2)}) copy-start(bf16[2048,352]{0,1:T(8,128)(2,1)} %param.23) | copy-start | bytes 4325380
Sparse Core Ops, SparseCore 0:
  10.5 73.8 all-gather.2
  101.7 33.6 all-gather.4
  144.7 48.7 reduce-scatter.1

commit v4 on v1

--- a/solution.py
+++ b/solution.py
@@ -40,31 +40,49 @@
     table = jnp.full((experts * capacity,), row_count, jnp.int32).at[slot].set(source_row)
     rows = jnp.arange(row_count, dtype=jnp.int32)
     pick = (table.reshape(experts, capacity)[:, :, None] == rows[None, None, :]).astype(jnp.bfloat16)
-    outgoing = jnp.einsum(
-        "ecr,rd->ecd", pick, normed, preferred_element_type=jnp.float32
-    ).astype(jnp.bfloat16)
-    joined = lax.all_to_all(outgoing, "exp", split_axis=0, concat_axis=0, tiled=True)
-    gate_part = jnp.einsum("scd,df->scf", joined, expert_gate[0], preferred_element_type=jnp.float32)
-    up_part = jnp.einsum("scd,df->scf", joined, expert_up[0], preferred_element_type=jnp.float32)
+    half = width // 2
+    joined = []
+    for part in range(2):
+        cols = normed[:, part * half:(part + 1) * half]
+        outgoing = jnp.einsum(
+            "ecr,rd->ecd", pick, cols, preferred_element_type=jnp.float32
+        ).astype(jnp.bfloat16)
+        joined.append(lax.all_to_all(outgoing, "exp", split_axis=0, concat_axis=0, tiled=True))
+    w_gate, w_up, w_down = expert_gate[0], expert_up[0], expert_down[0]
+    gate_part = sum(
+        jnp.einsum("scd,df->scf", joined[p], w_gate[p * half:(p + 1) * half],
+                   preferred_element_type=jnp.float32)
+        for p in range(2)
+    )
+    up_part = sum(
+        jnp.einsum("scd,df->scf", joined[p], w_up[p * half:(p + 1) * half],
+                   preferred_element_type=jnp.float32)
+        for p in range(2)
+    )
     hidden = (jax.nn.silu(gate_part) * up_part).astype(jnp.bfloat16)
-    hidden = lax.optimization_barrier(hidden)
-    result = jnp.einsum(
-        "scf,fd->scd", hidden, expert_down[0], preferred_element_type=jnp.float32
-    ).astype(jnp.bfloat16)
-    returned = lax.all_to_all(result, "exp", split_axis=0, concat_axis=0, tiled=True)
+    returned = []
+    for part in range(2):
+        result = jnp.einsum(
+            "scf,fd->scd", hidden, w_down[:, part * half:(part + 1) * half],
+            preferred_element_type=jnp.float32,
+        ).astype(jnp.bfloat16)
+        returned.append(lax.all_to_all(result, "exp", split_axis=0, concat_axis=0, tiled=True))
     slot_weight = jnp.zeros((experts * capacity,), jnp.float32).at[slot].set(gate_weights.reshape(-1))
     combine = jnp.where(
         table.reshape(experts, capacity)[None, :, :] == rows[:, None, None],
         slot_weight.reshape(experts, capacity)[None, :, :],
         0.0,
     )
-    routed = jnp.einsum(
-        "rec,ecd->rd",
-        combine,
-        returned.astype(jnp.float32),
-        precision=lax.Precision.HIGHEST,
-        preferred_element_type=jnp.float32,
-    )
+    routed = jnp.concatenate([
+        jnp.einsum(
+            "rec,ecd->rd",
+            combine,
+            returned[p].astype(jnp.float32),
+            precision=lax.Precision.HIGHEST,
+            preferred_element_type=jnp.float32,
+        )
+        for p in range(2)
+    ], axis=1)
 
     group_rows = lax.all_gather(normed, "req", axis=0, tiled=True)
     s_gate = jnp.dot(group_rows, shared_gate, preferred_element_type=jnp.float32)

time: 271 us -> 276 us (1.018)
  waiting for transfers between devices: 167 us -> 138 us
  matrix products: 60.6 us -> 86 us
  starting transfers between devices: 15.7 us -> 21.9 us
    all_gather x1, waiting for transfers between devices: 33.7 us -> 0.01 us  [body(): group_rows = lax.all_gather(normed, 'req', axis=0, tiled=True)]
    dot_general x5 -> x10, matrix products: 45.4 us -> 70.9 us  [the longest x2 24.2 us: body(): jnp.einsum('scd,df->scf', joined[p], w_up[p * half:(p + 1) * half], prefe...]
    all_to_all x1 -> x2, waiting for transfers between devices: 19.6 us -> 34 us  [body(): lax.all_to_all(outgoing, 'exp', split_axis=0, concat_axis=0, tiled=True)]
    all_to_all x1 -> x2, waiting for transfers between devices: 60.9 us -> 51.7 us  [body(): lax.all_to_all(result, 'exp', split_axis=0, concat_axis=0, tiled=True)]
    all_to_all x1 -> x2, starting transfers between devices: 5.52 us -> 10.9 us  [body(): lax.all_to_all(outgoing, 'exp', split_axis=0, concat_axis=0, tiled=True)]
    all_to_all x1 -> x2, starting transfers between devices: 9.95 us -> 10.8 us  [body(): lax.all_to_all(result, 'exp', split_axis=0, concat_axis=0, tiled=True)]
  transfers between devices with their start and end apart: 5 -> 7, of which waited for: 4 -> 5; matrix products, arithmetic and copies ran while one was open for 21% -> 33% of each run, Pallas kernels for 0% -> 0%
where the time goes in v4:
time: 276 us; the launch traced here: 275 us
  waiting for transfers between devices  138 us (50%)
  matrix products  86 us (31%)
  starting transfers between devices  21.9 us (8%)
  between operations  13.3 us (5%)
  local copies, waits for them, and re-layouts  11 us (4%)
  other arithmetic  4.96 us (2%)
    all_to_all x2, waiting for transfers between devices, body(): lax.all_to_all(result, 'exp', split_axis=0, concat_axis=0, tiled=True)  51.7 us
    all_gather x1, waiting for transfers between devices, body(): lax.all_gather(out_weight, 'exp', axis=0, tiled=True)  51.1 us
    all_to_all x2, waiting for transfers between devices, body(): lax.all_to_all(outgoing, 'exp', split_axis=0, concat_axis=0, tiled=True)  34 us
    dot_general x2, matrix products, body(): jnp.einsum('scd,df->scf', joined[p], w_up[p * half:(p + 1) * half], prefe...  24.2 us
    dot_general x2, matrix products, body(): jnp.einsum('scd,df->scf', joined[p], w_gate[p * half:(p + 1) * half], pre...  19.7 us
    dot_general x2, matrix products, body(): jnp.einsum('scf,fd->scd', hidden, w_down[:, part * half:(part + 1) * half...  14.4 us
    all_to_all x2, starting transfers between devices, body(): lax.all_to_all(outgoing, 'exp', split_axis=0, concat_axis=0, tiled=True)  10.9 us
    all_to_all x2, starting transfers between devices, body(): lax.all_to_all(result, 'exp', split_axis=0, concat_axis=0, tiled=True)  10.8 us
  transfers between devices with their start and end apart: 7, of which 5 were waited for; matrix products, arithmetic and copies ran while one was open for 33% of the time, Pallas kernels for 0%

profile of v4, /device:TPU:1, one launch (start us, length us, event | category | flops | bytes accessed | tf_op | source)
XLA Modules:
  0.0 275.3 jit_solution(15110559170019796313)
XLA Ops:
  6.5 0.7 all-gather.3.cloned.1.call-update
  7.3 0.8 copy.14
  8.3 1.7 reduce-window.6
  10.1 0.3 slice_reduce_fusion
  10.4 0.7 broadcast_multiply_fusion
  11.5 3.4 %scatter_custom_fusion = s32[1152]{0:T(1024)S(1)} fusion(s32[768]{0:T(1024)S(1)} %fusion.47, s32[768]{0:T(1024)S(1)} %add_select_fusion, s32[]{:T(128)} %constant.11.clone.1), kind=kCustom, calls=%fused_computation.72 | custom fusion | bytes 4612 | tf_op jit(solution)/shard_map/scatter | solution.py:40
  15.0 51.1 %all-gather.3.cloned.1.call-done = bf16[2048,2048]{1,0:T(8,128)(2,1)} async-done(((bf16[64,2048]{1,0:T(8,128)(2,1)}), bf16[2048,2048]{1,0:T(8,128)(2,1)}) %all-gather.3.cloned.1.call-update) | async-done | bytes 8388624 | tf_op jit(solution)/shard_map/all_gather | solution.py:27
  66.1 5.0 %multiply_reduce_fusion = (f32[128]{0:T(128)S(1)}, f32[128,2048]{1,0:T(8,128)S(1)}) fusion(bf16[128,2048]{1,0:T(8,128)(2,1)} %param.12, bf16[2048,2048]{1,0:T(8,128)(2,1)} %all-gather.3.cloned.1.call-done, bf16[128,2048]{1,0:T(8,128)(2,1)} %param.13), kind=kOutput, calls=%fused_computation.34 | convolution fusion | flops 1075314560 | bytes 10486272 | tf_op jit(solution)/shard_map/dot_general | solution.py:25
  71.2 2.4 convolution_convert_fusion.1
  73.6 5.5 %all-to-all-start = ((bf16[32,36,1024]{2,1,0:T(8,128)(2,1)}), bf16[32,36,1024]{2,1,0:T(8,128)(2,1)}, u32[]{:S(2)}, u32[]{:S(2)}) async-start(bf16[32,36,1024]{2,1,0:T(8,128)(2,1)} %convolution_convert_fusion.1), calls=%async_computation | async-start | bytes 5242880 | tf_op jit(solution)/shard_map/all_to_all | solution.py:50
  79.2 0.7 all-gather.5.cloned.1.call-update
  79.9 3.3 %convolution_convert_fusion = bf16[32,36,1024]{2,1,0:T(8,128)(2,1)} fusion(s32[32,36]{1,0:T(8,128)S(1)} %eq.61, bf16[128,2048]{1,0:T(8,128)(2,1)} %copy-done.2), kind=kOutput, calls=%fused_computation.23 | convolution fusion | flops 303316992 | bytes 2626048 | tf_op jit(solution)/shard_map/ecr,rd->ecd/dot_general | solution.py:47
  83.2 29.9 %all-to-all-done = bf16[32,36,1024]{2,1,0:T(8,128)(2,1)} async-done(((bf16[32,36,1024]{2,1,0:T(8,128)(2,1)}), bf16[32,36,1024]{2,1,0:T(8,128)(2,1)}, u32[]{:S(2)}, u32[]{:S(2)}) %all-to-all-start) | async-done | bytes 2359328 | tf_op jit(solution)/shard_map/all_to_all | solution.py:50
  113.1 5.4 %all-to-all-start.1 = ((bf16[32,36,1024]{2,1,0:T(8,128)(2,1)}), bf16[32,36,1024]{2,1,0:T(8,128)(2,1)}, u32[]{:S(2)}, u32[]{:S(2)}) async-start(bf16[32,36,1024]{2,1,0:T(8,128)(2,1)} %convolution_convert_fusion), calls=%async_computation.1 | async-start | bytes 5242880 | tf_op jit(solution)/shard_map/all_to_all | solution.py:50
  118.7 9.8 %fusion.3 = f32[32,36,1408]{2,1,0:T(8,128)} fusion(bf16[32,36,1024]{2,1,0:T(8,128)(2,1)} %all-to-all-done, bf16[1,2048,1408]{2,1,0:T(8,128)(2,1)} %param.19), kind=kOutput, calls=%fused_computation.8 | convolution fusion | flops 3321888768 | bytes 11993088 | tf_op jit(solution)/shard_map/scd,df->scf/dot_general | solution.py:58
  128.5 9.8 %fusion.7 = f32[32,36,1408]{2,1,0:T(8,128)} fusion(bf16[32,36,1024]{2,1,0:T(8,128)(2,1)} %all-to-all-done, bf16[1,2048,1408]{2,1,0:T(8,128)(2,1)} %param.18), kind=kOutput, calls=%fused_computation.12 | convolution fusion | flops 3321888768 | bytes 11993088 | tf_op jit(solution)/shard_map/scd,df->scf/dot_general | solution.py:53
  138.3 3.8 %fusion.51 = f32[512,352]{0,1:T(8,128)} fusion(bf16[512,2048]{1,0:T(8,128)(2,1)} %all-gather.5.cloned.1.call-done, bf16[2048,352]{0,1:T(8,128)(2,1)} %param.21), kind=kOutput, calls=%fused_computation.82 | convolution fusion | flops 738197504 | bytes 4259840 | tf_op jit(solution)/shard_map/dot_general | solution.py:88
  142.1 6.3 %fusion.18 = f32[512,2048]{1,0:T(8,128)} fusion(bf16[2048,352]{0,1:T(8,128)(2,1)S(1)} %copy-done, bf16[512,2048]{1,0:T(8,128)(2,1)} %all-gather.5.cloned.1.call-done, bf16[2048,352]{0,1:T(8,128)(2,1)} %param.22, f32[512,352]{0,1:T(8,128)} %fusion.51), kind=kOutput, calls=%fused_computation.29 | convolution fusion | flops 1477476352 | bytes 9895936 | tf_op jit(solution)/shard_map/dot_general | solution.py:91
  148.4 4.1 %all-to-all-done.1 = bf16[32,36,1024]{2,1,0:T(8,128)(2,1)} async-done(((bf16[32,36,1024]{2,1,0:T(8,128)(2,1)}), bf16[32,36,1024]{2,1,0:T(8,128)(2,1)}, u32[]{:S(2)}, u32[]{:S(2)}) %all-to-all-start.1) | async-done | bytes 2359328 | tf_op jit(solution)/shard_map/all_to_all | solution.py:50
  152.5 9.9 %fusion.5 = f32[32,36,1408]{2,1,0:T(8,128)} fusion(bf16[32,36,1024]{2,1,0:T(8,128)(2,1)} %all-to-all-done.1, bf16[1,2048,1408]{2,1,0:T(8,128)(2,1)} %param.18), kind=kOutput, calls=%fused_computation.10 | convolution fusion | flops 3321888768 | bytes 11993088 | tf_op jit(solution)/shard_map/scd,df->scf/dot_general | solution.py:53
  162.4 14.3 %multiply_convert_fusion = bf16[32,36,1408]{2,1,0:T(8,128)(2,1)S(1)} fusion(f32[32,36,1408]{2,1,0:T(8,128)} %fusion.3, f32[32,36,1408]{2,1,0:T(8,128)} %fusion.7, f32[32,36,1408]{2,1,0:T(8,128)} %fusion.5, bf16[32,36,1024]{2,1,0:T(8,128)(2,1)} %all-to-all-done.1, bf16[1,2048,1408]{2,1,0:T(8,128)(2,1)} %param.19), kind=kOutput, calls=%fused_computation.2 | convolution fusion | flops 3334864896 | bytes 30375936 | tf_op jit(solution)/shard_map/scd,df->scf/dot_general | solution.py:58
  176.8 1.9 copy-done.6
  178.7 5.6 %fusion.15 = bf16[32,36,1024]{2,1,0:T(8,128)(2,1)} fusion(bf16[32,36,1408]{2,1,0:T(8,128)(2,1)S(1)} %multiply_convert_fusion, bf16[1408,2048]{1,0:T(8,128)(2,1)S(1)} %bitcast.72), kind=kOutput, calls=%fused_computation.21 | convolution fusion | flops 3323068416 | bytes 8847360 | tf_op jit(solution)/shard_map/scf,fd->scd/dot_general | solution.py:65
  184.3 5.4 %all-to-all-start.2 = ((bf16[32,36,1024]{2,1,0:T(8,128)(2,1)}), bf16[32,36,1024]{2,1,0:T(8,128)(2,1)}, u32[]{:S(2)}, u32[]{:S(2)}) async-start(bf16[32,36,1024]{2,1,0:T(8,128)(2,1)} %fusion.15), calls=%async_computation.2 | async-start | bytes 5242880 | tf_op jit(solution)/shard_map/all_to_all | solution.py:69
  189.7 8.8 %fusion.16 = bf16[32,36,1024]{2,1,0:T(8,128)(2,1)} fusion(bf16[32,36,1408]{2,1,0:T(8,128)(2,1)} %copy-done.6, bf16[1408,2048]{1,0:T(8,128)(2,1)} %bitcast.69), kind=kOutput, calls=%fused_computation.22 | convolution fusion | flops 3323068416 | bytes 8847360 | tf_op jit(solution)/shard_map/scf,fd->scd/dot_general | solution.py:65
  198.5 25.2 %all-to-all-done.2 = bf16[32,36,1024]{2,1,0:T(8,128)(2,1)} async-done(((bf16[32,36,1024]{2,1,0:T(8,128)(2,1)}), bf16[32,36,1024]{2,1,0:T(8,128)(2,1)}, u32[]{:S(2)}, u32[]{:S(2)}) %all-to-all-start.2) | async-done | bytes 2359328 | tf_op jit(solution)/shard_map/all_to_all | solution.py:69
  223.7 5.4 %all-to-all-start.3 = ((bf16[32,36,1024]{2,1,0:T(8,128)(2,1)}), bf16[32,36,1024]{2,1,0:T(8,128)(2,1)}, u32[]{:S(2)}, u32[]{:S(2)}) async-start(bf16[32,36,1024]{2,1,0:T(8,128)(2,1)} %fusion.16), calls=%async_computation.3 | async-start | bytes 5242880 | tf_op jit(solution)/shard_map/all_to_all | solution.py:69
  229.4 3.6 %scatter_custom_fusion.1 = f32[1152]{0:T(1024)S(1)} fusion(s32[768]{0:T(1024)S(1)} %fusion.47, f32[768]{0:T(1024)S(1)} %reshape.84, f32[]{:T(128)} %constant.34.clone.1), kind=kCustom, calls=%fused_computation.70 | custom fusion | bytes 4612 | tf_op jit(solution)/shard_map/scatter | solution.py:70
  233.2 3.5 %convolution_bitcast_fusion.1 = f32[128,1024]{1,0:T(8,128)S(1)} fusion(bf16[32,36,1024]{2,1,0:T(8,128)(2,1)} %all-to-all-done.2, f32[32,36]{1,0:T(8,128)S(1)} %broadcast_in_dim.29, s32[32,36]{1,0:T(8,128)S(1)} %eq.61), kind=kOutput, calls=%fused_computation.28 | convolution fusion | flops 1812234240 | bytes 2892800 | tf_op jit(solution)/shard_map/rec,ecd->rd/dot_general | solution.py:77
  236.7 26.4 %all-to-all-done.3 = bf16[32,36,1024]{2,1,0:T(8,128)(2,1)} async-done(((bf16[32,36,1024]{2,1,0:T(8,128)(2,1)}), bf16[32,36,1024]{2,1,0:T(8,128)(2,1)}, u32[]{:S(2)}, u32[]{:S(2)}) %all-to-all-start.3) | async-done | bytes 2359328 | tf_op jit(solution)/shard_map/all_to_all | solution.py:69
  263.1 3.4 %convolution_bitcast_fusion = f32[128,1024]{1,0:T(8,128)S(1)} fusion(bf16[32,36,1024]{2,1,0:T(8,128)(2,1)} %all-to-all-done.3, f32[32,36]{1,0:T(8,128)} %copy-done.3, s32[32,36]{1,0:T(8,128)S(1)} %eq.61), kind=kOutput, calls=%fused_computation.27 | convolution fusion | flops 1812234240 | bytes 2892800 | tf_op jit(solution)/shard_map/rec,ecd->rd/dot_general | solution.py:77
  266.6 2.2 fusion.20
  (40 shorter events, 1.6 us)
Async XLA Ops:
  6.5 135.6 %copy-start = (bf16[2048,352]{0,1:T(8,128)(2,1)S(1)}, bf16[2048,352]{0,1:T(8,128)(2,1)}, u32[]{:S(2)}) copy-start(bf16[2048,352]{0,1:T(8,128)(2,1)} %param.23) | copy-start | bytes 4325380
  6.5 59.5 %all-gather.3.cloned.1.call-start = ((), (), s32[]{:S(2)}) async-start(), calls=%async_computation.5 | async-start | bytes 8650752 | tf_op jit(solution)/shard_map/all_gather | solution.py:27
  15.0 56.0 %copy-start.4 = (f32[2048]{0:T(1024)S(1)}, f32[2048]{0:T(1024)}, u32[]{:S(2)}) copy-start(f32[2048]{0:T(1024)} %param.15) | copy-start | bytes 24580
  71.2 2.4 copy-start.2
  73.6 39.5 %all-to-all-start = ((bf16[32,36,1024]{2,1,0:T(8,128)(2,1)}), bf16[32,36,1024]{2,1,0:T(8,128)(2,1)}, u32[]{:S(2)}, u32[]{:S(2)}) async-start(bf16[32,36,1024]{2,1,0:T(8,128)(2,1)} %convolution_convert_fusion.1), calls=%async_computation | async-start | bytes 5242880 | tf_op jit(solution)/shard_map/all_to_all | solution.py:50
  79.1 59.2 %all-gather.5.cloned.1.call-start = ((), (), s32[]{:S(2)}) async-start(), calls=%async_computation.6 | async-start | bytes 2621440 | tf_op jit(solution)/shard_map/all_gather | solution.py:87
  113.1 39.4 %all-to-all-start.1 = ((bf16[32,36,1024]{2,1,0:T(8,128)(2,1)}), bf16[32,36,1024]{2,1,0:T(8,128)(2,1)}, u32[]{:S(2)}, u32[]{:S(2)}) async-start(bf16[32,36,1024]{2,1,0:T(8,128)(2,1)} %convolution_convert_fusion), calls=%async_computation.1 | async-start | bytes 5242880 | tf_op jit(solution)/shard_map/all_to_all | solution.py:50
  118.5 148.1 %reduce-scatter.2.cloned.1.call-start = ((), (), s32[]{:S(2)}) async-start(), calls=%async_computation.7 | async-start | bytes 5242880 | tf_op jit(solution)/shard_map/reduce_scatter | solution.py:94
  152.5 26.2 %slice-start = ((s8[5767168]{0:T(1024)(128)(4,1)}), s8[4194304]{0:T(1024)(128)(4,1)S(1)}, s32[]{:S(2)}) async-start(s8[5767168]{0:T(1024)(128)(4,1)} %bitcast.70), calls=%async_computation.8 | async-start | bytes 8388608
  162.4 16.3 %slice-start.1 = ((s8[5767168]{0:T(1024)(128)(4,1)}), s8[1572864]{0:T(1024)(128)(4,1)S(1)}, s32[]{:S(2)}) async-start(s8[5767168]{0:T(1024)(128)(4,1)} %bitcast.70), calls=%async_computation.9 | async-start | bytes 3145728
  176.8 1.9 copy-start.6
  184.3 39.4 %all-to-all-start.2 = ((bf16[32,36,1024]{2,1,0:T(8,128)(2,1)}), bf16[32,36,1024]{2,1,0:T(8,128)(2,1)}, u32[]{:S(2)}, u32[]{:S(2)}) async-start(bf16[32,36,1024]{2,1,0:T(8,128)(2,1)} %fusion.15), calls=%async_computation.2 | async-start | bytes 5242880 | tf_op jit(solution)/shard_map/all_to_all | solution.py:69
  198.5 30.6 %copy-start.5 = (f32[128,6]{0,1:T(8,128)S(1)}, f32[128,6]{0,1:T(8,128)}, u32[]{:S(2)}) copy-start(f32[128,6]{0,1:T(8,128)} %param.17) | copy-start | bytes 9220
  223.7 39.4 %all-to-all-start.3 = ((bf16[32,36,1024]{2,1,0:T(8,128)(2,1)}), bf16[32,36,1024]{2,1,0:T(8,128)(2,1)}, u32[]{:S(2)}, u32[]{:S(2)}) async-start(bf16[32,36,1024]{2,1,0:T(8,128)(2,1)} %fusion.16), calls=%async_computation.3 | async-start | bytes 5242880 | tf_op jit(solution)/shard_map/all_to_all | solution.py:69
  233.1 3.6 %copy-start.3 = (f32[32,36]{1,0:T(8,128)}, f32[32,36]{1,0:T(8,128)S(1)}, u32[]{:S(2)}) copy-start(f32[32,36]{1,0:T(8,128)S(1)} %broadcast_in_dim.29) | copy-start | bytes 13828
  233.1 35.7 %copy-start.1 = (bf16[2048,352]{0,1:T(8,128)(2,1)S(1)}, bf16[2048,352]{0,1:T(8,128)(2,1)}, u32[]{:S(2)}) copy-start(bf16[2048,352]{0,1:T(8,128)(2,1)} %param.23) | copy-start | bytes 4325380
Sparse Core Ops, SparseCore 0:
  9.6 56.3 all-gather.2
  81.7 32.1 all-gather.4
  148.6 48.2 reduce-scatter.1

commit v5 on v1

--- a/solution.py
+++ b/solution.py
@@ -2,6 +2,53 @@
 import jax.numpy as jnp
 from jax import lax
 from jax.sharding import PartitionSpec as P
+from jax.experimental import pallas as pl
+from jax.experimental.pallas import tpu as pltpu
+
+
+def _exchange_kernel(x_hbm, o_hbm, send_sems, recv_sems, local_sem):
+    n = lax.axis_size("exp")
+    me = lax.axis_index("exp")
+    grp = lax.axis_index("req")
+    mesh_id = pl.DeviceIdType.MESH
+    barrier = pltpu.get_barrier_semaphore()
+    for k in range(1, n):
+        pl.semaphore_signal(barrier, 1, device_id=(grp, lax.rem(me + k, n)), device_id_type=mesh_id)
+    pl.semaphore_wait(barrier, n - 1)
+    local = pltpu.make_async_copy(x_hbm.at[me], o_hbm.at[me], local_sem)
+    local.start()
+    copies = []
+    for k in range(1, n):
+        dest = lax.rem(me + k, n)
+        copy = pltpu.make_async_remote_copy(
+            src_ref=x_hbm.at[dest],
+            dst_ref=o_hbm.at[me],
+            send_sem=send_sems.at[k],
+            recv_sem=recv_sems.at[k],
+            device_id=(grp, dest),
+            device_id_type=mesh_id,
+        )
+        copy.start()
+        copies.append(copy)
+    for copy in copies:
+        copy.wait()
+    local.wait()
+
+
+def exchange(x, collective_id):
+    n = x.shape[0]
+    return pl.pallas_call(
+        _exchange_kernel,
+        out_shape=jax.ShapeDtypeStruct(x.shape, x.dtype),
+        in_specs=[pl.BlockSpec(memory_space=pl.ANY)],
+        out_specs=pl.BlockSpec(memory_space=pl.ANY),
+        scratch_shapes=[
+            pltpu.SemaphoreType.DMA((n,)),
+            pltpu.SemaphoreType.DMA((n,)),
+            pltpu.SemaphoreType.DMA,
+        ],
+        compiler_params=pltpu.CompilerParams(collective_id=collective_id, has_side_effects=True),
+    )(x)
 
 
 def body(
@@ -43,7 +90,7 @@
     outgoing = jnp.einsum(
         "ecr,rd->ecd", pick, normed, preferred_element_type=jnp.float32
     ).astype(jnp.bfloat16)
-    joined = lax.all_to_all(outgoing, "exp", split_axis=0, concat_axis=0, tiled=True)
+    joined = exchange(outgoing, 0)
     gate_part = jnp.einsum("scd,df->scf", joined, expert_gate[0], preferred_element_type=jnp.float32)
     up_part = jnp.einsum("scd,df->scf", joined, expert_up[0], preferred_element_type=jnp.float32)
     hidden = (jax.nn.silu(gate_part) * up_part).astype(jnp.bfloat16)
@@ -51,7 +98,7 @@
     result = jnp.einsum(
         "scf,fd->scd", hidden, expert_down[0], preferred_element_type=jnp.float32
     ).astype(jnp.bfloat16)
-    returned = lax.all_to_all(result, "exp", split_axis=0, concat_axis=0, tiled=True)
+    returned = exchange(result, 1)
     slot_weight = jnp.zeros((experts * capacity,), jnp.float32).at[slot].set(gate_weights.reshape(-1))
     combine = jnp.where(
         table.reshape(experts, capacity)[None, :, :] == rows[:, None, None],

time: 271 us -> 409 us (1.51)
  the two profiles are of different devices: /device:TPU:1 before, /device:TPU:29 now
where the time goes in v5:
time: 409 us
  Pallas kernels  237 us (58%)
  waiting for transfers between devices  88.7 us (22%)
  matrix products  58.8 us (14%)
  between operations  13.4 us (3%)
  local copies, waits for them, and re-layouts  8.15 us (2%)
    pallas_call x2, Pallas kernels, exchange(): pl.pallas_call(_exchange_kernel, out_shape=jax.ShapeDtypeStruct(x.shape,...  237 us
    all_gather x1, waiting for transfers between devices, body(): lax.all_gather(out_weight, 'exp', axis=0, tiled=True)  55.8 us
    all_gather x1, waiting for transfers between devices, body(): group_rows = lax.all_gather(normed, 'req', axis=0, tiled=True)  32.2 us
    dot_general x1, matrix products, body(): jnp.einsum('scd,df->scf', joined, expert_up[0], preferred_element_type=jn...  12.3 us
    dot_general x1, matrix products, body(): jnp.einsum('scd,df->scf', joined, expert_gate[0], preferred_element_type=...  12.1 us
    dot_general x1, matrix products, body(): jnp.einsum('scf,fd->scd', hidden, expert_down[0], preferred_element_type=...  10.2 us
  transfers between devices with their start and end apart: 3, of which 2 were waited for; matrix products, arithmetic and copies ran while one was open for 12% of the time, Pallas kernels for 58%

profile of v5, /device:TPU:29, one launch (start us, length us, event | category | flops | bytes accessed | tf_op | source)
XLA Modules:
  0.0 408.8 jit_solution(14644722011334882081)
XLA Ops:
  6.5 0.7 all-gather.3.cloned.1.call-update
  7.3 0.0 all-gather.5.cloned.1.call-start
  7.3 55.8 %all-gather.3.cloned.1.call-done = bf16[2048,2048]{1,0:T(8,128)(2,1)} async-done(((bf16[64,2048]{1,0:T(8,128)(2,1)}), bf16[2048,2048]{1,0:T(8,128)(2,1)}) %all-gather.3.cloned.1.call-update) | async-done | bytes 8388624 | tf_op jit(solution)/shard_map/all_gather | solution.py:74
  63.1 5.0 %multiply_reduce_fusion = (f32[128]{0:T(128)S(1)}, f32[128,2048]{1,0:T(8,128)S(1)}) fusion(bf16[128,2048]{1,0:T(8,128)(2,1)} %param.12, bf16[2048,2048]{1,0:T(8,128)(2,1)} %all-gather.3.cloned.1.call-done, bf16[128,2048]{1,0:T(8,128)(2,1)} %param.13), kind=kOutput, calls=%fused_computation.21 | convolution fusion | flops 1075314560 | bytes 10486272 | tf_op jit(solution)/shard_map/dot_general | solution.py:72
  68.1 0.9 multiply_convert_fusion.1
  69.0 0.0 all-gather.5.cloned.1.call-update
  69.1 0.0 reduce-scatter.2.cloned.1.call-start
  69.1 32.2 %all-gather.5.cloned.1.call-done = bf16[512,2048]{1,0:T(8,128)(2,1)} async-done(((bf16[128,2048]{1,0:T(8,128)(2,1)}), bf16[512,2048]{1,0:T(8,128)(2,1)}) %all-gather.5.cloned.1.call-update) | async-done | bytes 2097168 | tf_op jit(solution)/shard_map/all_gather | solution.py:116
  101.3 2.9 fusion.40
  104.3 6.3 %fusion.14 = f32[512,2048]{1,0:T(8,128)} fusion(bf16[2048,352]{0,1:T(8,128)(2,1)S(1)} %copy-done, bf16[512,2048]{1,0:T(8,128)(2,1)} %all-gather.5.cloned.1.call-done, bf16[2048,352]{0,1:T(8,128)(2,1)} %param.22, f32[512,352]{0,1:T(8,128)S(1)} %fusion.40), kind=kOutput, calls=%fused_computation.19 | convolution fusion | flops 1477476352 | bytes 9895936 | tf_op jit(solution)/shard_map/dot_general | solution.py:120
  110.6 0.1 copy.14
  110.7 0.1 eq.57
  110.9 0.1 eq.53
  111.0 1.7 reduce-window.6
  112.8 0.3 slice_reduce_fusion
  113.1 0.1 copy.13
  113.2 0.1 mul.54
  113.3 0.1 fusion.28
  113.5 3.4 scatter_custom_fusion
  116.9 0.1 eq.61
  117.0 0.1 copy.17
  117.1 0.1 reshape.80
  117.2 3.4 scatter_custom_fusion.1
  120.6 0.1 broadcast_in_dim.29
  120.8 3.9 convolution_convert_fusion.x_hbm
  124.6 120.4 %shard_map.118 = bf16[32,36,2048]{2,1,0:T(8,128)(2,1)} custom-call(bf16[32,36,2048]{2,1,0:T(8,128)(2,1)} %convolution_convert_fusion.x_hbm), custom_call_target="tpu_custom_call" | custom-call | tf_op jit(solution)/shard_map/pallas_call | solution.py:40
  245.1 12.3 %fusion.2 = f32[32,36,1408]{2,1,0:T(8,128)S(1)} fusion(bf16[32,36,2048]{2,1,0:T(8,128)(2,1)} %shard_map.118, bf16[1,2048,1408]{2,1,0:T(8,128)(2,1)} %param.19), kind=kOutput, calls=%fused_computation.5 | convolution fusion | flops 6643777536 | bytes 16973824 | tf_op jit(solution)/shard_map/scd,df->scf/dot_general | solution.py:95
  257.4 12.1 %multiply_convert_fusion = bf16[32,36,1408]{2,1,0:T(8,128)(2,1)S(1)} fusion(f32[32,36,1408]{2,1,0:T(8,128)S(1)} %fusion.2, bf16[32,36,2048]{2,1,0:T(8,128)(2,1)S(1)} %copy-done.2, bf16[1,2048,1408]{2,1,0:T(8,128)(2,1)} %param.18), kind=kOutput, calls=%fused_computation.2 | convolution fusion | flops 6653509632 | bytes 20217856 | tf_op jit(solution)/shard_map/scd,df->scf/dot_general | solution.py:94
  269.5 10.2 %fusion.5.x_hbm = bf16[32,36,2048]{2,1,0:T(8,128)(2,1)} fusion(bf16[32,36,1408]{2,1,0:T(8,128)(2,1)S(1)} %multiply_convert_fusion, bf16[1,1408,2048]{2,1,0:T(8,128)(2,1)S(1)} %bitcast.54), kind=kOutput, calls=%fused_computation.9 | convolution fusion | flops 6646136832 | bytes 13729792 | tf_op jit(solution)/shard_map/scf,fd->scd/dot_general | solution.py:98
  279.7 116.4 %shard_map.119 = bf16[32,36,2048]{2,1,0:T(8,128)(2,1)} custom-call(bf16[32,36,2048]{2,1,0:T(8,128)(2,1)} %fusion.5.x_hbm), custom_call_target="tpu_custom_call" | custom-call | tf_op jit(solution)/shard_map/pallas_call | solution.py:40
  396.1 0.0 reduce-scatter.2.cloned.1.call-done
  396.1 6.2 %fusion.10 = bf16[128,2048]{1,0:T(8,128)(2,1)} fusion(f32[128,2048]{1,0:T(8,128)} %reduce-scatter.2.cloned.1.call-done, f32[128,2048]{1,0:T(8,128)S(1)} %get-tuple-element.6, bf16[32,36,2048]{2,1,0:T(8,128)(2,1)} %shard_map.119, f32[32,36]{1,0:T(8,128)S(1)} %broadcast_in_dim.29, s32[32,36]{1,0:T(8,128)S(1)} %eq.61), kind=kOutput, calls=%fused_computation.14 | convolution fusion | flops 3624960000 | bytes 7349248 | tf_op jit(solution)/shard_map/rec,ecd->rd/dot_general | solution.py:108
  (28 shorter events, 0.1 us)
Async XLA Ops:
  6.5 97.7 %copy-start = (bf16[2048,352]{0,1:T(8,128)(2,1)S(1)}, bf16[2048,352]{0,1:T(8,128)(2,1)}, u32[]{:S(2)}) copy-start(bf16[2048,352]{0,1:T(8,128)(2,1)} %param.23) | copy-start | bytes 4325380
  6.5 56.5 %all-gather.3.cloned.1.call-start = ((), (), s32[]{:S(2)}) async-start(), calls=%async_computation.1 | async-start | bytes 8650752 | tf_op jit(solution)/shard_map/all_gather | solution.py:74
  7.3 60.8 %copy-start.5 = (f32[2048]{0:T(1024)S(1)}, f32[2048]{0:T(1024)}, u32[]{:S(2)}) copy-start(f32[2048]{0:T(1024)} %param.15) | copy-start | bytes 24580
  7.3 94.0 %all-gather.5.cloned.1.call-start = ((), (), s32[]{:S(2)}) async-start(), calls=%async_computation.2 | async-start | bytes 2621440 | tf_op jit(solution)/shard_map/all_gather | solution.py:116
  69.1 327.1 %reduce-scatter.2.cloned.1.call-start = ((), (), s32[]{:S(2)}) async-start(), calls=%async_computation.3 | async-start | bytes 5242880 | tf_op jit(solution)/shard_map/reduce_scatter | solution.py:123
  104.2 6.4 %copy-start.4 = (s32[128,6]{0,1:T(8,128)S(1)}, s32[128,6]{0,1:T(8,128)}, u32[]{:S(2)}) copy-start(s32[128,6]{0,1:T(8,128)} %param.16) | copy-start | bytes 9220
  104.3 12.7 %copy-start.6 = (f32[128,6]{0,1:T(8,128)S(1)}, f32[128,6]{0,1:T(8,128)}, u32[]{:S(2)}) copy-start(f32[128,6]{0,1:T(8,128)} %param.17) | copy-start | bytes 9220
  110.6 10.2 %copy-start.3 = (bf16[128,2048]{1,0:T(8,128)(2,1)S(1)}, bf16[128,2048]{1,0:T(8,128)(2,1)}, u32[]{:S(2)}) copy-start(bf16[128,2048]{1,0:T(8,128)(2,1)} %multiply_convert_fusion.1) | copy-start | bytes 1572868
  245.1 12.3 %copy-start.2 = (bf16[32,36,2048]{2,1,0:T(8,128)(2,1)S(1)}, bf16[32,36,2048]{2,1,0:T(8,128)(2,1)}, u32[]{:S(2)}) copy-start(bf16[32,36,2048]{2,1,0:T(8,128)(2,1)} %shard_map.118) | copy-start | bytes 14155780
  245.1 24.4 %slice-start = ((s8[5767168]{0:T(1024)(128)(4,1)}), s8[4194304]{0:T(1024)(128)(4,1)S(1)}, s32[]{:S(2)}) async-start(s8[5767168]{0:T(1024)(128)(4,1)} %bitcast.53), calls=%async_computation.4 | async-start | bytes 8388608
  257.4 12.1 %slice-start.1 = ((s8[5767168]{0:T(1024)(128)(4,1)}), s8[1572864]{0:T(1024)(128)(4,1)S(1)}, s32[]{:S(2)}) async-start(s8[5767168]{0:T(1024)(128)(4,1)} %bitcast.53), calls=%async_computation.5 | async-start | bytes 3145728
  279.7 122.6 %copy-start.1 = (bf16[2048,352]{0,1:T(8,128)(2,1)S(1)}, bf16[2048,352]{0,1:T(8,128)(2,1)}, u32[]{:S(2)}) copy-start(bf16[2048,352]{0,1:T(8,128)(2,1)} %param.23) | copy-start | bytes 4325380
Sparse Core Ops, SparseCore 0:
  9.6 53.4 all-gather.2
  69.2 32.0 all-gather.4
  110.7 46.9 reduce-scatter.1

commit v6 on v4

--- a/solution.py
+++ b/solution.py
@@ -40,31 +40,19 @@
     table = jnp.full((experts * capacity,), row_count, jnp.int32).at[slot].set(source_row)
     rows = jnp.arange(row_count, dtype=jnp.int32)
     pick = (table.reshape(experts, capacity)[:, :, None] == rows[None, None, :]).astype(jnp.bfloat16)
-    half = width // 2
-    joined = []
-    for part in range(2):
-        cols = normed[:, part * half:(part + 1) * half]
+    w_gate, w_up, w_down = expert_gate[0], expert_up[0], expert_down[0]
+    bounds = [0, min(16, capacity), capacity] if capacity > 16 else [0, capacity]
+    returned = []
+    for lo, hi in zip(bounds[:-1], bounds[1:]):
         outgoing = jnp.einsum(
-            "ecr,rd->ecd", pick, cols, preferred_element_type=jnp.float32
+            "ecr,rd->ecd", pick[:, lo:hi], normed, preferred_element_type=jnp.float32
         ).astype(jnp.bfloat16)
-        joined.append(lax.all_to_all(outgoing, "exp", split_axis=0, concat_axis=0, tiled=True))
-    w_gate, w_up, w_down = expert_gate[0], expert_up[0], expert_down[0]
-    gate_part = sum(
-        jnp.einsum("scd,df->scf", joined[p], w_gate[p * half:(p + 1) * half],
-                   preferred_element_type=jnp.float32)
-        for p in range(2)
-    )
-    up_part = sum(
-        jnp.einsum("scd,df->scf", joined[p], w_up[p * half:(p + 1) * half],
-                   preferred_element_type=jnp.float32)
-        for p in range(2)
-    )
-    hidden = (jax.nn.silu(gate_part) * up_part).astype(jnp.bfloat16)
-    returned = []
-    for part in range(2):
+        joined = lax.all_to_all(outgoing, "exp", split_axis=0, concat_axis=0, tiled=True)
+        gate_part = jnp.einsum("scd,df->scf", joined, w_gate, preferred_element_type=jnp.float32)
+        up_part = jnp.einsum("scd,df->scf", joined, w_up, preferred_element_type=jnp.float32)
+        hidden = (jax.nn.silu(gate_part) * up_part).astype(jnp.bfloat16)
         result = jnp.einsum(
-            "scf,fd->scd", hidden, w_down[:, part * half:(part + 1) * half],
-            preferred_element_type=jnp.float32,
+            "scf,fd->scd", hidden, w_down, preferred_element_type=jnp.float32
         ).astype(jnp.bfloat16)
         returned.append(lax.all_to_all(result, "exp", split_axis=0, concat_axis=0, tiled=True))
     slot_weight = jnp.zeros((experts * capacity,), jnp.float32).at[slot].set(gate_weights.reshape(-1))
@@ -73,16 +61,16 @@
         slot_weight.reshape(experts, capacity)[None, :, :],
         0.0,
     )
-    routed = jnp.concatenate([
+    routed = sum(
         jnp.einsum(
             "rec,ecd->rd",
-            combine,
-            returned[p].astype(jnp.float32),
+            combine[:, :, lo:hi],
+            part.astype(jnp.float32),
             precision=lax.Precision.HIGHEST,
             preferred_element_type=jnp.float32,
         )
-        for p in range(2)
-    ], axis=1)
+        for lo, hi, part in zip(bounds[:-1], bounds[1:], returned)
+    )
 
     group_rows = lax.all_gather(normed, "req", axis=0, tiled=True)
     s_gate = jnp.dot(group_rows, shared_gate, preferred_element_type=jnp.float32)

time: 276 us -> 252 us (0.913)
  matrix products: 86 us -> 67.5 us
  waiting for transfers between devices: 138 us -> 128 us
  local copies, waits for them, and re-layouts: 11 us -> 18.6 us
    dot_general x10, matrix products: 70.9 us -> 52.4 us  [the longest x2 15.4 us: body(): jnp.einsum('scd,df->scf', joined, w_up, preferred_element_type=jnp.float32)]
    all_to_all x2, waiting for transfers between devices: 51.7 us -> 34.6 us  [body(): lax.all_to_all(result, 'exp', split_axis=0, concat_axis=0, tiled=True)]
    all_gather x1, waiting for transfers between devices: 0.01 us -> 11 us  [body(): group_rows = lax.all_gather(normed, 'req', axis=0, tiled=True)]
    all_to_all x2, waiting for transfers between devices: 34 us -> 23 us  [body(): lax.all_to_all(outgoing, 'exp', split_axis=0, concat_axis=0, tiled=True)]
    convert_element_type x0 -> x3, local copies, waits for them, and re-layouts: none -> 8.8 us  [the longest x2 5.65 us: body(): result = jnp.einsum('scf,fd->scd', hidden, w_down, preferred_element_type...]
    all_gather x1, waiting for transfers between devices: 51.1 us -> 58.7 us  [body(): lax.all_gather(out_weight, 'exp', axis=0, tiled=True)]
  transfers between devices with their start and end apart: 7 -> 7, of which waited for: 5 -> 6; matrix products, arithmetic and copies ran while one was open for 33% -> 31% of each run, Pallas kernels for 0% -> 0%
where the time goes in v6:
time: 252 us
  waiting for transfers between devices  128 us (51%)
  matrix products  67.5 us (27%)
  starting transfers between devices  21.1 us (8%)
  local copies, waits for them, and re-layouts  18.6 us (7%)
  between operations  13.4 us (5%)
  other arithmetic  3.11 us (1%)
    all_gather x1, waiting for transfers between devices, body(): lax.all_gather(out_weight, 'exp', axis=0, tiled=True)  58.7 us
    all_to_all x2, waiting for transfers between devices, body(): lax.all_to_all(result, 'exp', split_axis=0, concat_axis=0, tiled=True)  34.6 us
    all_to_all x2, waiting for transfers between devices, body(): lax.all_to_all(outgoing, 'exp', split_axis=0, concat_axis=0, tiled=True)  23 us
    dot_general x2, matrix products, body(): jnp.einsum('scd,df->scf', joined, w_up, preferred_element_type=jnp.float32)  15.4 us
    dot_general x2, matrix products, body(): jnp.einsum('scd,df->scf', joined, w_gate, preferred_element_type=jnp.floa...  15.3 us
    all_gather x1, waiting for transfers between devices, body(): group_rows = lax.all_gather(normed, 'req', axis=0, tiled=True)  11 us
    all_to_all x2, starting transfers between devices, body(): lax.all_to_all(outgoing, 'exp', split_axis=0, concat_axis=0, tiled=True)  10.8 us
    all_to_all x2, starting transfers between devices, body(): lax.all_to_all(result, 'exp', split_axis=0, concat_axis=0, tiled=True)  10.2 us
  transfers between devices with their start and end apart: 7, of which 6 were waited for; matrix products, arithmetic and copies ran while one was open for 31% of the time, Pallas kernels for 0%

profile of v6, /device:TPU:1, one launch (start us, length us, event | category | flops | bytes accessed | tf_op | source)
XLA Modules:
  0.0 251.8 jit_solution(16423598688308512334)
XLA Ops:
  6.5 0.7 all-gather.3.cloned.1.call-update
  7.3 58.7 %all-gather.3.cloned.1.call-done = bf16[2048,2048]{1,0:T(8,128)(2,1)} async-done(((bf16[64,2048]{1,0:T(8,128)(2,1)}), bf16[2048,2048]{1,0:T(8,128)(2,1)}) %all-gather.3.cloned.1.call-update) | async-done | bytes 8388624 | tf_op jit(solution)/shard_map/all_gather | solution.py:27
  66.1 5.0 %multiply_reduce_fusion = (f32[128]{0:T(128)S(1)}, f32[128,2048]{1,0:T(8,128)S(1)}) fusion(bf16[128,2048]{1,0:T(8,128)(2,1)} %param.12, bf16[2048,2048]{1,0:T(8,128)(2,1)} %all-gather.3.cloned.1.call-done, bf16[128,2048]{1,0:T(8,128)(2,1)} %param.13), kind=kOutput, calls=%fused_computation.41 | convolution fusion | flops 1075314560 | bytes 10486272 | tf_op jit(solution)/shard_map/dot_general | solution.py:25
  71.0 0.9 multiply_convert_fusion
  72.7 1.7 reduce-window.6
  74.9 3.4 %scatter_custom_fusion = s32[1152]{0:T(1024)S(1)} fusion(s32[768]{0:T(1024)S(1)} %fusion.83, s32[768]{0:T(1024)S(1)} %add_select_fusion, s32[]{:T(128)} %constant.13.clone.1), kind=kCustom, calls=%fused_computation.79 | custom fusion | bytes 4612 | tf_op jit(solution)/shard_map/scatter | solution.py:40
  78.6 3.2 %convolution_convert_fusion.1 = bf16[32,16,2048]{2,1,0:T(8,128)(2,1)} fusion(bf16[128,2048]{1,0:T(8,128)(2,1)} %multiply_convert_fusion, pred[32,36,128]{2,1,0:T(8,128)(4,1)S(1)} %iota_compare_fusion), kind=kOutput, calls=%fused_computation.20 | convolution fusion | flops 269484032 | bytes 2686976 | tf_op jit(solution)/shard_map/ecr,rd->ecd/dot_general | solution.py:47
  81.8 5.5 %all-to-all-start = ((bf16[32,16,2048]{2,1,0:T(8,128)(2,1)}), bf16[32,16,2048]{2,1,0:T(8,128)(2,1)}, u32[]{:S(2)}, u32[]{:S(2)}) async-start(bf16[32,16,2048]{2,1,0:T(8,128)(2,1)} %convolution_convert_fusion.1), calls=%async_computation | async-start | bytes 4194304 | tf_op jit(solution)/shard_map/all_to_all | solution.py:50
  87.5 0.8 convolution_convert_fusion
  88.3 3.1 %copy.34 = bf16[32,20,2048]{2,1,0:T(8,128)(2,1)} copy(bf16[32,20,2048]{2,0,1:T(8,128)(2,1)S(1)} %convolution_convert_fusion) | data formatting | bytes 5242880 | tf_op jit(solution)/shard_map/convert_element_type | solution.py:49
  91.4 11.0 %all-gather.5.cloned.1.call-done = bf16[512,2048]{1,0:T(8,128)(2,1)} async-done(((bf16[128,2048]{1,0:T(8,128)(2,1)}), bf16[512,2048]{1,0:T(8,128)(2,1)}) %all-gather.5.cloned.1.call-update) | async-done | bytes 2097168 | tf_op jit(solution)/shard_map/all_gather | solution.py:75
  102.4 3.8 %fusion.87 = f32[512,352]{0,1:T(8,128)} fusion(bf16[512,2048]{1,0:T(8,128)(2,1)} %all-gather.5.cloned.1.call-done, bf16[2048,352]{0,1:T(8,128)(2,1)} %param.21), kind=kOutput, calls=%fused_computation.89 | convolution fusion | flops 738197504 | bytes 4259840 | tf_op jit(solution)/shard_map/dot_general | solution.py:76
  106.2 6.3 %fusion.54 = f32[512,2048]{1,0:T(8,128)} fusion(bf16[2048,352]{0,1:T(8,128)(2,1)S(1)} %copy-done, bf16[512,2048]{1,0:T(8,128)(2,1)} %all-gather.5.cloned.1.call-done, bf16[2048,352]{0,1:T(8,128)(2,1)} %param.22, f32[512,352]{0,1:T(8,128)} %fusion.87), kind=kOutput, calls=%fused_computation.39 | convolution fusion | flops 1477476352 | bytes 9895936 | tf_op jit(solution)/shard_map/dot_general | solution.py:79
  112.6 3.1 %all-to-all-done = bf16[32,16,2048]{2,1,0:T(8,128)(2,1)} async-done(((bf16[32,16,2048]{2,1,0:T(8,128)(2,1)}), bf16[32,16,2048]{2,1,0:T(8,128)(2,1)}, u32[]{:S(2)}, u32[]{:S(2)}) %all-to-all-start) | async-done | bytes 2097184 | tf_op jit(solution)/shard_map/all_to_all | solution.py:50
  115.7 5.3 %all-to-all-start.2 = ((bf16[32,20,2048]{2,1,0:T(8,128)(2,1)}), bf16[32,20,2048]{2,1,0:T(8,128)(2,1)}, u32[]{:S(2)}, u32[]{:S(2)}) async-start(bf16[32,20,2048]{2,1,0:T(8,128)(2,1)} %copy.34), calls=%async_computation.2 | async-start | bytes 6291456 | tf_op jit(solution)/shard_map/all_to_all | solution.py:50
  121.0 7.0 %fusion.10 = f32[32,16,1408]{2,1,0:T(8,128)S(1)} fusion(bf16[32,16,2048]{2,1,0:T(8,128)(2,1)} %all-to-all-done, bf16[1,2048,1408]{2,1,0:T(8,128)(2,1)} %param.18), kind=kOutput, calls=%fused_computation.12 | convolution fusion | flops 2952790016 | bytes 10747904 | tf_op jit(solution)/shard_map/scd,df->scf/dot_general | solution.py:51
  128.1 6.9 %fusion.24 = bf16[32,16,1408]{2,1,0:T(8,128)(2,1)S(1)} fusion(bf16[32,16,2048]{2,1,0:T(8,128)(2,1)} %all-to-all-done, bf16[1,2048,1408]{2,1,0:T(8,128)(2,1)} %param.19, f32[32,16,1408]{2,1,0:T(8,128)S(1)} %fusion.10), kind=kOutput, calls=%fused_computation.19 | convolution fusion | flops 2957115392 | bytes 12189696 | tf_op jit(solution)/shard_map/scd,df->scf/dot_general | solution.py:52
  135.0 3.6 %fusion.27 = bf16[32,16,2048]{2,0,1:T(8,128)(2,1)S(1)} fusion(bf16[1,1408,2048]{2,1,0:T(8,128)(2,1)S(1)} %bitcast.77, bf16[32,16,1408]{2,1,0:T(8,128)(2,1)S(1)} %fusion.24), kind=kOutput, calls=%fused_computation.21 | convolution fusion | flops 2953838592 | bytes 9306112 | tf_op jit(solution)/shard_map/scf,fd->scd/dot_general | solution.py:54
  138.6 2.5 copy.31
  141.1 19.8 %all-to-all-done.2 = bf16[32,20,2048]{2,1,0:T(8,128)(2,1)} async-done(((bf16[32,20,2048]{2,1,0:T(8,128)(2,1)}), bf16[32,20,2048]{2,1,0:T(8,128)(2,1)}, u32[]{:S(2)}, u32[]{:S(2)}) %all-to-all-start.2) | async-done | bytes 2621472 | tf_op jit(solution)/shard_map/all_to_all | solution.py:50
  160.9 5.0 %all-to-all-start.1 = ((bf16[32,16,2048]{2,1,0:T(8,128)(2,1)}), bf16[32,16,2048]{2,1,0:T(8,128)(2,1)}, u32[]{:S(2)}, u32[]{:S(2)}) async-start(bf16[32,16,2048]{2,1,0:T(8,128)(2,1)} %copy.31), calls=%async_computation.1 | async-start | bytes 4194304 | tf_op jit(solution)/shard_map/all_to_all | solution.py:57
  165.9 8.3 %fusion.8 = f32[32,20,1408]{2,0,1:T(8,128)S(1)} fusion(bf16[1,2048,1408]{2,1,0:T(8,128)(2,1)} %param.18, bf16[32,20,2048]{2,1,0:T(8,128)(2,1)} %all-to-all-done.2), kind=kOutput, calls=%fused_computation.10 | convolution fusion | flops 3690987520 | bytes 11993088 | tf_op jit(solution)/shard_map/scd,df->scf/dot_general | solution.py:51
  174.2 8.5 %fusion.18 = bf16[32,20,1408]{2,0,1:T(8,128)(2,1)S(1)} fusion(bf16[1,2048,1408]{2,1,0:T(8,128)(2,1)} %param.19, f32[32,20,1408]{2,0,1:T(8,128)S(1)} %fusion.8, bf16[32,20,2048]{2,1,0:T(8,128)(2,1)} %all-to-all-done.2), kind=kOutput, calls=%fused_computation.16 | convolution fusion | flops 3696394240 | bytes 13795328 | tf_op jit(solution)/shard_map/scd,df->scf/dot_general | solution.py:52
  182.7 4.4 %fusion.21 = bf16[32,20,2048]{2,0,1:T(8,128)(2,1)S(1)} fusion(bf16[32,20,1408]{2,0,1:T(8,128)(2,1)S(1)} %fusion.18, bf16[1,1408,2048]{2,1,0:T(8,128)(2,1)S(1)} %bitcast.79), kind=kOutput, calls=%fused_computation.17 | convolution fusion | flops 3692298240 | bytes 10190848 | tf_op jit(solution)/shard_map/scf,fd->scd/dot_general | solution.py:54
  187.2 3.2 %copy.37 = bf16[32,20,2048]{2,1,0:T(8,128)(2,1)} copy(bf16[32,20,2048]{2,0,1:T(8,128)(2,1)S(1)} %fusion.21) | data formatting | bytes 5242880 | tf_op jit(solution)/shard_map/convert_element_type | solution.py:56
  190.3 3.9 %all-to-all-done.1 = bf16[32,16,2048]{2,1,0:T(8,128)(2,1)} async-done(((bf16[32,16,2048]{2,1,0:T(8,128)(2,1)}), bf16[32,16,2048]{2,1,0:T(8,128)(2,1)}, u32[]{:S(2)}, u32[]{:S(2)}) %all-to-all-start.1) | async-done | bytes 2097184 | tf_op jit(solution)/shard_map/all_to_all | solution.py:57
  194.2 5.3 %all-to-all-start.3 = ((bf16[32,20,2048]{2,1,0:T(8,128)(2,1)}), bf16[32,20,2048]{2,1,0:T(8,128)(2,1)}, u32[]{:S(2)}, u32[]{:S(2)}) async-start(bf16[32,20,2048]{2,1,0:T(8,128)(2,1)} %copy.37), calls=%async_computation.3 | async-start | bytes 6291456 | tf_op jit(solution)/shard_map/all_to_all | solution.py:57
  199.5 0.7 copy.27
  200.5 3.6 %scatter_custom_fusion.1 = f32[1152]{0:T(1024)S(1)} fusion(s32[768]{0:T(1024)S(1)} %fusion.83, f32[768]{0:T(1024)S(1)} %reshape.80, f32[]{:T(128)} %constant.36.clone.1), kind=kCustom, calls=%fused_computation.77 | custom fusion | bytes 4612 | tf_op jit(solution)/shard_map/scatter | solution.py:58
  204.9 3.9 %convolution_bitcast_fusion = f32[128,2048]{1,0:T(8,128)S(1)} fusion(bf16[32,16,2048]{2,1,0:T(8,128)(2,1)} %all-to-all-done.1, f32[32,36]{0,1:T(8,128)} %copy.29, s32[32,36]{0,1:T(8,128)} %copy.27), kind=kOutput, calls=%fused_computation.25 | convolution fusion | flops 1610907648 | bytes 3154944 | tf_op jit(solution)/shard_map/rec,ecd->rd/dot_general | solution.py:65
  208.8 30.7 %all-to-all-done.3 = bf16[32,20,2048]{2,1,0:T(8,128)(2,1)} async-done(((bf16[32,20,2048]{2,1,0:T(8,128)(2,1)}), bf16[32,20,2048]{2,1,0:T(8,128)(2,1)}, u32[]{:S(2)}, u32[]{:S(2)}) %all-to-all-start.3) | async-done | bytes 2621472 | tf_op jit(solution)/shard_map/all_to_all | solution.py:57
  239.5 5.8 %fusion.46 = bf16[128,2048]{1,0:T(8,128)(2,1)} fusion(f32[128,2048]{1,0:T(8,128)} %reduce-scatter.2.cloned.1.call-done, f32[128,2048]{1,0:T(8,128)S(1)} %get-tuple-element.6, f32[128,2048]{1,0:T(8,128)S(1)} %convolution_bitcast_fusion, bf16[32,20,2048]{2,1,0:T(8,128)(2,1)} %all-to-all-done.3, f32[32,36]{0,1:T(8,128)} %copy.29, s32[32,36]{0,1:T(8,128)} %copy.27), kind=kOutput, calls=%fused_computation.32 | convolution fusion | flops 2014609408 | bytes 6300672 | tf_op jit(solution)/shard_map/rec,ecd->rd/dot_general | solution.py:65
  (49 shorter events, 2.6 us)
Async XLA Ops:
  6.5 99.7 %copy-start = (bf16[2048,352]{0,1:T(8,128)(2,1)S(1)}, bf16[2048,352]{0,1:T(8,128)(2,1)}, u32[]{:S(2)}) copy-start(bf16[2048,352]{0,1:T(8,128)(2,1)} %param.23) | copy-start | bytes 4325380
  6.5 59.5 %all-gather.3.cloned.1.call-start = ((), (), s32[]{:S(2)}) async-start(), calls=%async_computation.5 | async-start | bytes 8650752 | tf_op jit(solution)/shard_map/all_gather | solution.py:27
  7.3 63.8 %copy-start.4 = (f32[2048]{0:T(1024)S(1)}, f32[2048]{0:T(1024)}, u32[]{:S(2)}) copy-start(f32[2048]{0:T(1024)} %param.15) | copy-start | bytes 24580
  7.3 64.8 %copy-start.3 = (s32[128,6]{0,1:T(8,128)S(1)}, s32[128,6]{0,1:T(8,128)}, u32[]{:S(2)}) copy-start(s32[128,6]{0,1:T(8,128)} %param.16) | copy-start | bytes 9220
  7.3 95.2 %all-gather.5.cloned.1.call-start = ((), (), s32[]{:S(2)}) async-start(), calls=%async_computation.6 | async-start | bytes 2621440 | tf_op jit(solution)/shard_map/all_gather | solution.py:75
  78.6 8.8 %copy-start.2 = (bf16[128,2048]{1,0:T(8,128)(2,1)S(1)}, bf16[128,2048]{1,0:T(8,128)(2,1)}, u32[]{:S(2)}) copy-start(bf16[128,2048]{1,0:T(8,128)(2,1)} %multiply_convert_fusion) | copy-start | bytes 1572868
  81.8 33.9 %all-to-all-start = ((bf16[32,16,2048]{2,1,0:T(8,128)(2,1)}), bf16[32,16,2048]{2,1,0:T(8,128)(2,1)}, u32[]{:S(2)}, u32[]{:S(2)}) async-start(bf16[32,16,2048]{2,1,0:T(8,128)(2,1)} %convolution_convert_fusion.1), calls=%async_computation | async-start | bytes 4194304 | tf_op jit(solution)/shard_map/all_to_all | solution.py:50
  87.4 152.1 %reduce-scatter.2.cloned.1.call-start = ((), (), s32[]{:S(2)}) async-start(), calls=%async_computation.7 | async-start | bytes 5242880 | tf_op jit(solution)/shard_map/reduce_scatter | solution.py:82
  115.7 45.2 %all-to-all-start.2 = ((bf16[32,20,2048]{2,1,0:T(8,128)(2,1)}), bf16[32,20,2048]{2,1,0:T(8,128)(2,1)}, u32[]{:S(2)}, u32[]{:S(2)}) async-start(bf16[32,20,2048]{2,1,0:T(8,128)(2,1)} %copy.34), calls=%async_computation.2 | async-start | bytes 6291456 | tf_op jit(solution)/shard_map/all_to_all | solution.py:50
  121.0 14.0 %slice-start = ((s8[5767168]{0:T(1024)(128)(4,1)}), s8[4194304]{0:T(1024)(128)(4,1)S(1)}, s32[]{:S(2)}) async-start(s8[5767168]{0:T(1024)(128)(4,1)} %bitcast.76), calls=%async_computation.8 | async-start | bytes 8388608
  128.0 6.9 %slice-start.1 = ((s8[5767168]{0:T(1024)(128)(4,1)}), s8[1572864]{0:T(1024)(128)(4,1)S(1)}, s32[]{:S(2)}) async-start(s8[5767168]{0:T(1024)(128)(4,1)} %bitcast.76), calls=%async_computation.9 | async-start | bytes 3145728
  160.9 33.3 %all-to-all-start.1 = ((bf16[32,16,2048]{2,1,0:T(8,128)(2,1)}), bf16[32,16,2048]{2,1,0:T(8,128)(2,1)}, u32[]{:S(2)}, u32[]{:S(2)}) async-start(bf16[32,16,2048]{2,1,0:T(8,128)(2,1)} %copy.31), calls=%async_computation.1 | async-start | bytes 4194304 | tf_op jit(solution)/shard_map/all_to_all | solution.py:57
  165.9 16.8 %slice-start.2 = ((s8[5767168]{0:T(1024)(128)(4,1)}), s8[4194304]{0:T(1024)(128)(4,1)S(1)}, s32[]{:S(2)}) async-start(s8[5767168]{0:T(1024)(128)(4,1)} %bitcast.78), calls=%async_computation.10 | async-start | bytes 8388608
  174.2 8.5 %slice-start.3 = ((s8[5767168]{0:T(1024)(128)(4,1)}), s8[1572864]{0:T(1024)(128)(4,1)S(1)}, s32[]{:S(2)}) async-start(s8[5767168]{0:T(1024)(128)(4,1)} %bitcast.78), calls=%async_computation.11 | async-start | bytes 3145728
  190.3 9.9 %copy-start.5 = (f32[128,6]{0,1:T(8,128)S(1)}, f32[128,6]{0,1:T(8,128)}, u32[]{:S(2)}) copy-start(f32[128,6]{0,1:T(8,128)} %param.17) | copy-start | bytes 9220
  194.2 45.2 %all-to-all-start.3 = ((bf16[32,20,2048]{2,1,0:T(8,128)(2,1)}), bf16[32,20,2048]{2,1,0:T(8,128)(2,1)}, u32[]{:S(2)}, u32[]{:S(2)}) async-start(bf16[32,20,2048]{2,1,0:T(8,128)(2,1)} %copy.37), calls=%async_computation.3 | async-start | bytes 6291456 | tf_op jit(solution)/shard_map/all_to_all | solution.py:57
  204.9 40.4 %copy-start.1 = (bf16[2048,352]{0,1:T(8,128)(2,1)S(1)}, bf16[2048,352]{0,1:T(8,128)(2,1)}, u32[]{:S(2)}) copy-start(bf16[2048,352]{0,1:T(8,128)(2,1)} %param.23) | copy-start | bytes 4325380
Sparse Core Ops, SparseCore 0:
  9.6 56.3 all-gather.2
  72.1 30.2 all-gather.4
  112.7 46.9 reduce-scatter.1

commit v7 on v6

--- a/solution.py
+++ b/solution.py
@@ -22,6 +22,14 @@
     topk = expert_ids.shape[1]
     experts = lax.axis_size("exp")
     capacity = min(row_count, 3 * row_count * topk // (2 * experts))
+    flat_ids = expert_ids.reshape(-1)
+    onehot = (flat_ids[:, None] == jnp.arange(experts, dtype=jnp.int32)[None, :]).astype(jnp.int32)
+    position = jnp.sum(jnp.cumsum(onehot, axis=0) * onehot, axis=1) - 1
+    slot = flat_ids * capacity + position
+    source_row = jnp.arange(row_count * topk, dtype=jnp.int32) // topk
+    table = jnp.full((experts * capacity,), row_count, jnp.int32).at[slot].set(source_row)
+    rows = jnp.arange(row_count, dtype=jnp.int32)
+    table, attn_out = lax.optimization_barrier((table, attn_out))
     proj = jnp.dot(
         attn_out,
         lax.all_gather(out_weight, "exp", axis=0, tiled=True),
@@ -32,13 +40,6 @@
     scale = lax.rsqrt(jnp.mean(stream_f * stream_f, axis=1, keepdims=True) + 1e-06)
     normed = (stream_f * scale * norm_gain).astype(jnp.bfloat16)
 
-    flat_ids = expert_ids.reshape(-1)
-    onehot = (flat_ids[:, None] == jnp.arange(experts, dtype=jnp.int32)[None, :]).astype(jnp.int32)
-    position = jnp.sum(jnp.cumsum(onehot, axis=0) * onehot, axis=1) - 1
-    slot = flat_ids * capacity + position
-    source_row = jnp.arange(row_count * topk, dtype=jnp.int32) // topk
-    table = jnp.full((experts * capacity,), row_count, jnp.int32).at[slot].set(source_row)
-    rows = jnp.arange(row_count, dtype=jnp.int32)
     pick = (table.reshape(experts, capacity)[:, :, None] == rows[None, None, :]).astype(jnp.bfloat16)
     w_gate, w_up, w_down = expert_gate[0], expert_up[0], expert_down[0]
     bounds = [0, min(16, capacity), capacity] if capacity > 16 else [0, capacity]
@@ -61,15 +62,12 @@
         slot_weight.reshape(experts, capacity)[None, :, :],
         0.0,
     )
+    combine_hi = combine.astype(jnp.bfloat16)
+    combine_lo = (combine - combine_hi.astype(jnp.float32)).astype(jnp.bfloat16)
     routed = sum(
-        jnp.einsum(
-            "rec,ecd->rd",
-            combine[:, :, lo:hi],
-            part.astype(jnp.float32),
-            precision=lax.Precision.HIGHEST,
-            preferred_element_type=jnp.float32,
-        )
+        jnp.einsum("rec,ecd->rd", weights[:, :, lo:hi], part, preferred_element_type=jnp.float32)
         for lo, hi, part in zip(bounds[:-1], bounds[1:], returned)
+        for weights in (combine_hi, combine_lo)
     )
 
     group_rows = lax.all_gather(normed, "req", axis=0, tiled=True)

time: 252 us -> 256 us (1.016)
  matrix products: 67.5 us -> 79.3 us
  waiting for transfers between devices: 128 us -> 121 us
    dot_general x2, matrix products: 8.05 us -> 19 us  [body(): jnp.einsum('scf,fd->scd', hidden, w_down, preferred_element_type=jnp.floa...]
    all_to_all x2, waiting for transfers between devices: 23 us -> 14.6 us  [body(): lax.all_to_all(outgoing, 'exp', split_axis=0, concat_axis=0, tiled=True)]
    all_gather x1, waiting for transfers between devices: 58.7 us -> 51.1 us  [body(): lax.all_gather(out_weight, 'exp', axis=0, tiled=True)]
    dot_general x2 -> x4, matrix products: 9.67 us -> 16.9 us  [body(): jnp.einsum('rec,ecd->rd', weights[:, :, lo:hi], part, preferred_element_t...]
    dot_general x2 -> x1, matrix products: 15.4 us -> 8.57 us  [body(): jnp.einsum('scd,df->scf', joined, w_up, preferred_element_type=jnp.float32)]
    all_gather x1, waiting for transfers between devices: 11 us -> 17.3 us  [body(): group_rows = lax.all_gather(normed, 'req', axis=0, tiled=True)]
    convert_element_type x2 -> x1, local copies, waits for them, and re-layouts: 5.65 us -> 3.19 us  [body(): result = jnp.einsum('scf,fd->scd', hidden, w_down, preferred_element_type...]
  transfers between devices with their start and end apart: 7 -> 7, of which waited for: 6 -> 6; matrix products, arithmetic and copies ran while one was open for 31% -> 35% of each run, Pallas kernels for 0% -> 0%
where the time goes in v7:
time: 256 us; the launch traced here: 255 us
  waiting for transfers between devices  121 us (47%)
  matrix products  79.3 us (31%)
  starting transfers between devices  21.2 us (8%)
  local copies, waits for them, and re-layouts  16.7 us (7%)
  between operations  13.4 us (5%)
  other arithmetic  3.8 us (1%)
    all_gather x1, waiting for transfers between devices, body(): lax.all_gather(out_weight, 'exp', axis=0, tiled=True)  51.1 us
    all_to_all x2, waiting for transfers between devices, body(): lax.all_to_all(result, 'exp', split_axis=0, concat_axis=0, tiled=True)  36.9 us
    dot_general x2, matrix products, body(): jnp.einsum('scf,fd->scd', hidden, w_down, preferred_element_type=jnp.floa...  19 us
    all_gather x1, waiting for transfers between devices, body(): group_rows = lax.all_gather(normed, 'req', axis=0, tiled=True)  17.3 us
    dot_general x4, matrix products, body(): jnp.einsum('rec,ecd->rd', weights[:, :, lo:hi], part, preferred_element_t...  16.9 us
    dot_general x2, matrix products, body(): jnp.einsum('scd,df->scf', joined, w_gate, preferred_element_type=jnp.floa...  16.7 us
    all_to_all x2, waiting for transfers between devices, body(): lax.all_to_all(outgoing, 'exp', split_axis=0, concat_axis=0, tiled=True)  14.6 us
    all_to_all x2, starting transfers between devices, body(): lax.all_to_all(outgoing, 'exp', split_axis=0, concat_axis=0, tiled=True)  10.8 us
  transfers between devices with their start and end apart: 7, of which 6 were waited for; matrix products, arithmetic and copies ran while one was open for 35% of the time, Pallas kernels for 0%

profile of v7, /device:TPU:1, one launch (start us, length us, event | category | flops | bytes accessed | tf_op | source)
XLA Modules:
  0.0 255.1 jit_solution(2176299839863590023)
XLA Ops:
  7.3 0.8 copy.28
  9.3 1.7 reduce-window.6
  11.5 3.4 %scatter_custom_fusion = s32[1152]{0:T(1024)S(1)} fusion(s32[768]{0:T(1024)S(1)} %fusion.77, s32[768]{0:T(1024)S(1)} %add_select_fusion, s32[]{:T(128)} %constant.13.clone.1), kind=kCustom, calls=%fused_computation.84 | custom fusion | bytes 4612 | tf_op jit(solution)/shard_map/scatter | solution.py:30
  15.0 51.1 %all-gather.3.cloned.1.call-done = bf16[2048,2048]{1,0:T(8,128)(2,1)} async-done(((bf16[64,2048]{1,0:T(8,128)(2,1)}), bf16[2048,2048]{1,0:T(8,128)(2,1)}) %all-gather.3.cloned.1.call-update) | async-done | bytes 8388624 | tf_op jit(solution)/shard_map/all_gather | solution.py:35
  66.1 5.0 %multiply_reduce_fusion = (f32[128]{0:T(128)S(1)}, f32[128,2048]{1,0:T(8,128)S(1)}) fusion(bf16[128,2048]{1,0:T(8,128)(2,1)} %param.12, bf16[2048,2048]{1,0:T(8,128)(2,1)} %all-gather.3.cloned.1.call-done, bf16[128,2048]{1,0:T(8,128)(2,1)} %param.13), kind=kOutput, calls=%fused_computation.45 | convolution fusion | flops 1075314560 | bytes 10486272 | tf_op jit(solution)/shard_map/dot_general | solution.py:33
  71.1 1.0 copy-done.2
  72.0 0.9 multiply_convert_fusion
  73.4 3.2 %convolution_convert_fusion.1 = bf16[32,16,2048]{2,1,0:T(8,128)(2,1)} fusion(bf16[128,2048]{1,0:T(8,128)(2,1)} %multiply_convert_fusion, pred[32,36,128]{2,1,0:T(8,128)(4,1)S(1)} %iota_compare_fusion), kind=kOutput, calls=%fused_computation.20 | convolution fusion | flops 269484032 | bytes 2686976 | tf_op jit(solution)/shard_map/ecr,rd->ecd/dot_general | solution.py:48
  76.6 5.5 %all-to-all-start = ((bf16[32,16,2048]{2,1,0:T(8,128)(2,1)}), bf16[32,16,2048]{2,1,0:T(8,128)(2,1)}, u32[]{:S(2)}, u32[]{:S(2)}) async-start(bf16[32,16,2048]{2,1,0:T(8,128)(2,1)} %convolution_convert_fusion.1), calls=%async_computation | async-start | bytes 4194304 | tf_op jit(solution)/shard_map/all_to_all | solution.py:51
  82.1 0.8 convolution_convert_fusion
  83.0 3.1 %copy.37 = bf16[32,20,2048]{2,1,0:T(8,128)(2,1)} copy(bf16[32,20,2048]{2,0,1:T(8,128)(2,1)S(1)} %convolution_convert_fusion) | data formatting | bytes 5242880 | tf_op jit(solution)/shard_map/convert_element_type | solution.py:50
  86.1 17.3 %all-gather.5.cloned.1.call-done = bf16[512,2048]{1,0:T(8,128)(2,1)} async-done(((bf16[128,2048]{1,0:T(8,128)(2,1)}), bf16[512,2048]{1,0:T(8,128)(2,1)}) %all-gather.5.cloned.1.call-update) | async-done | bytes 2097168 | tf_op jit(solution)/shard_map/all_gather | solution.py:73
  103.4 3.4 %fusion.84 = f32[512,352]{0,1:T(8,128)} fusion(bf16[512,2048]{1,0:T(8,128)(2,1)} %all-gather.5.cloned.1.call-done, bf16[2048,352]{0,1:T(8,128)(2,1)S(1)} %copy-done.10), kind=kOutput, calls=%fused_computation.97 | convolution fusion | flops 738197504 | bytes 4259840 | tf_op jit(solution)/shard_map/dot_general | solution.py:74
  106.9 3.6 %all-to-all-done = bf16[32,16,2048]{2,1,0:T(8,128)(2,1)} async-done(((bf16[32,16,2048]{2,1,0:T(8,128)(2,1)}), bf16[32,16,2048]{2,1,0:T(8,128)(2,1)}, u32[]{:S(2)}, u32[]{:S(2)}) %all-to-all-start) | async-done | bytes 2097184 | tf_op jit(solution)/shard_map/all_to_all | solution.py:51
  110.4 5.3 %all-to-all-start.2 = ((bf16[32,20,2048]{2,1,0:T(8,128)(2,1)}), bf16[32,20,2048]{2,1,0:T(8,128)(2,1)}, u32[]{:S(2)}, u32[]{:S(2)}) async-start(bf16[32,20,2048]{2,1,0:T(8,128)(2,1)} %copy.37), calls=%async_computation.2 | async-start | bytes 6291456 | tf_op jit(solution)/shard_map/all_to_all | solution.py:51
  116.0 5.7 %fusion.45 = f32[512,2048]{1,0:T(8,128)} fusion(bf16[2048,352]{0,1:T(8,128)(2,1)S(1)} %copy-done, bf16[512,2048]{1,0:T(8,128)(2,1)S(1)} %copy-done.9, bf16[2048,352]{0,1:T(8,128)(2,1)} %param.22, f32[512,352]{0,1:T(8,128)} %fusion.84), kind=kOutput, calls=%fused_computation.43 | convolution fusion | flops 1477476352 | bytes 9895936 | tf_op jit(solution)/shard_map/dot_general | solution.py:77
  121.7 8.4 %fusion.10 = f32[32,16,1408]{2,1,0:T(8,128)} fusion(bf16[32,16,2048]{2,1,0:T(8,128)(2,1)} %all-to-all-done, bf16[1,2048,1408]{2,1,0:T(8,128)(2,1)} %param.18), kind=kOutput, calls=%fused_computation.12 | convolution fusion | flops 2952790016 | bytes 10747904 | tf_op jit(solution)/shard_map/scd,df->scf/dot_general | solution.py:52
  130.0 14.6 %fusion.27 = bf16[32,16,2048]{2,1,0:T(8,128)(2,1)} fusion(bf16[1,1408,2048]{2,1,0:T(8,128)(2,1)} %param.20, bf16[32,16,2048]{2,1,0:T(8,128)(2,1)} %all-to-all-done, bf16[1,2048,1408]{2,1,0:T(8,128)(2,1)} %param.19, f32[32,16,1408]{2,1,0:T(8,128)} %fusion.10), kind=kOutput, calls=%fused_computation.21 | convolution fusion | flops 5910953984 | bytes 18612224 | tf_op jit(solution)/shard_map/scf,fd->scd/dot_general | solution.py:55
  144.6 11.1 %all-to-all-done.2 = bf16[32,20,2048]{2,1,0:T(8,128)(2,1)} async-done(((bf16[32,20,2048]{2,1,0:T(8,128)(2,1)}), bf16[32,20,2048]{2,1,0:T(8,128)(2,1)}, u32[]{:S(2)}, u32[]{:S(2)}) %all-to-all-start.2) | async-done | bytes 2621472 | tf_op jit(solution)/shard_map/all_to_all | solution.py:51
  155.7 4.9 %all-to-all-start.1 = ((bf16[32,16,2048]{2,1,0:T(8,128)(2,1)}), bf16[32,16,2048]{2,1,0:T(8,128)(2,1)S(1)}, u32[]{:S(2)}, u32[]{:S(2)}) async-start(bf16[32,16,2048]{2,1,0:T(8,128)(2,1)} %fusion.27), calls=%async_computation.1 | async-start | bytes 4194304 | tf_op jit(solution)/shard_map/all_to_all | solution.py:58
  160.6 8.3 %fusion.8 = f32[32,20,1408]{2,0,1:T(8,128)S(1)} fusion(bf16[1,2048,1408]{2,1,0:T(8,128)(2,1)} %param.18, bf16[32,20,2048]{2,1,0:T(8,128)(2,1)} %all-to-all-done.2), kind=kOutput, calls=%fused_computation.10 | convolution fusion | flops 3690987520 | bytes 11993088 | tf_op jit(solution)/shard_map/scd,df->scf/dot_general | solution.py:52
  169.0 8.6 %fusion.18 = bf16[32,20,1408]{2,0,1:T(8,128)(2,1)S(1)} fusion(bf16[1,2048,1408]{2,1,0:T(8,128)(2,1)} %param.19, f32[32,20,1408]{2,0,1:T(8,128)S(1)} %fusion.8, bf16[32,20,2048]{2,1,0:T(8,128)(2,1)} %all-to-all-done.2), kind=kOutput, calls=%fused_computation.16 | convolution fusion | flops 3696394240 | bytes 13795328 | tf_op jit(solution)/shard_map/scd,df->scf/dot_general | solution.py:53
  177.6 4.4 %fusion.21 = bf16[32,20,2048]{2,0,1:T(8,128)(2,1)S(1)} fusion(bf16[32,20,1408]{2,0,1:T(8,128)(2,1)S(1)} %fusion.18, bf16[1,1408,2048]{2,1,0:T(8,128)(2,1)S(1)} %bitcast.85), kind=kOutput, calls=%fused_computation.17 | convolution fusion | flops 3692298240 | bytes 10190848 | tf_op jit(solution)/shard_map/scf,fd->scd/dot_general | solution.py:55
  182.0 3.2 %copy.40 = bf16[32,20,2048]{2,1,0:T(8,128)(2,1)} copy(bf16[32,20,2048]{2,0,1:T(8,128)(2,1)S(1)} %fusion.21) | data formatting | bytes 5242880 | tf_op jit(solution)/shard_map/convert_element_type | solution.py:57
  185.2 3.7 %all-to-all-done.1 = bf16[32,16,2048]{2,1,0:T(8,128)(2,1)S(1)} async-done(((bf16[32,16,2048]{2,1,0:T(8,128)(2,1)}), bf16[32,16,2048]{2,1,0:T(8,128)(2,1)S(1)}, u32[]{:S(2)}, u32[]{:S(2)}) %all-to-all-start.1) | async-done | bytes 2097184 | tf_op jit(solution)/shard_map/all_to_all | solution.py:58
  188.9 5.3 %all-to-all-start.3 = ((bf16[32,20,2048]{2,1,0:T(8,128)(2,1)}), bf16[32,20,2048]{2,1,0:T(8,128)(2,1)}, u32[]{:S(2)}, u32[]{:S(2)}) async-start(bf16[32,20,2048]{2,1,0:T(8,128)(2,1)} %copy.40), calls=%async_computation.3 | async-start | bytes 6291456 | tf_op jit(solution)/shard_map/all_to_all | solution.py:58
  194.5 3.8 %scatter_custom_fusion.1 = f32[1152]{0:T(1024)S(1)} fusion(s32[768]{0:T(1024)} %copy-done.8, f32[768]{0:T(1024)S(1)} %reshape.80, f32[]{:T(128)} %constant.36.clone.1), kind=kCustom, calls=%fused_computation.82 | custom fusion | bytes 5120 | tf_op jit(solution)/shard_map/scatter | solution.py:59
  198.5 2.4 convolution_bitcast_fusion.2
  200.9 33.2 %all-to-all-done.3 = bf16[32,20,2048]{2,1,0:T(8,128)(2,1)} async-done(((bf16[32,20,2048]{2,1,0:T(8,128)(2,1)}), bf16[32,20,2048]{2,1,0:T(8,128)(2,1)}, u32[]{:S(2)}, u32[]{:S(2)}) %all-to-all-start.3) | async-done | bytes 2621472 | tf_op jit(solution)/shard_map/all_to_all | solution.py:58
  234.1 4.7 %convolution_bitcast_fusion = f32[128,2048]{1,0:T(8,128)} fusion(bf16[32,20,2048]{2,1,0:T(8,128)(2,1)} %all-to-all-done.3, f32[32,36]{0,1:T(8,128)S(1)} %copy.33, s32[32,36]{0,1:T(8,128)S(1)} %copy.31), kind=kOutput, calls=%fused_computation.22 | convolution fusion | flops 336429056 | bytes 3679232 | tf_op jit(solution)/shard_map/rec,ecd->rd/dot_general | solution.py:68
  238.8 4.9 %convolution_bitcast_fusion.1 = f32[128,2048]{1,0:T(8,128)} fusion(bf16[32,20,2048]{2,1,0:T(8,128)(2,1)} %all-to-all-done.3, f32[32,36]{0,1:T(8,128)} %copy-done.5, s32[32,36]{0,1:T(8,128)} %copy-done.4), kind=kOutput, calls=%fused_computation.23 | convolution fusion | flops 335839232 | bytes 3679232 | tf_op jit(solution)/shard_map/rec,ecd->rd/dot_general | solution.py:68
  243.7 4.9 %fusion.37 = bf16[128,2048]{1,0:T(8,128)(2,1)} fusion(f32[128,2048]{1,0:T(8,128)} %reduce-scatter.2.cloned.1.call-done, f32[128,2048]{1,0:T(8,128)} %copy-done.2, f32[128,2048]{1,0:T(8,128)} %convolution_bitcast_fusion, f32[128,2048]{1,0:T(8,128)} %convolution_bitcast_fusion.1, f32[128,2048]{1,0:T(8,128)} %convolution_bitcast_fusion.2, ...), kind=kOutput, calls=%fused_computation.34 | convolution fusion | flops 270303232 | bytes 7873536 | tf_op jit(solution)/shard_map/rec,ecd->rd/dot_general | solution.py:68
  (54 shorter events, 3.6 us)
Async XLA Ops:
  6.5 109.4 %copy-start = (bf16[2048,352]{0,1:T(8,128)(2,1)S(1)}, bf16[2048,352]{0,1:T(8,128)(2,1)}, u32[]{:S(2)}) copy-start(bf16[2048,352]{0,1:T(8,128)(2,1)} %param.23) | copy-start | bytes 4325380
  6.5 59.5 %all-gather.3.cloned.1.call-start = ((), (), s32[]{:S(2)}) async-start(), calls=%async_computation.5 | async-start | bytes 8650752 | tf_op jit(solution)/shard_map/all_gather | solution.py:35
  7.3 96.2 %all-gather.5.cloned.1.call-start = ((), (), s32[]{:S(2)}) async-start(), calls=%async_computation.6 | async-start | bytes 2621440 | tf_op jit(solution)/shard_map/all_gather | solution.py:73
  11.5 59.5 %copy-start.8 = (s32[768]{0:T(1024)}, s32[768]{0:T(1024)S(1)}, u32[]{:S(2)}) copy-start(s32[768]{0:T(1024)S(1)} %fusion.77) | copy-start | bytes 9220
  14.9 57.1 %copy-start.6 = (f32[2048]{0:T(1024)S(1)}, f32[2048]{0:T(1024)}, u32[]{:S(2)}) copy-start(f32[2048]{0:T(1024)} %param.15) | copy-start | bytes 24580
  71.0 1.0 copy-start.2
  73.4 8.8 %copy-start.3 = (bf16[128,2048]{1,0:T(8,128)(2,1)S(1)}, bf16[128,2048]{1,0:T(8,128)(2,1)}, u32[]{:S(2)}) copy-start(bf16[128,2048]{1,0:T(8,128)(2,1)} %multiply_convert_fusion) | copy-start | bytes 1572868
  76.6 33.9 %all-to-all-start = ((bf16[32,16,2048]{2,1,0:T(8,128)(2,1)}), bf16[32,16,2048]{2,1,0:T(8,128)(2,1)}, u32[]{:S(2)}, u32[]{:S(2)}) async-start(bf16[32,16,2048]{2,1,0:T(8,128)(2,1)} %convolution_convert_fusion.1), calls=%async_computation | async-start | bytes 4194304 | tf_op jit(solution)/shard_map/all_to_all | solution.py:51
  83.0 20.5 %copy-start.10 = (bf16[2048,352]{0,1:T(8,128)(2,1)S(1)}, bf16[2048,352]{0,1:T(8,128)(2,1)}, u32[]{:S(2)}) copy-start(bf16[2048,352]{0,1:T(8,128)(2,1)} %param.21) | copy-start | bytes 4325380
  106.9 9.1 %copy-start.9 = (bf16[512,2048]{1,0:T(8,128)(2,1)S(1)}, bf16[512,2048]{1,0:T(8,128)(2,1)}, u32[]{:S(2)}) copy-start(bf16[512,2048]{1,0:T(8,128)(2,1)} %all-gather.5.cloned.1.call-done) | copy-start | bytes 6291460
  110.4 45.2 %all-to-all-start.2 = ((bf16[32,20,2048]{2,1,0:T(8,128)(2,1)}), bf16[32,20,2048]{2,1,0:T(8,128)(2,1)}, u32[]{:S(2)}, u32[]{:S(2)}) async-start(bf16[32,20,2048]{2,1,0:T(8,128)(2,1)} %copy.37), calls=%async_computation.2 | async-start | bytes 6291456 | tf_op jit(solution)/shard_map/all_to_all | solution.py:51
  115.7 128.0 %reduce-scatter.2.cloned.1.call-start = ((), (), s32[]{:S(2)}) async-start(), calls=%async_computation.7 | async-start | bytes 5242880 | tf_op jit(solution)/shard_map/reduce_scatter | solution.py:80
  155.7 33.2 %all-to-all-start.1 = ((bf16[32,16,2048]{2,1,0:T(8,128)(2,1)}), bf16[32,16,2048]{2,1,0:T(8,128)(2,1)S(1)}, u32[]{:S(2)}, u32[]{:S(2)}) async-start(bf16[32,16,2048]{2,1,0:T(8,128)(2,1)} %fusion.27), calls=%async_computation.1 | async-start | bytes 4194304 | tf_op jit(solution)/shard_map/all_to_all | solution.py:58
  160.6 17.0 %slice-start = ((s8[5767168]{0:T(1024)(128)(4,1)}), s8[4194304]{0:T(1024)(128)(4,1)S(1)}, s32[]{:S(2)}) async-start(s8[5767168]{0:T(1024)(128)(4,1)} %bitcast.84), calls=%async_computation.8 | async-start | bytes 8388608
  168.9 8.6 %slice-start.1 = ((s8[5767168]{0:T(1024)(128)(4,1)}), s8[1572864]{0:T(1024)(128)(4,1)S(1)}, s32[]{:S(2)}) async-start(s8[5767168]{0:T(1024)(128)(4,1)} %bitcast.84), calls=%async_computation.9 | async-start | bytes 3145728
  185.2 9.0 %copy-start.7 = (f32[128,6]{0,1:T(8,128)S(1)}, f32[128,6]{0,1:T(8,128)}, u32[]{:S(2)}) copy-start(f32[128,6]{0,1:T(8,128)} %param.17) | copy-start | bytes 9220
  188.9 45.2 %all-to-all-start.3 = ((bf16[32,20,2048]{2,1,0:T(8,128)(2,1)}), bf16[32,20,2048]{2,1,0:T(8,128)(2,1)}, u32[]{:S(2)}, u32[]{:S(2)}) async-start(bf16[32,20,2048]{2,1,0:T(8,128)(2,1)} %copy.40), calls=%async_computation.3 | async-start | bytes 6291456 | tf_op jit(solution)/shard_map/all_to_all | solution.py:58
  194.2 39.9 %copy-start.4 = (s32[32,36]{0,1:T(8,128)}, s32[32,36]{0,1:T(8,128)S(1)}, u32[]{:S(2)}) copy-start(s32[32,36]{0,1:T(8,128)S(1)} %copy.31) | copy-start | bytes 13828
  198.5 35.6 %copy-start.5 = (f32[32,36]{0,1:T(8,128)}, f32[32,36]{0,1:T(8,128)S(1)}, u32[]{:S(2)}) copy-start(f32[32,36]{0,1:T(8,128)S(1)} %copy.33) | copy-start | bytes 13828
  238.8 9.8 %copy-start.1 = (bf16[2048,352]{0,1:T(8,128)(2,1)S(1)}, bf16[2048,352]{0,1:T(8,128)(2,1)}, u32[]{:S(2)}) copy-start(bf16[2048,352]{0,1:T(8,128)(2,1)} %param.23) | copy-start | bytes 4325380
Sparse Core Ops, SparseCore 0:
  9.6 56.3 all-gather.2
  73.1 30.2 all-gather.4
  121.8 48.3 reduce-scatter.1

commit v8 on v7

--- a/solution.py
+++ b/solution.py
@@ -62,12 +62,15 @@
         slot_weight.reshape(experts, capacity)[None, :, :],
         0.0,
     )
-    combine_hi = combine.astype(jnp.bfloat16)
-    combine_lo = (combine - combine_hi.astype(jnp.float32)).astype(jnp.bfloat16)
     routed = sum(
-        jnp.einsum("rec,ecd->rd", weights[:, :, lo:hi], part, preferred_element_type=jnp.float32)
+        jnp.einsum(
+            "rec,ecd->rd",
+            combine[:, :, lo:hi],
+            part.astype(jnp.float32),
+            precision=lax.Precision.HIGHEST,
+            preferred_element_type=jnp.float32,
+        )
         for lo, hi, part in zip(bounds[:-1], bounds[1:], returned)
-        for weights in (combine_hi, combine_lo)
     )
 
     group_rows = lax.all_gather(normed, "req", axis=0, tiled=True)

time: 256 us -> 251 us (0.980)
  matrix products: 79.3 us -> 67.8 us
  local copies, waits for them, and re-layouts: 16.7 us -> 19.3 us
    dot_general x2, matrix products: 19 us -> 8.05 us  [body(): jnp.einsum('scf,fd->scd', hidden, w_down, preferred_element_type=jnp.floa...]
    dot_general x4 -> x2, matrix products: 16.9 us -> 9.67 us  [body(): jnp.einsum('rec,ecd->rd', combine[:, :, lo:hi], part.astype(jnp.float32),...]
    dot_general x1 -> x2, matrix products: 8.57 us -> 15.4 us  [body(): jnp.einsum('scd,df->scf', joined, w_up, preferred_element_type=jnp.float32)]
    all_to_all x2, waiting for transfers between devices: 14.6 us -> 19.4 us  [body(): lax.all_to_all(outgoing, 'exp', split_axis=0, concat_axis=0, tiled=True)]
    convert_element_type x1 -> x2, local copies, waits for them, and re-layouts: 3.19 us -> 5.67 us  [body(): result = jnp.einsum('scf,fd->scd', hidden, w_down, preferred_element_type...]
  transfers between devices with their start and end apart: 7 -> 7, of which waited for: 6 -> 5; matrix products, arithmetic and copies ran while one was open for 35% -> 32% of each run, Pallas kernels for 0% -> 0%
where the time goes in v8:
time: 251 us
  waiting for transfers between devices  123 us (49%)
  matrix products  67.8 us (27%)
  starting transfers between devices  23.5 us (9%)
  local copies, waits for them, and re-layouts  19.3 us (8%)
  between operations  13.4 us (5%)
  other arithmetic  3.8 us (2%)
    all_gather x1, waiting for transfers between devices, body(): lax.all_gather(out_weight, 'exp', axis=0, tiled=True)  51.1 us
    all_to_all x2, waiting for transfers between devices, body(): lax.all_to_all(result, 'exp', split_axis=0, concat_axis=0, tiled=True)  34.6 us
    all_to_all x2, waiting for transfers between devices, body(): lax.all_to_all(outgoing, 'exp', split_axis=0, concat_axis=0, tiled=True)  19.4 us
    all_gather x1, waiting for transfers between devices, body(): group_rows = lax.all_gather(normed, 'req', axis=0, tiled=True)  17.3 us
    dot_general x2, matrix products, body(): jnp.einsum('scd,df->scf', joined, w_gate, preferred_element_type=jnp.floa...  15.6 us
    dot_general x2, matrix products, body(): jnp.einsum('scd,df->scf', joined, w_up, preferred_element_type=jnp.float32)  15.4 us
    all_to_all x2, starting transfers between devices, body(): lax.all_to_all(outgoing, 'exp', split_axis=0, concat_axis=0, tiled=True)  13.1 us
    all_to_all x2, starting transfers between devices, body(): lax.all_to_all(result, 'exp', split_axis=0, concat_axis=0, tiled=True)  10.3 us
  transfers between devices with their start and end apart: 7, of which 5 were waited for; matrix products, arithmetic and copies ran while one was open for 32% of the time, Pallas kernels for 0%

profile of v8, /device:TPU:1, one launch (start us, length us, event | category | flops | bytes accessed | tf_op | source)
XLA Modules:
  0.0 251.0 jit_solution(3804597486548060042)
XLA Ops:
  6.5 0.7 all-gather.3.cloned.1.call-update
  7.3 0.8 copy.24
  9.3 1.7 reduce-window.6
  11.5 3.4 %scatter_custom_fusion = s32[1152]{0:T(1024)S(1)} fusion(s32[768]{0:T(1024)S(1)} %fusion.83, s32[768]{0:T(1024)S(1)} %add_select_fusion, s32[]{:T(128)} %constant.13.clone.1), kind=kCustom, calls=%fused_computation.79 | custom fusion | bytes 4612 | tf_op jit(solution)/shard_map/scatter | solution.py:30
  14.9 51.1 %all-gather.3.cloned.1.call-done = bf16[2048,2048]{1,0:T(8,128)(2,1)} async-done(((bf16[64,2048]{1,0:T(8,128)(2,1)}), bf16[2048,2048]{1,0:T(8,128)(2,1)}) %all-gather.3.cloned.1.call-update) | async-done | bytes 8388624 | tf_op jit(solution)/shard_map/all_gather | solution.py:35
  66.1 5.0 %multiply_reduce_fusion = (f32[128]{0:T(128)S(1)}, f32[128,2048]{1,0:T(8,128)S(1)}) fusion(bf16[128,2048]{1,0:T(8,128)(2,1)} %param.12, bf16[2048,2048]{1,0:T(8,128)(2,1)} %all-gather.3.cloned.1.call-done, bf16[128,2048]{1,0:T(8,128)(2,1)} %param.13), kind=kOutput, calls=%fused_computation.41 | convolution fusion | flops 1075314560 | bytes 10486272 | tf_op jit(solution)/shard_map/dot_general | solution.py:33
  71.0 1.0 multiply_convert_fusion
  72.4 3.2 %convolution_convert_fusion.1 = bf16[32,16,2048]{2,1,0:T(8,128)(2,1)} fusion(bf16[128,2048]{1,0:T(8,128)(2,1)} %multiply_convert_fusion, pred[32,36,128]{2,1,0:T(8,128)(4,1)S(1)} %iota_compare_fusion), kind=kOutput, calls=%fused_computation.20 | convolution fusion | flops 269484032 | bytes 2686976 | tf_op jit(solution)/shard_map/ecr,rd->ecd/dot_general | solution.py:48
  75.6 5.5 %all-to-all-start = ((bf16[32,16,2048]{2,1,0:T(8,128)(2,1)}), bf16[32,16,2048]{2,1,0:T(8,128)(2,1)}, u32[]{:S(2)}, u32[]{:S(2)}) async-start(bf16[32,16,2048]{2,1,0:T(8,128)(2,1)} %convolution_convert_fusion.1), calls=%async_computation | async-start | bytes 4194304 | tf_op jit(solution)/shard_map/all_to_all | solution.py:51
  81.2 0.8 convolution_convert_fusion
  82.0 3.2 %copy.34 = bf16[32,20,2048]{2,1,0:T(8,128)(2,1)} copy(bf16[32,20,2048]{2,0,1:T(8,128)(2,1)S(1)} %convolution_convert_fusion) | data formatting | bytes 5242880 | tf_op jit(solution)/shard_map/convert_element_type | solution.py:50
  85.2 17.3 %all-gather.5.cloned.1.call-done = bf16[512,2048]{1,0:T(8,128)(2,1)} async-done(((bf16[128,2048]{1,0:T(8,128)(2,1)}), bf16[512,2048]{1,0:T(8,128)(2,1)}) %all-gather.5.cloned.1.call-update) | async-done | bytes 2097168 | tf_op jit(solution)/shard_map/all_gather | solution.py:76
  102.4 3.8 %fusion.87 = f32[512,352]{0,1:T(8,128)} fusion(bf16[512,2048]{1,0:T(8,128)(2,1)} %all-gather.5.cloned.1.call-done, bf16[2048,352]{0,1:T(8,128)(2,1)} %param.21), kind=kOutput, calls=%fused_computation.89 | convolution fusion | flops 738197504 | bytes 4259840 | tf_op jit(solution)/shard_map/dot_general | solution.py:77
  106.2 6.3 %fusion.54 = f32[512,2048]{1,0:T(8,128)} fusion(bf16[2048,352]{0,1:T(8,128)(2,1)S(1)} %copy-done, bf16[512,2048]{1,0:T(8,128)(2,1)} %all-gather.5.cloned.1.call-done, bf16[2048,352]{0,1:T(8,128)(2,1)} %param.22, f32[512,352]{0,1:T(8,128)} %fusion.87), kind=kOutput, calls=%fused_computation.39 | convolution fusion | flops 1477476352 | bytes 9895936 | tf_op jit(solution)/shard_map/dot_general | solution.py:80
  112.6 7.6 %all-to-all-start.2 = ((bf16[32,20,2048]{2,1,0:T(8,128)(2,1)}), bf16[32,20,2048]{2,1,0:T(8,128)(2,1)}, u32[]{:S(2)}, u32[]{:S(2)}) async-start(bf16[32,20,2048]{2,1,0:T(8,128)(2,1)} %copy.34), calls=%async_computation.2 | async-start | bytes 6291456 | tf_op jit(solution)/shard_map/all_to_all | solution.py:51
  120.2 7.3 %fusion.10 = f32[32,16,1408]{2,1,0:T(8,128)S(1)} fusion(bf16[32,16,2048]{2,1,0:T(8,128)(2,1)} %all-to-all-done, bf16[1,2048,1408]{2,1,0:T(8,128)(2,1)} %param.18), kind=kOutput, calls=%fused_computation.12 | convolution fusion | flops 2952790016 | bytes 10747904 | tf_op jit(solution)/shard_map/scd,df->scf/dot_general | solution.py:52
  127.6 6.9 %fusion.24 = bf16[32,16,1408]{2,1,0:T(8,128)(2,1)S(1)} fusion(bf16[32,16,2048]{2,1,0:T(8,128)(2,1)} %all-to-all-done, bf16[1,2048,1408]{2,1,0:T(8,128)(2,1)} %param.19, f32[32,16,1408]{2,1,0:T(8,128)S(1)} %fusion.10), kind=kOutput, calls=%fused_computation.19 | convolution fusion | flops 2957115392 | bytes 12189696 | tf_op jit(solution)/shard_map/scd,df->scf/dot_general | solution.py:53
  134.5 3.6 %fusion.27 = bf16[32,16,2048]{2,0,1:T(8,128)(2,1)S(1)} fusion(bf16[1,1408,2048]{2,1,0:T(8,128)(2,1)S(1)} %bitcast.77, bf16[32,16,1408]{2,1,0:T(8,128)(2,1)S(1)} %fusion.24), kind=kOutput, calls=%fused_computation.21 | convolution fusion | flops 2953838592 | bytes 9306112 | tf_op jit(solution)/shard_map/scf,fd->scd/dot_general | solution.py:55
  138.2 2.5 copy.31
  140.6 19.4 %all-to-all-done.2 = bf16[32,20,2048]{2,1,0:T(8,128)(2,1)} async-done(((bf16[32,20,2048]{2,1,0:T(8,128)(2,1)}), bf16[32,20,2048]{2,1,0:T(8,128)(2,1)}, u32[]{:S(2)}, u32[]{:S(2)}) %all-to-all-start.2) | async-done | bytes 2621472 | tf_op jit(solution)/shard_map/all_to_all | solution.py:51
  160.0 5.0 %all-to-all-start.1 = ((bf16[32,16,2048]{2,1,0:T(8,128)(2,1)}), bf16[32,16,2048]{2,1,0:T(8,128)(2,1)}, u32[]{:S(2)}, u32[]{:S(2)}) async-start(bf16[32,16,2048]{2,1,0:T(8,128)(2,1)} %copy.31), calls=%async_computation.1 | async-start | bytes 4194304 | tf_op jit(solution)/shard_map/all_to_all | solution.py:58
  165.1 8.3 %fusion.8 = f32[32,20,1408]{2,0,1:T(8,128)S(1)} fusion(bf16[1,2048,1408]{2,1,0:T(8,128)(2,1)} %param.18, bf16[32,20,2048]{2,1,0:T(8,128)(2,1)} %all-to-all-done.2), kind=kOutput, calls=%fused_computation.10 | convolution fusion | flops 3690987520 | bytes 11993088 | tf_op jit(solution)/shard_map/scd,df->scf/dot_general | solution.py:52
  173.4 8.5 %fusion.18 = bf16[32,20,1408]{2,0,1:T(8,128)(2,1)S(1)} fusion(bf16[1,2048,1408]{2,1,0:T(8,128)(2,1)} %param.19, f32[32,20,1408]{2,0,1:T(8,128)S(1)} %fusion.8, bf16[32,20,2048]{2,1,0:T(8,128)(2,1)} %all-to-all-done.2), kind=kOutput, calls=%fused_computation.16 | convolution fusion | flops 3696394240 | bytes 13795328 | tf_op jit(solution)/shard_map/scd,df->scf/dot_general | solution.py:53
  181.9 4.4 %fusion.21 = bf16[32,20,2048]{2,0,1:T(8,128)(2,1)S(1)} fusion(bf16[32,20,1408]{2,0,1:T(8,128)(2,1)S(1)} %fusion.18, bf16[1,1408,2048]{2,1,0:T(8,128)(2,1)S(1)} %bitcast.79), kind=kOutput, calls=%fused_computation.17 | convolution fusion | flops 3692298240 | bytes 10190848 | tf_op jit(solution)/shard_map/scf,fd->scd/dot_general | solution.py:55
  186.4 3.2 %copy.37 = bf16[32,20,2048]{2,1,0:T(8,128)(2,1)} copy(bf16[32,20,2048]{2,0,1:T(8,128)(2,1)S(1)} %fusion.21) | data formatting | bytes 5242880 | tf_op jit(solution)/shard_map/convert_element_type | solution.py:57
  189.5 3.9 %all-to-all-done.1 = bf16[32,16,2048]{2,1,0:T(8,128)(2,1)} async-done(((bf16[32,16,2048]{2,1,0:T(8,128)(2,1)}), bf16[32,16,2048]{2,1,0:T(8,128)(2,1)}, u32[]{:S(2)}, u32[]{:S(2)}) %all-to-all-start.1) | async-done | bytes 2097184 | tf_op jit(solution)/shard_map/all_to_all | solution.py:58
  193.4 5.3 %all-to-all-start.3 = ((bf16[32,20,2048]{2,1,0:T(8,128)(2,1)}), bf16[32,20,2048]{2,1,0:T(8,128)(2,1)}, u32[]{:S(2)}, u32[]{:S(2)}) async-start(bf16[32,20,2048]{2,1,0:T(8,128)(2,1)} %copy.37), calls=%async_computation.3 | async-start | bytes 6291456 | tf_op jit(solution)/shard_map/all_to_all | solution.py:58
  198.7 0.7 copy.27
  199.6 3.6 %scatter_custom_fusion.1 = f32[1152]{0:T(1024)S(1)} fusion(s32[768]{0:T(1024)S(1)} %fusion.83, f32[768]{0:T(1024)S(1)} %reshape.80, f32[]{:T(128)} %constant.36.clone.1), kind=kCustom, calls=%fused_computation.77 | custom fusion | bytes 4612 | tf_op jit(solution)/shard_map/scatter | solution.py:59
  204.1 3.9 %convolution_bitcast_fusion = f32[128,2048]{1,0:T(8,128)S(1)} fusion(bf16[32,16,2048]{2,1,0:T(8,128)(2,1)} %all-to-all-done.1, f32[32,36]{0,1:T(8,128)} %copy.29, s32[32,36]{0,1:T(8,128)} %copy.27), kind=kOutput, calls=%fused_computation.25 | convolution fusion | flops 1610907648 | bytes 3154944 | tf_op jit(solution)/shard_map/rec,ecd->rd/dot_general | solution.py:66
  207.9 30.7 %all-to-all-done.3 = bf16[32,20,2048]{2,1,0:T(8,128)(2,1)} async-done(((bf16[32,20,2048]{2,1,0:T(8,128)(2,1)}), bf16[32,20,2048]{2,1,0:T(8,128)(2,1)}, u32[]{:S(2)}, u32[]{:S(2)}) %all-to-all-start.3) | async-done | bytes 2621472 | tf_op jit(solution)/shard_map/all_to_all | solution.py:58
  238.6 5.8 %fusion.46 = bf16[128,2048]{1,0:T(8,128)(2,1)} fusion(f32[128,2048]{1,0:T(8,128)} %reduce-scatter.2.cloned.1.call-done, f32[128,2048]{1,0:T(8,128)S(1)} %get-tuple-element.10, f32[128,2048]{1,0:T(8,128)S(1)} %convolution_bitcast_fusion, bf16[32,20,2048]{2,1,0:T(8,128)(2,1)} %all-to-all-done.3, f32[32,36]{0,1:T(8,128)} %copy.29, s32[32,36]{0,1:T(8,128)} %copy.27), kind=kOutput, calls=%fused_computation.32 | convolution fusion | flops 2014609408 | bytes 6300672 | tf_op jit(solution)/shard_map/rec,ecd->rd/dot_general | solution.py:66
  (47 shorter events, 3.2 us)
Async XLA Ops:
  6.5 99.7 %copy-start = (bf16[2048,352]{0,1:T(8,128)(2,1)S(1)}, bf16[2048,352]{0,1:T(8,128)(2,1)}, u32[]{:S(2)}) copy-start(bf16[2048,352]{0,1:T(8,128)(2,1)} %param.23) | copy-start | bytes 4325380
  6.5 59.5 %all-gather.3.cloned.1.call-start = ((), (), s32[]{:S(2)}) async-start(), calls=%async_computation.5 | async-start | bytes 8650752 | tf_op jit(solution)/shard_map/all_gather | solution.py:35
  7.3 95.2 %all-gather.5.cloned.1.call-start = ((), (), s32[]{:S(2)}) async-start(), calls=%async_computation.6 | async-start | bytes 2621440 | tf_op jit(solution)/shard_map/all_gather | solution.py:76
  14.9 56.1 %copy-start.3 = (f32[2048]{0:T(1024)S(1)}, f32[2048]{0:T(1024)}, u32[]{:S(2)}) copy-start(f32[2048]{0:T(1024)} %param.15) | copy-start | bytes 24580
  72.4 8.8 %copy-start.2 = (bf16[128,2048]{1,0:T(8,128)(2,1)S(1)}, bf16[128,2048]{1,0:T(8,128)(2,1)}, u32[]{:S(2)}) copy-start(bf16[128,2048]{1,0:T(8,128)(2,1)} %multiply_convert_fusion) | copy-start | bytes 1572868
  75.6 37.0 %all-to-all-start = ((bf16[32,16,2048]{2,1,0:T(8,128)(2,1)}), bf16[32,16,2048]{2,1,0:T(8,128)(2,1)}, u32[]{:S(2)}, u32[]{:S(2)}) async-start(bf16[32,16,2048]{2,1,0:T(8,128)(2,1)} %convolution_convert_fusion.1), calls=%async_computation | async-start | bytes 4194304 | tf_op jit(solution)/shard_map/all_to_all | solution.py:51
  81.1 157.5 %reduce-scatter.2.cloned.1.call-start = ((), (), s32[]{:S(2)}) async-start(), calls=%async_computation.7 | async-start | bytes 5242880 | tf_op jit(solution)/shard_map/reduce_scatter | solution.py:83
  112.6 47.4 %all-to-all-start.2 = ((bf16[32,20,2048]{2,1,0:T(8,128)(2,1)}), bf16[32,20,2048]{2,1,0:T(8,128)(2,1)}, u32[]{:S(2)}, u32[]{:S(2)}) async-start(bf16[32,20,2048]{2,1,0:T(8,128)(2,1)} %copy.34), calls=%async_computation.2 | async-start | bytes 6291456 | tf_op jit(solution)/shard_map/all_to_all | solution.py:51
  120.2 14.3 %slice-start = ((s8[5767168]{0:T(1024)(128)(4,1)}), s8[4194304]{0:T(1024)(128)(4,1)S(1)}, s32[]{:S(2)}) async-start(s8[5767168]{0:T(1024)(128)(4,1)} %bitcast.76), calls=%async_computation.8 | async-start | bytes 8388608
  127.6 7.0 %slice-start.1 = ((s8[5767168]{0:T(1024)(128)(4,1)}), s8[1572864]{0:T(1024)(128)(4,1)S(1)}, s32[]{:S(2)}) async-start(s8[5767168]{0:T(1024)(128)(4,1)} %bitcast.76), calls=%async_computation.9 | async-start | bytes 3145728
  160.0 33.4 %all-to-all-start.1 = ((bf16[32,16,2048]{2,1,0:T(8,128)(2,1)}), bf16[32,16,2048]{2,1,0:T(8,128)(2,1)}, u32[]{:S(2)}, u32[]{:S(2)}) async-start(bf16[32,16,2048]{2,1,0:T(8,128)(2,1)} %copy.31), calls=%async_computation.1 | async-start | bytes 4194304 | tf_op jit(solution)/shard_map/all_to_all | solution.py:58
  165.1 16.8 %slice-start.2 = ((s8[5767168]{0:T(1024)(128)(4,1)}), s8[4194304]{0:T(1024)(128)(4,1)S(1)}, s32[]{:S(2)}) async-start(s8[5767168]{0:T(1024)(128)(4,1)} %bitcast.78), calls=%async_computation.10 | async-start | bytes 8388608
  173.4 8.6 %slice-start.3 = ((s8[5767168]{0:T(1024)(128)(4,1)}), s8[1572864]{0:T(1024)(128)(4,1)S(1)}, s32[]{:S(2)}) async-start(s8[5767168]{0:T(1024)(128)(4,1)} %bitcast.78), calls=%async_computation.11 | async-start | bytes 3145728
  189.5 9.8 %copy-start.4 = (f32[128,6]{0,1:T(8,128)S(1)}, f32[128,6]{0,1:T(8,128)}, u32[]{:S(2)}) copy-start(f32[128,6]{0,1:T(8,128)} %param.17) | copy-start | bytes 9220
  193.4 45.2 %all-to-all-start.3 = ((bf16[32,20,2048]{2,1,0:T(8,128)(2,1)}), bf16[32,20,2048]{2,1,0:T(8,128)(2,1)}, u32[]{:S(2)}, u32[]{:S(2)}) async-start(bf16[32,20,2048]{2,1,0:T(8,128)(2,1)} %copy.37), calls=%async_computation.3 | async-start | bytes 6291456 | tf_op jit(solution)/shard_map/all_to_all | solution.py:58
  204.1 40.4 %copy-start.1 = (bf16[2048,352]{0,1:T(8,128)(2,1)S(1)}, bf16[2048,352]{0,1:T(8,128)(2,1)}, u32[]{:S(2)}) copy-start(bf16[2048,352]{0,1:T(8,128)(2,1)} %param.23) | copy-start | bytes 4325380
Sparse Core Ops, SparseCore 0:
  9.6 56.3 all-gather.2
  72.1 30.2 all-gather.4
  112.7 46.9 reduce-scatter.1

commit v9 on v8

--- a/solution.py
+++ b/solution.py
@@ -42,20 +42,51 @@
 
     pick = (table.reshape(experts, capacity)[:, :, None] == rows[None, None, :]).astype(jnp.bfloat16)
     w_gate, w_up, w_down = expert_gate[0], expert_up[0], expert_down[0]
-    bounds = [0, min(16, capacity), capacity] if capacity > 16 else [0, capacity]
+    tail = min(16, capacity)
+    bounds = [0, capacity - tail, capacity] if capacity > tail else [0, capacity]
+    lanes = 128
+    blocks = width // lanes
     returned = []
+    landed = None
     for lo, hi in zip(bounds[:-1], bounds[1:]):
-        outgoing = jnp.einsum(
-            "ecr,rd->ecd", pick[:, lo:hi], normed, preferred_element_type=jnp.float32
-        ).astype(jnp.bfloat16)
-        joined = lax.all_to_all(outgoing, "exp", split_axis=0, concat_axis=0, tiled=True)
-        gate_part = jnp.einsum("scd,df->scf", joined, w_gate, preferred_element_type=jnp.float32)
-        up_part = jnp.einsum("scd,df->scf", joined, w_up, preferred_element_type=jnp.float32)
+        size = hi - lo
+        chunk_pick = pick[:, lo:hi]
+        if landed is not None:
+            chunk_pick, _ = lax.optimization_barrier((chunk_pick, landed))
+        if size % 16:
+            outgoing = jnp.einsum(
+                "ecr,rjk->ecjk", chunk_pick, normed.reshape(row_count, blocks, lanes),
+                preferred_element_type=jnp.float32,
+            ).astype(jnp.bfloat16).reshape(experts, size * blocks, lanes)
+            joined = lax.all_to_all(
+                outgoing, "exp", split_axis=0, concat_axis=0, tiled=True
+            ).reshape(experts, size, blocks, lanes)
+            gate_part = jnp.einsum("scjk,jkf->scf", joined, w_gate.reshape(blocks, lanes, -1),
+                                   preferred_element_type=jnp.float32)
+            up_part = jnp.einsum("scjk,jkf->scf", joined, w_up.reshape(blocks, lanes, -1),
+                                 preferred_element_type=jnp.float32)
+        else:
+            outgoing = jnp.einsum(
+                "ecr,rd->ecd", chunk_pick, normed, preferred_element_type=jnp.float32
+            ).astype(jnp.bfloat16)
+            joined = lax.all_to_all(outgoing, "exp", split_axis=0, concat_axis=0, tiled=True)
+            gate_part = jnp.einsum("scd,df->scf", joined, w_gate, preferred_element_type=jnp.float32)
+            up_part = jnp.einsum("scd,df->scf", joined, w_up, preferred_element_type=jnp.float32)
+        landed = joined
         hidden = (jax.nn.silu(gate_part) * up_part).astype(jnp.bfloat16)
         result = jnp.einsum(
             "scf,fd->scd", hidden, w_down, preferred_element_type=jnp.float32
         ).astype(jnp.bfloat16)
-        returned.append(lax.all_to_all(result, "exp", split_axis=0, concat_axis=0, tiled=True))
+        if returned:
+            result, _ = lax.optimization_barrier((result, returned[-1]))
+        if size % 16:
+            back = lax.all_to_all(
+                result.reshape(experts, size * blocks, lanes), "exp",
+                split_axis=0, concat_axis=0, tiled=True,
+            )
+            returned.append(back.reshape(experts, size, width))
+        else:
+            returned.append(lax.all_to_all(result, "exp", split_axis=0, concat_axis=0, tiled=True))
     slot_weight = jnp.zeros((experts * capacity,), jnp.float32).at[slot].set(gate_weights.reshape(-1))
     combine = jnp.where(
         table.reshape(experts, capacity)[None, :, :] == rows[:, None, None],

time: 251 us -> 276 us (1.100)
  local copies, waits for them, and re-layouts: 19.3 us -> 37.9 us
  matrix products: 67.8 us -> 71.5 us
    all_gather x1, waiting for transfers between devices: 17.3 us -> 0.02 us  [body(): group_rows = lax.all_gather(normed, 'req', axis=0, tiled=True)]
    all_to_all x0 -> x1, waiting for transfers between devices: none -> 15.8 us  [body(): lax.all_to_all(result.reshape(experts, size * blocks, lanes), 'exp', spli...]
    all_to_all x2, waiting for transfers between devices: 19.4 us -> 33.9 us  [body(): lax.all_to_all(outgoing, 'exp', split_axis=0, concat_axis=0, tiled=True)]
    reshape x0 -> x3, local copies, waits for them, and re-layouts: none -> 13.7 us  [the longest x1 5.58 us: body(): result.reshape(experts, size * blocks, lanes)]
    dot_general x2, matrix products: 8.05 us -> 21.6 us  [body(): jnp.einsum('scf,fd->scd', hidden, w_down, preferred_element_type=jnp.floa...]
    all_to_all x2 -> x1, waiting for transfers between devices: 34.6 us -> 23.7 us  [body(): lax.all_to_all(result, 'exp', split_axis=0, concat_axis=0, tiled=True)]
    dot_general x2 -> x1, matrix products: 15.6 us -> 6.62 us  [body(): jnp.einsum('scd,df->scf', joined, w_gate, preferred_element_type=jnp.floa...]
    dot_general x2 -> x1, matrix products: 15.4 us -> 6.84 us  [body(): jnp.einsum('scd,df->scf', joined, w_up, preferred_element_type=jnp.float32)]
  transfers between devices with their start and end apart: 7 -> 7, of which waited for: 5 -> 4; matrix products, arithmetic and copies ran while one was open for 32% -> 37% of each run, Pallas kernels for 0% -> 0%
where the time goes in v9:
time: 276 us; the launch traced here: 275 us
  waiting for transfers between devices  125 us (45%)
  matrix products  71.5 us (26%)
  local copies, waits for them, and re-layouts  37.9 us (14%)
  starting transfers between devices  24.1 us (9%)
  between operations  13.4 us (5%)
  other arithmetic  3.83 us (1%)
    all_gather x1, waiting for transfers between devices, body(): lax.all_gather(out_weight, 'exp', axis=0, tiled=True)  50.3 us
    all_to_all x2, waiting for transfers between devices, body(): lax.all_to_all(outgoing, 'exp', split_axis=0, concat_axis=0, tiled=True)  33.9 us
    all_to_all x1, waiting for transfers between devices, body(): lax.all_to_all(result, 'exp', split_axis=0, concat_axis=0, tiled=True)  23.7 us
    dot_general x2, matrix products, body(): jnp.einsum('scf,fd->scd', hidden, w_down, preferred_element_type=jnp.floa...  21.6 us
    all_to_all x1, waiting for transfers between devices, body(): lax.all_to_all(result.reshape(experts, size * blocks, lanes), 'exp', spli...  15.8 us
    all_to_all x2, starting transfers between devices, body(): lax.all_to_all(outgoing, 'exp', split_axis=0, concat_axis=0, tiled=True)  10.8 us
    dot_general x2, matrix products, body(): jnp.einsum('rec,ecd->rd', combine[:, :, lo:hi], part.astype(jnp.float32),...  9.68 us
    dot_general x1, matrix products, body(): jnp.einsum('scjk,jkf->scf', joined, w_up.reshape(blocks, lanes, -1), pref...  8.8 us
  transfers between devices with their start and end apart: 7, of which 4 were waited for; matrix products, arithmetic and copies ran while one was open for 37% of the time, Pallas kernels for 0%

profile of v9, /device:TPU:1, one launch (start us, length us, event | category | flops | bytes accessed | tf_op | source)
XLA Modules:
  0.0 275.3 jit_solution(7892987330593577609)
XLA Ops:
  6.5 0.7 all-gather.3.cloned.1.call-update
  7.3 0.8 copy.28
  8.4 1.7 reduce-window.6
  11.5 3.4 %scatter_custom_fusion = s32[1152]{0:T(1024)S(1)} fusion(s32[768]{0:T(1024)S(1)} %fusion.74, s32[768]{0:T(1024)S(1)} %add_select_fusion, s32[]{:T(128)} %constant.13.clone.1), kind=kCustom, calls=%fused_computation.80 | custom fusion | bytes 4612 | tf_op jit(solution)/shard_map/scatter | solution.py:30
  15.7 50.3 %all-gather.3.cloned.1.call-done = bf16[2048,2048]{1,0:T(8,128)(2,1)} async-done(((bf16[64,2048]{1,0:T(8,128)(2,1)}), bf16[2048,2048]{1,0:T(8,128)(2,1)}) %all-gather.3.cloned.1.call-update) | async-done | bytes 8388624 | tf_op jit(solution)/shard_map/all_gather | solution.py:35
  66.1 5.0 %multiply_reduce_fusion = (f32[128]{0:T(128)S(1)}, f32[128,2048]{1,0:T(8,128)S(1)}) fusion(bf16[128,2048]{1,0:T(8,128)(2,1)} %param.12, bf16[2048,2048]{1,0:T(8,128)(2,1)} %all-gather.3.cloned.1.call-done, bf16[128,2048]{1,0:T(8,128)(2,1)} %param.13), kind=kOutput, calls=%fused_computation.40 | convolution fusion | flops 1075314560 | bytes 10486272 | tf_op jit(solution)/shard_map/dot_general | solution.py:33
  71.0 0.9 multiply_convert_fusion
  72.0 0.9 convolution_convert_fusion.1
  73.0 2.5 copy.36
  75.5 5.5 %all-to-all-start = ((bf16[32,320,128]{2,1,0:T(8,128)(2,1)}), bf16[32,320,128]{2,1,0:T(8,128)(2,1)}, u32[]{:S(2)}, u32[]{:S(2)}) async-start(bf16[32,320,128]{2,1,0:T(8,128)(2,1)} %copy.36), calls=%async_computation | async-start | bytes 5242880 | tf_op jit(solution)/shard_map/all_to_all | solution.py:61
  81.1 33.9 %all-to-all-done = bf16[32,320,128]{2,1,0:T(8,128)(2,1)} async-done(((bf16[32,320,128]{2,1,0:T(8,128)(2,1)}), bf16[32,320,128]{2,1,0:T(8,128)(2,1)}, u32[]{:S(2)}, u32[]{:S(2)}) %all-to-all-start) | async-done | bytes 2621472 | tf_op jit(solution)/shard_map/all_to_all | solution.py:61
  115.0 5.0 %copy.37 = bf16[32,320,128]{2,0,1:T(8,128)(2,1)} copy(bf16[32,320,128]{2,1,0:T(8,128)(2,1)} %all-to-all-done) | data formatting | bytes 5242880 | tf_op jit(solution)/shard_map/all_to_all | solution.py:61
  120.0 2.0 convolution_convert_fusion
  122.0 5.3 %all-to-all-start.2 = ((bf16[32,16,2048]{2,1,0:T(8,128)(2,1)}), bf16[32,16,2048]{2,1,0:T(8,128)(2,1)}, u32[]{:S(2)}, u32[]{:S(2)}) async-start(bf16[32,16,2048]{2,1,0:T(8,128)(2,1)} %convolution_convert_fusion), calls=%async_computation.2 | async-start | bytes 4194304 | tf_op jit(solution)/shard_map/all_to_all | solution.py:72
  127.6 3.8 %fusion.80 = f32[512,352]{0,1:T(8,128)} fusion(bf16[512,2048]{1,0:T(8,128)(2,1)} %all-gather.5.cloned.1.call-done, bf16[2048,352]{0,1:T(8,128)(2,1)} %param.21), kind=kOutput, calls=%fused_computation.92 | convolution fusion | flops 738197504 | bytes 4259840 | tf_op jit(solution)/shard_map/dot_general | solution.py:108
  131.4 6.3 %fusion.46 = f32[512,2048]{1,0:T(8,128)} fusion(bf16[2048,352]{0,1:T(8,128)(2,1)S(1)} %copy-done, bf16[512,2048]{1,0:T(8,128)(2,1)} %all-gather.5.cloned.1.call-done, bf16[2048,352]{0,1:T(8,128)(2,1)} %param.22, f32[512,352]{0,1:T(8,128)} %fusion.80), kind=kOutput, calls=%fused_computation.38 | convolution fusion | flops 1477476352 | bytes 9895936 | tf_op jit(solution)/shard_map/dot_general | solution.py:111
  137.7 8.8 %fusion.79 = f32[32,20,1408,1]{2,0,3,1:T(8,128)} fusion(bf16[32,20,16,128]{3,0,2,1:T(8,128)(2,1)} %bitcast.113, bf16[16,128,1408,1]{2,1,0,3:T(8,128)(2,1)} %bitcast.117), kind=kOutput, calls=%fused_computation.91 | convolution fusion | flops 3690987520 | bytes 11993088 | tf_op jit(solution)/shard_map/scjk,jkf->scf/dot_general | solution.py:66
  146.5 16.9 %fusion.15 = bf16[32,20,2048]{2,0,1:T(8,128)(2,1)} fusion(bf16[1,1408,2048]{2,1,0:T(8,128)(2,1)} %param.20, f32[32,20,1408,1]{2,0,3,1:T(8,128)} %fusion.79, bf16[32,20,16,128]{3,0,2,1:T(8,128)(2,1)} %bitcast.114, bf16[16,128,1408,1]{2,1,0,3:T(8,128)(2,1)} %bitcast.116), kind=kOutput, calls=%fused_computation.18 | convolution fusion | flops 7388692480 | bytes 20381696 | tf_op jit(solution)/shard_map/scf,fd->scd/dot_general | solution.py:77
  163.4 4.9 %copy.38 = bf16[32,20,2048]{2,1,0:T(8,128)(2,1)} copy(bf16[32,20,2048]{2,0,1:T(8,128)(2,1)} %fusion.15) | data formatting | bytes 5242880 | tf_op jit(solution)/shard_map/convert_element_type | solution.py:79
  168.4 5.6 %reshape.86 = bf16[32,320,128]{2,1,0:T(8,128)(2,1)} reshape(bf16[32,20,2048]{2,1,0:T(8,128)(2,1)} %copy.38) | data formatting | bytes 5242880 | tf_op jit(solution)/shard_map/reshape | solution.py:84
  174.0 7.6 %all-to-all-start.1 = ((bf16[32,320,128]{2,1,0:T(8,128)(2,1)}), bf16[32,320,128]{2,1,0:T(8,128)(2,1)}, u32[]{:S(2)}, u32[]{:S(2)}) async-start(bf16[32,320,128]{2,1,0:T(8,128)(2,1)} %reshape.86), calls=%async_computation.1 | async-start | bytes 5242880 | tf_op jit(solution)/shard_map/all_to_all | solution.py:83
  181.5 6.6 %fusion.2 = f32[32,16,1408]{2,1,0:T(8,128)S(1)} fusion(bf16[32,16,2048]{2,1,0:T(8,128)(2,1)} %all-to-all-done.2, bf16[1,2048,1408]{2,1,0:T(8,128)(2,1)} %param.18), kind=kOutput, calls=%fused_computation.4 | convolution fusion | flops 2952790016 | bytes 10747904 | tf_op jit(solution)/shard_map/scd,df->scf/dot_general | solution.py:73
  188.2 6.8 %fusion.18 = bf16[32,16,1408]{2,1,0:T(8,128)(2,1)S(1)} fusion(bf16[32,16,2048]{2,1,0:T(8,128)(2,1)} %all-to-all-done.2, bf16[1,2048,1408]{2,1,0:T(8,128)(2,1)} %param.19, f32[32,16,1408]{2,1,0:T(8,128)S(1)} %fusion.2), kind=kOutput, calls=%fused_computation.20 | convolution fusion | flops 2957115392 | bytes 12189696 | tf_op jit(solution)/shard_map/scd,df->scf/dot_general | solution.py:74
  195.1 4.6 %fusion.21 = bf16[32,16,2048]{2,0,1:T(8,128)(2,1)} fusion(bf16[1,1408,2048]{2,1,0:T(8,128)(2,1)S(1)} %bitcast.119, bf16[32,16,1408]{2,1,0:T(8,128)(2,1)S(1)} %fusion.18), kind=kOutput, calls=%fused_computation.21 | convolution fusion | flops 2953838592 | bytes 9306112 | tf_op jit(solution)/shard_map/scf,fd->scd/dot_general | solution.py:77
  199.7 15.8 %all-to-all-done.1 = bf16[32,320,128]{2,1,0:T(8,128)(2,1)} async-done(((bf16[32,320,128]{2,1,0:T(8,128)(2,1)}), bf16[32,320,128]{2,1,0:T(8,128)(2,1)}, u32[]{:S(2)}, u32[]{:S(2)}) %all-to-all-start.1) | async-done | bytes 2621472 | tf_op jit(solution)/shard_map/all_to_all | solution.py:83
  215.5 5.6 %reshape.87 = bf16[32,20,2048]{2,1,0:T(8,128)(2,1)} reshape(bf16[32,320,128]{2,1,0:T(8,128)(2,1)} %all-to-all-done.1) | data formatting | bytes 5242880 | tf_op jit(solution)/shard_map/reshape | solution.py:87
  221.0 4.1 %copy.42 = bf16[32,16,2048]{2,1,0:T(8,128)(2,1)} copy(bf16[32,16,2048]{2,0,1:T(8,128)(2,1)} %fusion.21) | data formatting | bytes 4194304 | tf_op jit(solution)/shard_map/optimization_barrier | solution.py:81
  225.2 5.4 %all-to-all-start.3 = ((bf16[32,16,2048]{2,1,0:T(8,128)(2,1)}), bf16[32,16,2048]{2,1,0:T(8,128)(2,1)}, u32[]{:S(2)}, u32[]{:S(2)}) async-start(bf16[32,16,2048]{2,1,0:T(8,128)(2,1)} %copy.42), calls=%async_computation.3 | async-start | bytes 4194304 | tf_op jit(solution)/shard_map/all_to_all | solution.py:89
  230.9 3.6 %scatter_custom_fusion.1 = f32[1152]{0:T(1024)S(1)} fusion(s32[768]{0:T(1024)S(1)} %fusion.74, f32[768]{0:T(1024)S(1)} %reshape.100, f32[]{:T(128)} %constant.36.clone.1), kind=kCustom, calls=%fused_computation.78 | custom fusion | bytes 4612 | tf_op jit(solution)/shard_map/scatter | solution.py:90
  235.3 23.7 %all-to-all-done.3 = bf16[32,16,2048]{2,1,0:T(8,128)(2,1)} async-done(((bf16[32,16,2048]{2,1,0:T(8,128)(2,1)}), bf16[32,16,2048]{2,1,0:T(8,128)(2,1)}, u32[]{:S(2)}, u32[]{:S(2)}) %all-to-all-start.3) | async-done | bytes 2097184 | tf_op jit(solution)/shard_map/all_to_all | solution.py:89
  259.0 3.9 %convolution_bitcast_fusion = f32[128,2048]{1,0:T(8,128)S(1)} fusion(bf16[32,16,2048]{2,1,0:T(8,128)(2,1)} %all-to-all-done.3, f32[32,36]{0,1:T(8,128)} %copy.33, s32[32,36]{0,1:T(8,128)} %copy-done.3), kind=kOutput, calls=%fused_computation.25 | convolution fusion | flops 1610907648 | bytes 3154944 | tf_op jit(solution)/shard_map/rec,ecd->rd/dot_general | solution.py:97
  262.9 5.8 %fusion.40 = bf16[128,2048]{1,0:T(8,128)(2,1)} fusion(f32[128,2048]{1,0:T(8,128)} %reduce-scatter.2.cloned.1.call-done, f32[128,2048]{1,0:T(8,128)S(1)} %get-tuple-element.14, f32[128,2048]{1,0:T(8,128)S(1)} %convolution_bitcast_fusion, bf16[32,20,2048]{2,1,0:T(8,128)(2,1)} %reshape.87, f32[32,36]{0,1:T(8,128)} %copy.33, s32[32,36]{0,1:T(8,128)} %copy-done.3), kind=kOutput, calls=%fused_computation.32 | convolution fusion | flops 2014609408 | bytes 6300672 | tf_op jit(solution)/shard_map/rec,ecd->rd/dot_general | solution.py:97
  (46 shorter events, 3.9 us)
Async XLA Ops:
  6.5 124.8 %copy-start = (bf16[2048,352]{0,1:T(8,128)(2,1)S(1)}, bf16[2048,352]{0,1:T(8,128)(2,1)}, u32[]{:S(2)}) copy-start(bf16[2048,352]{0,1:T(8,128)(2,1)} %param.23) | copy-start | bytes 4325380
  6.5 59.5 %all-gather.3.cloned.1.call-start = ((), (), s32[]{:S(2)}) async-start(), calls=%async_computation.5 | async-start | bytes 8650752 | tf_op jit(solution)/shard_map/all_gather | solution.py:35
  7.3 120.3 %all-gather.5.cloned.1.call-start = ((), (), s32[]{:S(2)}) async-start(), calls=%async_computation.6 | async-start | bytes 2621440 | tf_op jit(solution)/shard_map/all_gather | solution.py:107
  15.1 0.6 copy-start.3
  15.7 55.3 %copy-start.4 = (f32[2048]{0:T(1024)S(1)}, f32[2048]{0:T(1024)}, u32[]{:S(2)}) copy-start(f32[2048]{0:T(1024)} %param.15) | copy-start | bytes 24580
  75.5 39.5 %all-to-all-start = ((bf16[32,320,128]{2,1,0:T(8,128)(2,1)}), bf16[32,320,128]{2,1,0:T(8,128)(2,1)}, u32[]{:S(2)}, u32[]{:S(2)}) async-start(bf16[32,320,128]{2,1,0:T(8,128)(2,1)} %copy.36), calls=%async_computation | async-start | bytes 5242880 | tf_op jit(solution)/shard_map/all_to_all | solution.py:61
  81.0 38.9 %copy-start.2 = (bf16[128,2048]{1,0:T(8,128)(2,1)S(1)}, bf16[128,2048]{1,0:T(8,128)(2,1)}, u32[]{:S(2)}) copy-start(bf16[128,2048]{1,0:T(8,128)(2,1)} %multiply_convert_fusion) | copy-start | bytes 1572868
  122.0 52.0 %all-to-all-start.2 = ((bf16[32,16,2048]{2,1,0:T(8,128)(2,1)}), bf16[32,16,2048]{2,1,0:T(8,128)(2,1)}, u32[]{:S(2)}, u32[]{:S(2)}) async-start(bf16[32,16,2048]{2,1,0:T(8,128)(2,1)} %convolution_convert_fusion), calls=%async_computation.2 | async-start | bytes 4194304 | tf_op jit(solution)/shard_map/all_to_all | solution.py:72
  127.3 135.6 %reduce-scatter.2.cloned.1.call-start = ((), (), s32[]{:S(2)}) async-start(), calls=%async_computation.7 | async-start | bytes 5242880 | tf_op jit(solution)/shard_map/reduce_scatter | solution.py:114
  174.0 41.5 %all-to-all-start.1 = ((bf16[32,320,128]{2,1,0:T(8,128)(2,1)}), bf16[32,320,128]{2,1,0:T(8,128)(2,1)}, u32[]{:S(2)}, u32[]{:S(2)}) async-start(bf16[32,320,128]{2,1,0:T(8,128)(2,1)} %reshape.86), calls=%async_computation.1 | async-start | bytes 5242880 | tf_op jit(solution)/shard_map/all_to_all | solution.py:83
  181.5 13.5 %slice-start = ((s8[5767168]{0:T(1024)(128)(4,1)}), s8[4194304]{0:T(1024)(128)(4,1)S(1)}, s32[]{:S(2)}) async-start(s8[5767168]{0:T(1024)(128)(4,1)} %bitcast.118), calls=%async_computation.8 | async-start | bytes 8388608
  188.2 6.9 %slice-start.1 = ((s8[5767168]{0:T(1024)(128)(4,1)}), s8[1572864]{0:T(1024)(128)(4,1)S(1)}, s32[]{:S(2)}) async-start(s8[5767168]{0:T(1024)(128)(4,1)} %bitcast.118), calls=%async_computation.9 | async-start | bytes 3145728
  225.2 5.5 %copy-start.5 = (f32[128,6]{0,1:T(8,128)S(1)}, f32[128,6]{0,1:T(8,128)}, u32[]{:S(2)}) copy-start(f32[128,6]{0,1:T(8,128)} %param.17) | copy-start | bytes 9220
  225.2 33.9 %all-to-all-start.3 = ((bf16[32,16,2048]{2,1,0:T(8,128)(2,1)}), bf16[32,16,2048]{2,1,0:T(8,128)(2,1)}, u32[]{:S(2)}, u32[]{:S(2)}) async-start(bf16[32,16,2048]{2,1,0:T(8,128)(2,1)} %copy.42), calls=%async_computation.3 | async-start | bytes 4194304 | tf_op jit(solution)/shard_map/all_to_all | solution.py:89
  259.0 9.7 %copy-start.1 = (bf16[2048,352]{0,1:T(8,128)(2,1)S(1)}, bf16[2048,352]{0,1:T(8,128)(2,1)}, u32[]{:S(2)}) copy-start(bf16[2048,352]{0,1:T(8,128)(2,1)} %param.23) | copy-start | bytes 4325380
Sparse Core Ops, SparseCore 0:
  9.6 56.3 all-gather.2
  72.1 30.2 all-gather.4
  137.8 48.3 reduce-scatter.1

commit v10 on v8

--- a/solution.py
+++ b/solution.py
@@ -42,11 +42,15 @@
 
     pick = (table.reshape(experts, capacity)[:, :, None] == rows[None, None, :]).astype(jnp.bfloat16)
     w_gate, w_up, w_down = expert_gate[0], expert_up[0], expert_down[0]
-    bounds = [0, min(16, capacity), capacity] if capacity > 16 else [0, capacity]
+    bounds = [0, capacity - 16, capacity] if capacity > 16 else [0, capacity]
     returned = []
+    landed = None
     for lo, hi in zip(bounds[:-1], bounds[1:]):
+        chunk_pick = pick[:, lo:hi]
+        if landed is not None:
+            chunk_pick, _ = lax.optimization_barrier((chunk_pick, landed))
         outgoing = jnp.einsum(
-            "ecr,rd->ecd", pick[:, lo:hi], normed, preferred_element_type=jnp.float32
+            "ecr,rd->ecd", chunk_pick, normed, preferred_element_type=jnp.float32
         ).astype(jnp.bfloat16)
         joined = lax.all_to_all(outgoing, "exp", split_axis=0, concat_axis=0, tiled=True)
         gate_part = jnp.einsum("scd,df->scf", joined, w_gate, preferred_element_type=jnp.float32)
@@ -55,6 +59,9 @@
         result = jnp.einsum(
             "scf,fd->scd", hidden, w_down, preferred_element_type=jnp.float32
         ).astype(jnp.bfloat16)
+        landed = joined
+        if returned:
+            result, _ = lax.optimization_barrier((result, returned[-1]))
         returned.append(lax.all_to_all(result, "exp", split_axis=0, concat_axis=0, tiled=True))
     slot_weight = jnp.zeros((experts * capacity,), jnp.float32).at[slot].set(gate_weights.reshape(-1))
     combine = jnp.where(

time: 251 us -> 268 us (1.068)
  waiting for transfers between devices: 123 us -> 140 us
    all_to_all x2, waiting for transfers between devices: 19.4 us -> 43.2 us  [body(): lax.all_to_all(outgoing, 'exp', split_axis=0, concat_axis=0, tiled=True)]
    all_gather x1, waiting for transfers between devices: 17.3 us -> 0.01 us  [body(): group_rows = lax.all_gather(normed, 'req', axis=0, tiled=True)]
    all_to_all x2, waiting for transfers between devices: 34.6 us -> 45.4 us  [body(): lax.all_to_all(result, 'exp', split_axis=0, concat_axis=0, tiled=True)]
    optimization_barrier x0 -> x1, local copies, waits for them, and re-layouts: none -> 4.13 us  [body(): result, _ = lax.optimization_barrier((result, returned[-1]))]
    convert_element_type x2 -> x1, local copies, waits for them, and re-layouts: 5.67 us -> 3.18 us  [body(): result = jnp.einsum('scf,fd->scd', hidden, w_down, preferred_element_type...]
  transfers between devices with their start and end apart: 7 -> 7, of which waited for: 5 -> 5; matrix products, arithmetic and copies ran while one was open for 32% -> 26% of each run, Pallas kernels for 0% -> 0%
where the time goes in v10:
time: 268 us; the launch traced here: 267 us
  waiting for transfers between devices  140 us (52%)
  matrix products  67.2 us (25%)
  local copies, waits for them, and re-layouts  21.3 us (8%)
  starting transfers between devices  21 us (8%)
  between operations  13.4 us (5%)
  other arithmetic  3.82 us (1%)
    all_gather x1, waiting for transfers between devices, body(): lax.all_gather(out_weight, 'exp', axis=0, tiled=True)  51.1 us
    all_to_all x2, waiting for transfers between devices, body(): lax.all_to_all(result, 'exp', split_axis=0, concat_axis=0, tiled=True)  45.4 us
    all_to_all x2, waiting for transfers between devices, body(): lax.all_to_all(outgoing, 'exp', split_axis=0, concat_axis=0, tiled=True)  43.2 us
    dot_general x2, matrix products, body(): jnp.einsum('scd,df->scf', joined, w_up, preferred_element_type=jnp.float32)  15.5 us
    dot_general x2, matrix products, body(): jnp.einsum('scd,df->scf', joined, w_gate, preferred_element_type=jnp.floa...  15 us
    all_to_all x2, starting transfers between devices, body(): lax.all_to_all(outgoing, 'exp', split_axis=0, concat_axis=0, tiled=True)  10.6 us
    all_to_all x2, starting transfers between devices, body(): lax.all_to_all(result, 'exp', split_axis=0, concat_axis=0, tiled=True)  10.4 us
    dot_general x2, matrix products, body(): jnp.einsum('rec,ecd->rd', combine[:, :, lo:hi], part.astype(jnp.float32),...  9.68 us
  transfers between devices with their start and end apart: 7, of which 5 were waited for; matrix products, arithmetic and copies ran while one was open for 26% of the time, Pallas kernels for 0%

profile of v10, /device:TPU:1, one launch (start us, length us, event | category | flops | bytes accessed | tf_op | source)
XLA Modules:
  0.0 267.2 jit_solution(13179970343461170224)
XLA Ops:
  6.5 0.7 all-gather.3.cloned.1.call-update
  7.3 0.8 copy.24
  8.4 1.7 reduce-window.6
  11.5 3.4 %scatter_custom_fusion = s32[1152]{0:T(1024)S(1)} fusion(s32[768]{0:T(1024)S(1)} %fusion.82, s32[768]{0:T(1024)S(1)} %add_select_fusion, s32[]{:T(128)} %constant.13.clone.1), kind=kCustom, calls=%fused_computation.79 | custom fusion | bytes 4612 | tf_op jit(solution)/shard_map/scatter | solution.py:30
  14.9 51.1 %all-gather.3.cloned.1.call-done = bf16[2048,2048]{1,0:T(8,128)(2,1)} async-done(((bf16[64,2048]{1,0:T(8,128)(2,1)}), bf16[2048,2048]{1,0:T(8,128)(2,1)}) %all-gather.3.cloned.1.call-update) | async-done | bytes 8388624 | tf_op jit(solution)/shard_map/all_gather | solution.py:35
  66.1 5.0 %multiply_reduce_fusion = (f32[128]{0:T(128)S(1)}, f32[128,2048]{1,0:T(8,128)S(1)}) fusion(bf16[128,2048]{1,0:T(8,128)(2,1)} %param.12, bf16[2048,2048]{1,0:T(8,128)(2,1)} %all-gather.3.cloned.1.call-done, bf16[128,2048]{1,0:T(8,128)(2,1)} %param.13), kind=kOutput, calls=%fused_computation.41 | convolution fusion | flops 1075314560 | bytes 10486272 | tf_op jit(solution)/shard_map/dot_general | solution.py:33
  71.0 1.0 multiply_convert_fusion
  72.2 1.9 convolution_convert_fusion
  74.2 3.1 %copy.31 = bf16[32,20,2048]{2,1,0:T(8,128)(2,1)} copy(bf16[32,20,2048]{2,0,1:T(8,128)(2,1)S(1)} %convolution_convert_fusion) | data formatting | bytes 5242880 | tf_op jit(solution)/shard_map/convert_element_type | solution.py:54
  77.3 5.5 %all-to-all-start = ((bf16[32,20,2048]{2,1,0:T(8,128)(2,1)}), bf16[32,20,2048]{2,1,0:T(8,128)(2,1)}, u32[]{:S(2)}, u32[]{:S(2)}) async-start(bf16[32,20,2048]{2,1,0:T(8,128)(2,1)} %copy.31), calls=%async_computation | async-start | bytes 6291456 | tf_op jit(solution)/shard_map/all_to_all | solution.py:55
  83.1 39.5 %all-to-all-done = bf16[32,20,2048]{2,1,0:T(8,128)(2,1)} async-done(((bf16[32,20,2048]{2,1,0:T(8,128)(2,1)}), bf16[32,20,2048]{2,1,0:T(8,128)(2,1)}, u32[]{:S(2)}, u32[]{:S(2)}) %all-to-all-start) | async-done | bytes 2621472 | tf_op jit(solution)/shard_map/all_to_all | solution.py:55
  122.6 2.9 %fusion.86 = f32[512,352]{0,1:T(8,128)S(1)} fusion(bf16[512,2048]{1,0:T(8,128)(2,1)} %all-gather.5.cloned.1.call-done, bf16[2048,352]{0,1:T(8,128)(2,1)} %param.21), kind=kOutput, calls=%fused_computation.89 | convolution fusion | flops 738197504 | bytes 4259840 | tf_op jit(solution)/shard_map/dot_general | solution.py:84
  125.6 6.2 %fusion.54 = f32[512,2048]{1,0:T(8,128)} fusion(bf16[2048,352]{0,1:T(8,128)(2,1)S(1)} %copy-done, bf16[512,2048]{1,0:T(8,128)(2,1)} %all-gather.5.cloned.1.call-done, bf16[2048,352]{0,1:T(8,128)(2,1)} %param.22, f32[512,352]{0,1:T(8,128)S(1)} %fusion.86), kind=kOutput, calls=%fused_computation.39 | convolution fusion | flops 1477476352 | bytes 9895936 | tf_op jit(solution)/shard_map/dot_general | solution.py:87
  131.8 1.0 copy-done.2
  132.8 2.0 convolution_convert_fusion.1
  134.8 5.1 %all-to-all-start.2 = ((bf16[32,16,2048]{2,1,0:T(8,128)(2,1)}), bf16[32,16,2048]{2,1,0:T(8,128)(2,1)}, u32[]{:S(2)}, u32[]{:S(2)}) async-start(bf16[32,16,2048]{2,1,0:T(8,128)(2,1)} %convolution_convert_fusion.1), calls=%async_computation.2 | async-start | bytes 4194304 | tf_op jit(solution)/shard_map/all_to_all | solution.py:55
  139.9 8.4 %fusion.10 = f32[32,20,1408]{2,0,1:T(8,128)S(1)} fusion(bf16[1,2048,1408]{2,1,0:T(8,128)(2,1)} %param.18, bf16[32,20,2048]{2,1,0:T(8,128)(2,1)} %all-to-all-done), kind=kOutput, calls=%fused_computation.12 | convolution fusion | flops 3690987520 | bytes 11993088 | tf_op jit(solution)/shard_map/scd,df->scf/dot_general | solution.py:56
  148.3 8.6 %fusion.18 = bf16[32,20,1408]{2,0,1:T(8,128)(2,1)S(1)} fusion(bf16[1,2048,1408]{2,1,0:T(8,128)(2,1)} %param.19, f32[32,20,1408]{2,0,1:T(8,128)S(1)} %fusion.10, bf16[32,20,2048]{2,1,0:T(8,128)(2,1)} %all-to-all-done), kind=kOutput, calls=%fused_computation.16 | convolution fusion | flops 3696394240 | bytes 13795328 | tf_op jit(solution)/shard_map/scd,df->scf/dot_general | solution.py:57
  156.9 4.4 %fusion.21 = bf16[32,20,2048]{2,0,1:T(8,128)(2,1)S(1)} fusion(bf16[32,20,1408]{2,0,1:T(8,128)(2,1)S(1)} %fusion.18, bf16[1,1408,2048]{2,1,0:T(8,128)(2,1)S(1)} %bitcast.75), kind=kOutput, calls=%fused_computation.17 | convolution fusion | flops 3692298240 | bytes 10190848 | tf_op jit(solution)/shard_map/scf,fd->scd/dot_general | solution.py:59
  161.4 3.2 %copy.34 = bf16[32,20,2048]{2,1,0:T(8,128)(2,1)} copy(bf16[32,20,2048]{2,0,1:T(8,128)(2,1)S(1)} %fusion.21) | data formatting | bytes 5242880 | tf_op jit(solution)/shard_map/convert_element_type | solution.py:61
  164.5 3.7 %all-to-all-done.2 = bf16[32,16,2048]{2,1,0:T(8,128)(2,1)} async-done(((bf16[32,16,2048]{2,1,0:T(8,128)(2,1)}), bf16[32,16,2048]{2,1,0:T(8,128)(2,1)}, u32[]{:S(2)}, u32[]{:S(2)}) %all-to-all-start.2) | async-done | bytes 2097184 | tf_op jit(solution)/shard_map/all_to_all | solution.py:55
  168.2 5.3 %all-to-all-start.1 = ((bf16[32,20,2048]{2,1,0:T(8,128)(2,1)}), bf16[32,20,2048]{2,1,0:T(8,128)(2,1)}, u32[]{:S(2)}, u32[]{:S(2)}) async-start(bf16[32,20,2048]{2,1,0:T(8,128)(2,1)} %copy.34), calls=%async_computation.1 | async-start | bytes 6291456 | tf_op jit(solution)/shard_map/all_to_all | solution.py:65
  173.5 6.6 %fusion.8 = f32[32,16,1408]{2,1,0:T(8,128)S(1)} fusion(bf16[32,16,2048]{2,1,0:T(8,128)(2,1)} %all-to-all-done.2, bf16[1,2048,1408]{2,1,0:T(8,128)(2,1)} %param.18), kind=kOutput, calls=%fused_computation.10 | convolution fusion | flops 2952790016 | bytes 10747904 | tf_op jit(solution)/shard_map/scd,df->scf/dot_general | solution.py:56
  180.2 6.8 %fusion.24 = bf16[32,16,1408]{2,1,0:T(8,128)(2,1)S(1)} fusion(bf16[32,16,2048]{2,1,0:T(8,128)(2,1)} %all-to-all-done.2, bf16[1,2048,1408]{2,1,0:T(8,128)(2,1)} %param.19, f32[32,16,1408]{2,1,0:T(8,128)S(1)} %fusion.8), kind=kOutput, calls=%fused_computation.20 | convolution fusion | flops 2957115392 | bytes 12189696 | tf_op jit(solution)/shard_map/scd,df->scf/dot_general | solution.py:57
  187.0 4.6 %fusion.27 = bf16[32,16,2048]{2,0,1:T(8,128)(2,1)} fusion(bf16[1,1408,2048]{2,1,0:T(8,128)(2,1)S(1)} %bitcast.77, bf16[32,16,1408]{2,1,0:T(8,128)(2,1)S(1)} %fusion.24), kind=kOutput, calls=%fused_computation.21 | convolution fusion | flops 2953838592 | bytes 9306112 | tf_op jit(solution)/shard_map/scf,fd->scd/dot_general | solution.py:59
  191.6 21.8 %all-to-all-done.1 = bf16[32,20,2048]{2,1,0:T(8,128)(2,1)} async-done(((bf16[32,20,2048]{2,1,0:T(8,128)(2,1)}), bf16[32,20,2048]{2,1,0:T(8,128)(2,1)}, u32[]{:S(2)}, u32[]{:S(2)}) %all-to-all-start.1) | async-done | bytes 2621472 | tf_op jit(solution)/shard_map/all_to_all | solution.py:65
  213.4 4.1 %copy.38 = bf16[32,16,2048]{2,1,0:T(8,128)(2,1)} copy(bf16[32,16,2048]{2,0,1:T(8,128)(2,1)} %fusion.27) | data formatting | bytes 4194304 | tf_op jit(solution)/shard_map/optimization_barrier | solution.py:64
  217.6 5.1 %all-to-all-start.3 = ((bf16[32,16,2048]{2,1,0:T(8,128)(2,1)}), bf16[32,16,2048]{2,1,0:T(8,128)(2,1)}, u32[]{:S(2)}, u32[]{:S(2)}) async-start(bf16[32,16,2048]{2,1,0:T(8,128)(2,1)} %copy.38), calls=%async_computation.3 | async-start | bytes 4194304 | tf_op jit(solution)/shard_map/all_to_all | solution.py:65
  222.9 3.6 %scatter_custom_fusion.1 = f32[1152]{0:T(1024)S(1)} fusion(s32[768]{0:T(1024)S(1)} %fusion.82, f32[768]{0:T(1024)S(1)} %reshape.80, f32[]{:T(128)} %constant.36.clone.1), kind=kCustom, calls=%fused_computation.77 | custom fusion | bytes 4612 | tf_op jit(solution)/shard_map/scatter | solution.py:66
  227.3 23.6 %all-to-all-done.3 = bf16[32,16,2048]{2,1,0:T(8,128)(2,1)} async-done(((bf16[32,16,2048]{2,1,0:T(8,128)(2,1)}), bf16[32,16,2048]{2,1,0:T(8,128)(2,1)}, u32[]{:S(2)}, u32[]{:S(2)}) %all-to-all-start.3) | async-done | bytes 2097184 | tf_op jit(solution)/shard_map/all_to_all | solution.py:65
  251.0 3.9 %convolution_bitcast_fusion = f32[128,2048]{1,0:T(8,128)S(1)} fusion(bf16[32,16,2048]{2,1,0:T(8,128)(2,1)} %all-to-all-done.3, f32[32,36]{0,1:T(8,128)} %copy.29, s32[32,36]{0,1:T(8,128)} %copy-done.3), kind=kOutput, calls=%fused_computation.25 | convolution fusion | flops 1610907648 | bytes 3154944 | tf_op jit(solution)/shard_map/rec,ecd->rd/dot_general | solution.py:73
  254.9 5.8 %fusion.46 = bf16[128,2048]{1,0:T(8,128)(2,1)} fusion(f32[128,2048]{1,0:T(8,128)} %reduce-scatter.2.cloned.1.call-done, f32[128,2048]{1,0:T(8,128)S(1)} %get-tuple-element.14, f32[128,2048]{1,0:T(8,128)S(1)} %convolution_bitcast_fusion, bf16[32,20,2048]{2,1,0:T(8,128)(2,1)} %all-to-all-done.1, f32[32,36]{0,1:T(8,128)} %copy.29, s32[32,36]{0,1:T(8,128)} %copy-done.3), kind=kOutput, calls=%fused_computation.32 | convolution fusion | flops 2014609408 | bytes 6300672 | tf_op jit(solution)/shard_map/rec,ecd->rd/dot_general | solution.py:73
  (49 shorter events, 3.3 us)
Async XLA Ops:
  6.5 119.0 %copy-start = (bf16[2048,352]{0,1:T(8,128)(2,1)S(1)}, bf16[2048,352]{0,1:T(8,128)(2,1)}, u32[]{:S(2)}) copy-start(bf16[2048,352]{0,1:T(8,128)(2,1)} %param.23) | copy-start | bytes 4325380
  6.5 59.5 %all-gather.3.cloned.1.call-start = ((), (), s32[]{:S(2)}) async-start(), calls=%async_computation.5 | async-start | bytes 8650752 | tf_op jit(solution)/shard_map/all_gather | solution.py:35
  7.3 115.4 %all-gather.5.cloned.1.call-start = ((), (), s32[]{:S(2)}) async-start(), calls=%async_computation.6 | async-start | bytes 2621440 | tf_op jit(solution)/shard_map/all_gather | solution.py:83
  14.9 56.1 %copy-start.4 = (f32[2048]{0:T(1024)S(1)}, f32[2048]{0:T(1024)}, u32[]{:S(2)}) copy-start(f32[2048]{0:T(1024)} %param.15) | copy-start | bytes 24580
  72.2 10.6 %copy-start.3 = (s32[32,36]{0,1:T(8,128)}, s32[32,36]{0,1:T(8,128)S(1)}, u32[]{:S(2)}) copy-start(s32[32,36]{0,1:T(8,128)S(1)} %copy.27) | copy-start | bytes 13828
  77.3 45.4 %all-to-all-start = ((bf16[32,20,2048]{2,1,0:T(8,128)(2,1)}), bf16[32,20,2048]{2,1,0:T(8,128)(2,1)}, u32[]{:S(2)}, u32[]{:S(2)}) async-start(bf16[32,20,2048]{2,1,0:T(8,128)(2,1)} %copy.31), calls=%async_computation | async-start | bytes 6291456 | tf_op jit(solution)/shard_map/all_to_all | solution.py:55
  82.8 172.1 %reduce-scatter.2.cloned.1.call-start = ((), (), s32[]{:S(2)}) async-start(), calls=%async_computation.7 | async-start | bytes 5242880 | tf_op jit(solution)/shard_map/reduce_scatter | solution.py:90
  131.7 1.0 copy-start.2
  134.8 33.4 %all-to-all-start.2 = ((bf16[32,16,2048]{2,1,0:T(8,128)(2,1)}), bf16[32,16,2048]{2,1,0:T(8,128)(2,1)}, u32[]{:S(2)}, u32[]{:S(2)}) async-start(bf16[32,16,2048]{2,1,0:T(8,128)(2,1)} %convolution_convert_fusion.1), calls=%async_computation.2 | async-start | bytes 4194304 | tf_op jit(solution)/shard_map/all_to_all | solution.py:55
  139.9 17.0 %slice-start = ((s8[5767168]{0:T(1024)(128)(4,1)}), s8[4194304]{0:T(1024)(128)(4,1)S(1)}, s32[]{:S(2)}) async-start(s8[5767168]{0:T(1024)(128)(4,1)} %bitcast.74), calls=%async_computation.8 | async-start | bytes 8388608
  148.3 8.6 %slice-start.1 = ((s8[5767168]{0:T(1024)(128)(4,1)}), s8[1572864]{0:T(1024)(128)(4,1)S(1)}, s32[]{:S(2)}) async-start(s8[5767168]{0:T(1024)(128)(4,1)} %bitcast.74), calls=%async_computation.9 | async-start | bytes 3145728
  168.2 45.2 %all-to-all-start.1 = ((bf16[32,20,2048]{2,1,0:T(8,128)(2,1)}), bf16[32,20,2048]{2,1,0:T(8,128)(2,1)}, u32[]{:S(2)}, u32[]{:S(2)}) async-start(bf16[32,20,2048]{2,1,0:T(8,128)(2,1)} %copy.34), calls=%async_computation.1 | async-start | bytes 6291456 | tf_op jit(solution)/shard_map/all_to_all | solution.py:65
  173.5 13.5 %slice-start.2 = ((s8[5767168]{0:T(1024)(128)(4,1)}), s8[4194304]{0:T(1024)(128)(4,1)S(1)}, s32[]{:S(2)}) async-start(s8[5767168]{0:T(1024)(128)(4,1)} %bitcast.76), calls=%async_computation.10 | async-start | bytes 8388608
  180.1 6.9 %slice-start.3 = ((s8[5767168]{0:T(1024)(128)(4,1)}), s8[1572864]{0:T(1024)(128)(4,1)S(1)}, s32[]{:S(2)}) async-start(s8[5767168]{0:T(1024)(128)(4,1)} %bitcast.76), calls=%async_computation.11 | async-start | bytes 3145728
  217.6 5.1 %copy-start.5 = (f32[128,6]{0,1:T(8,128)S(1)}, f32[128,6]{0,1:T(8,128)}, u32[]{:S(2)}) copy-start(f32[128,6]{0,1:T(8,128)} %param.17) | copy-start | bytes 9220
  217.6 33.4 %all-to-all-start.3 = ((bf16[32,16,2048]{2,1,0:T(8,128)(2,1)}), bf16[32,16,2048]{2,1,0:T(8,128)(2,1)}, u32[]{:S(2)}, u32[]{:S(2)}) async-start(bf16[32,16,2048]{2,1,0:T(8,128)(2,1)} %copy.38), calls=%async_computation.3 | async-start | bytes 4194304 | tf_op jit(solution)/shard_map/all_to_all | solution.py:65
  251.0 9.7 %copy-start.1 = (bf16[2048,352]{0,1:T(8,128)(2,1)S(1)}, bf16[2048,352]{0,1:T(8,128)(2,1)}, u32[]{:S(2)}) copy-start(bf16[2048,352]{0,1:T(8,128)(2,1)} %param.23) | copy-start | bytes 4325380
Sparse Core Ops, SparseCore 0:
  9.6 56.3 all-gather.2
  72.1 30.2 all-gather.4
  131.9 45.7 reduce-scatter.1

commit v11 on v8

--- a/solution.py
+++ b/solution.py
@@ -73,7 +73,14 @@
         for lo, hi, part in zip(bounds[:-1], bounds[1:], returned)
     )
 
-    group_rows = lax.all_gather(normed, "req", axis=0, tiled=True)
+    req = lax.axis_size("req")
+    me = lax.axis_index("req")
+    shifted = [normed] + [
+        lax.ppermute(normed, "req", perm=[(i, (i + k) % req) for i in range(req)])
+        for k in range(1, req)
+    ]
+    order = (me - jnp.arange(req)) % req
+    group_rows = jnp.take(jnp.stack(shifted), order, axis=0).reshape(req * row_count, width)
     s_gate = jnp.dot(group_rows, shared_gate, preferred_element_type=jnp.float32)
     s_up = jnp.dot(group_rows, shared_up, preferred_element_type=jnp.float32)
     s_hidden = (jax.nn.silu(s_gate) * s_up).astype(jnp.bfloat16)

time: 251 us -> 254 us (1.012)
  waiting for transfers between devices: 123 us -> 114 us
  starting transfers between devices: 23.5 us -> 28.8 us
  local copies, waits for them, and re-layouts: 19.3 us -> 24.3 us
  other arithmetic: 3.8 us -> 8.09 us
  matrix products: 67.8 us -> 64.5 us
    all_gather x1 -> x0, waiting for transfers between devices: 17.3 us -> none  [body(): group_rows = lax.all_gather(normed, 'req', axis=0, tiled=True)]
    ppermute x0 -> x3, waiting for transfers between devices: none -> 8.16 us  [body(): lax.ppermute(normed, 'req', perm=[(i, (i + k) % req) for i in range(req)])]
    ppermute x0 -> x3, starting transfers between devices: none -> 5.63 us  [body(): lax.ppermute(normed, 'req', perm=[(i, (i + k) % req) for i in range(req)])]
    gather x0 -> x1, local copies, waits for them, and re-layouts: none -> 3.59 us  [body(): jnp.take(jnp.stack(shifted), order, axis=0).reshape(req * row_count, width)]
    another operation x2 -> x4, other arithmetic: 1.77 us -> 4.87 us  [the longest x2 3.1 us: body(): jnp.stack(shifted)]
  transfers between devices with their start and end apart: 7 -> 9, of which waited for: 5 -> 5; matrix products, arithmetic and copies ran while one was open for 32% -> 33% of each run, Pallas kernels for 0% -> 0%
where the time goes in v11:
time: 254 us; the launch traced here: 253 us
  waiting for transfers between devices  114 us (45%)
  matrix products  64.5 us (25%)
  starting transfers between devices  28.8 us (11%)
  local copies, waits for them, and re-layouts  24.3 us (10%)
  between operations  13.8 us (5%)
  other arithmetic  8.09 us (3%)
    all_gather x1, waiting for transfers between devices, body(): lax.all_gather(out_weight, 'exp', axis=0, tiled=True)  50.7 us
    all_to_all x2, waiting for transfers between devices, body(): lax.all_to_all(result, 'exp', split_axis=0, concat_axis=0, tiled=True)  34.5 us
    all_to_all x2, waiting for transfers between devices, body(): lax.all_to_all(outgoing, 'exp', split_axis=0, concat_axis=0, tiled=True)  19.7 us
    dot_general x2, matrix products, body(): jnp.einsum('scd,df->scf', joined, w_up, preferred_element_type=jnp.float32)  15.4 us
    dot_general x2, matrix products, body(): jnp.einsum('scd,df->scf', joined, w_gate, preferred_element_type=jnp.floa...  15.3 us
    all_to_all x2, starting transfers between devices, body(): lax.all_to_all(outgoing, 'exp', split_axis=0, concat_axis=0, tiled=True)  12.6 us
    all_to_all x2, starting transfers between devices, body(): lax.all_to_all(result, 'exp', split_axis=0, concat_axis=0, tiled=True)  10.3 us
    dot_general x2, matrix products, body(): jnp.einsum('rec,ecd->rd', combine[:, :, lo:hi], part.astype(jnp.float32),...  9.68 us
  transfers between devices with their start and end apart: 9, of which 5 were waited for; matrix products, arithmetic and copies ran while one was open for 33% of the time, Pallas kernels for 0%

profile of v11, /device:TPU:1, one launch (start us, length us, event | category | flops | bytes accessed | tf_op | source)
XLA Modules:
  0.0 253.2 jit_solution(11187236703615669510)
XLA Ops:
  9.3 1.7 reduce-window.6
  11.5 3.4 %scatter_custom_fusion = s32[1152]{0:T(1024)S(1)} fusion(s32[768]{0:T(1024)S(1)} %fusion.83, s32[768]{0:T(1024)S(1)} %add_select_fusion, s32[]{:T(128)} %constant.59.clone.1), kind=kCustom, calls=%fused_computation.83 | custom fusion | bytes 4612 | tf_op jit(solution)/shard_map/scatter | solution.py:30
  15.4 50.7 %all-gather.2.cloned.1.call-done = bf16[2048,2048]{1,0:T(8,128)(2,1)} async-done(((bf16[64,2048]{1,0:T(8,128)(2,1)}), bf16[2048,2048]{1,0:T(8,128)(2,1)}) %all-gather.2.cloned.1.call-update) | async-done | bytes 8388624 | tf_op jit(solution)/shard_map/all_gather | solution.py:35
  66.1 5.0 %multiply_reduce_fusion = (f32[128]{0:T(128)S(1)}, f32[128,2048]{1,0:T(8,128)S(1)}) fusion(bf16[128,2048]{1,0:T(8,128)(2,1)} %param.12, bf16[2048,2048]{1,0:T(8,128)(2,1)} %all-gather.2.cloned.1.call-done, bf16[128,2048]{1,0:T(8,128)(2,1)} %param.13), kind=kOutput, calls=%fused_computation.44 | convolution fusion | flops 1075314560 | bytes 10486272 | tf_op jit(solution)/shard_map/dot_general | solution.py:33
  71.2 3.0 %collective-permute-start.1 = (bf16[128,2048]{1,0:T(8,128)(2,1)S(1)}, bf16[128,2048]{1,0:T(8,128)(2,1)}, u32[]{:S(2)}, u32[]{:S(2)}) collective-permute-start(bf16[128,2048]{1,0:T(8,128)(2,1)S(1)} %multiply_convert_fusion), channel_id=1, source_target_pairs={{0,64},{32,96},{64,0},{96,32},{1,65},{33,97},{65,1},{97,33},{2,66}... | collective-permute-start | bytes 1572872 | tf_op jit(solution)/shard_map/ppermute | solution.py:79
  74.5 2.3 collective-permute-start.2
  76.8 2.1 convolution_convert_fusion.1
  78.9 6.5 %all-to-all-start = ((bf16[32,16,2048]{2,1,0:T(8,128)(2,1)}), bf16[32,16,2048]{2,1,0:T(8,128)(2,1)}, u32[]{:S(2)}, u32[]{:S(2)}) async-start(bf16[32,16,2048]{2,1,0:T(8,128)(2,1)} %convolution_convert_fusion.1), calls=%async_computation | async-start | bytes 4194304 | tf_op jit(solution)/shard_map/all_to_all | solution.py:51
  86.5 3.1 %copy.34 = bf16[32,20,2048]{2,1,0:T(8,128)(2,1)} copy(bf16[32,20,2048]{2,0,1:T(8,128)(2,1)S(1)} %convolution_convert_fusion) | data formatting | bytes 5242880 | tf_op jit(solution)/shard_map/convert_element_type | solution.py:50
  89.8 8.2 %collective-permute-done = bf16[128,2048]{1,0:T(8,128)(2,1)} collective-permute-done((bf16[128,2048]{1,0:T(8,128)(2,1)S(1)}, bf16[128,2048]{1,0:T(8,128)(2,1)}, u32[]{:S(2)}, u32[]{:S(2)}) %collective-permute-start) | collective-permute-done | bytes 524320 | tf_op jit(solution)/shard_map/ppermute | solution.py:79
  98.0 3.0 %pad_maximum_fusion = bf16[4,128,2048]{2,1,0:T(8,128)(2,1)} fusion(bf16[1,128,2048]{2,1,0:T(8,128)(2,1)} %bitcast.14, bf16[1,128,2048]{2,1,0:T(8,128)(2,1)} %bitcast.13, bf16[1,128,2048]{2,1,0:T(8,128)(2,1)} %bitcast.12, bf16[1,128,2048]{2,1,0:T(8,128)(2,1)S(1)} %fusion.101), kind=kLoop, calls=%fused_computation.34 | loop fusion | flops 3145728 | bytes 4194304 | tf_op jit(solution)/shard_map/stack | solution.py:83
  100.9 3.6 %gather_fusion = bf16[4,128,2048]{2,1,0:T(8,128)(2,1)} fusion(bf16[4,128,2048]{2,1,0:T(8,128)(2,1)} %pad_maximum_fusion, s32[1024]{0:T(1024)S(1)} %pad_clamp_fusion), kind=kCustom, calls=%fused_computation | custom fusion | bytes 4194320 | tf_op jit(solution)/shard_map/jit(_take)/gather | solution.py:83
  104.5 2.0 bitcast_select_fusion
  107.8 1.8 fusion.90
  109.6 6.3 %fusion.54 = f32[512,2048]{1,0:T(8,128)} fusion(bf16[2048,352]{0,1:T(8,128)(2,1)S(1)} %copy-done, bf16[512,2048]{1,0:T(8,128)(2,1)} %copy-done.2, bf16[2048,352]{0,1:T(8,128)(2,1)} %param.22, f32[512,352]{0,1:T(8,128)} %fusion.90), kind=kOutput, calls=%fused_computation.42 | convolution fusion | flops 1477476352 | bytes 9895936 | tf_op jit(solution)/shard_map/dot_general | solution.py:87
  116.0 6.1 %all-to-all-start.2 = ((bf16[32,20,2048]{2,1,0:T(8,128)(2,1)}), bf16[32,20,2048]{2,1,0:T(8,128)(2,1)}, u32[]{:S(2)}, u32[]{:S(2)}) async-start(bf16[32,20,2048]{2,1,0:T(8,128)(2,1)} %copy.34), calls=%async_computation.2 | async-start | bytes 6291456 | tf_op jit(solution)/shard_map/all_to_all | solution.py:51
  122.1 7.0 %fusion.10 = f32[32,16,1408]{2,1,0:T(8,128)S(1)} fusion(bf16[32,16,2048]{2,1,0:T(8,128)(2,1)} %all-to-all-done, bf16[1,2048,1408]{2,1,0:T(8,128)(2,1)} %param.18), kind=kOutput, calls=%fused_computation.13 | convolution fusion | flops 2952790016 | bytes 10747904 | tf_op jit(solution)/shard_map/scd,df->scf/dot_general | solution.py:52
  129.2 6.9 %fusion.24 = bf16[32,16,1408]{2,1,0:T(8,128)(2,1)S(1)} fusion(bf16[32,16,2048]{2,1,0:T(8,128)(2,1)} %all-to-all-done, bf16[1,2048,1408]{2,1,0:T(8,128)(2,1)} %param.19, f32[32,16,1408]{2,1,0:T(8,128)S(1)} %fusion.10), kind=kOutput, calls=%fused_computation.20 | convolution fusion | flops 2957115392 | bytes 12189696 | tf_op jit(solution)/shard_map/scd,df->scf/dot_general | solution.py:53
  136.1 3.6 %fusion.27 = bf16[32,16,2048]{2,0,1:T(8,128)(2,1)S(1)} fusion(bf16[1,1408,2048]{2,1,0:T(8,128)(2,1)S(1)} %bitcast.88, bf16[32,16,1408]{2,1,0:T(8,128)(2,1)S(1)} %fusion.24), kind=kOutput, calls=%fused_computation.22 | convolution fusion | flops 2953838592 | bytes 9306112 | tf_op jit(solution)/shard_map/scf,fd->scd/dot_general | solution.py:55
  139.7 2.5 copy.31
  142.2 19.7 %all-to-all-done.2 = bf16[32,20,2048]{2,1,0:T(8,128)(2,1)} async-done(((bf16[32,20,2048]{2,1,0:T(8,128)(2,1)}), bf16[32,20,2048]{2,1,0:T(8,128)(2,1)}, u32[]{:S(2)}, u32[]{:S(2)}) %all-to-all-start.2) | async-done | bytes 2621472 | tf_op jit(solution)/shard_map/all_to_all | solution.py:51
  161.9 5.1 %all-to-all-start.1 = ((bf16[32,16,2048]{2,1,0:T(8,128)(2,1)}), bf16[32,16,2048]{2,1,0:T(8,128)(2,1)}, u32[]{:S(2)}, u32[]{:S(2)}) async-start(bf16[32,16,2048]{2,1,0:T(8,128)(2,1)} %copy.31), calls=%async_computation.1 | async-start | bytes 4194304 | tf_op jit(solution)/shard_map/all_to_all | solution.py:58
  167.0 8.3 %fusion.8 = f32[32,20,1408]{2,0,1:T(8,128)S(1)} fusion(bf16[1,2048,1408]{2,1,0:T(8,128)(2,1)} %param.18, bf16[32,20,2048]{2,1,0:T(8,128)(2,1)} %all-to-all-done.2), kind=kOutput, calls=%fused_computation.11 | convolution fusion | flops 3690987520 | bytes 11993088 | tf_op jit(solution)/shard_map/scd,df->scf/dot_general | solution.py:52
  175.3 8.5 %fusion.18 = bf16[32,20,1408]{2,0,1:T(8,128)(2,1)S(1)} fusion(bf16[1,2048,1408]{2,1,0:T(8,128)(2,1)} %param.19, f32[32,20,1408]{2,0,1:T(8,128)S(1)} %fusion.8, bf16[32,20,2048]{2,1,0:T(8,128)(2,1)} %all-to-all-done.2), kind=kOutput, calls=%fused_computation.17 | convolution fusion | flops 3696394240 | bytes 13795328 | tf_op jit(solution)/shard_map/scd,df->scf/dot_general | solution.py:53
  183.8 4.4 %fusion.21 = bf16[32,20,2048]{2,0,1:T(8,128)(2,1)S(1)} fusion(bf16[32,20,1408]{2,0,1:T(8,128)(2,1)S(1)} %fusion.18, bf16[1,1408,2048]{2,1,0:T(8,128)(2,1)S(1)} %bitcast.90), kind=kOutput, calls=%fused_computation.18 | convolution fusion | flops 3692298240 | bytes 10190848 | tf_op jit(solution)/shard_map/scf,fd->scd/dot_general | solution.py:55
  188.2 3.2 %copy.37 = bf16[32,20,2048]{2,1,0:T(8,128)(2,1)} copy(bf16[32,20,2048]{2,0,1:T(8,128)(2,1)S(1)} %fusion.21) | data formatting | bytes 5242880 | tf_op jit(solution)/shard_map/convert_element_type | solution.py:57
  191.4 3.9 %all-to-all-done.1 = bf16[32,16,2048]{2,1,0:T(8,128)(2,1)} async-done(((bf16[32,16,2048]{2,1,0:T(8,128)(2,1)}), bf16[32,16,2048]{2,1,0:T(8,128)(2,1)}, u32[]{:S(2)}, u32[]{:S(2)}) %all-to-all-start.1) | async-done | bytes 2097184 | tf_op jit(solution)/shard_map/all_to_all | solution.py:58
  195.3 5.3 %all-to-all-start.3 = ((bf16[32,20,2048]{2,1,0:T(8,128)(2,1)}), bf16[32,20,2048]{2,1,0:T(8,128)(2,1)}, u32[]{:S(2)}, u32[]{:S(2)}) async-start(bf16[32,20,2048]{2,1,0:T(8,128)(2,1)} %copy.37), calls=%async_computation.3 | async-start | bytes 6291456 | tf_op jit(solution)/shard_map/all_to_all | solution.py:58
  201.5 3.7 %scatter_custom_fusion.1 = f32[1152]{0:T(1024)S(1)} fusion(s32[768]{0:T(1024)S(1)} %fusion.83, f32[768]{0:T(1024)S(1)} %reshape.145, f32[]{:T(128)} %constant.66.clone.1), kind=kCustom, calls=%fused_computation.81 | custom fusion | bytes 4612 | tf_op jit(solution)/shard_map/scatter | solution.py:59
  206.0 3.9 %convolution_bitcast_fusion = f32[128,2048]{1,0:T(8,128)S(1)} fusion(bf16[32,16,2048]{2,1,0:T(8,128)(2,1)} %all-to-all-done.1, f32[32,36]{0,1:T(8,128)} %copy.29, s32[32,36]{0,1:T(8,128)} %copy.27), kind=kOutput, calls=%fused_computation.26 | convolution fusion | flops 1610907648 | bytes 3154944 | tf_op jit(solution)/shard_map/rec,ecd->rd/dot_general | solution.py:66
  209.9 30.6 %all-to-all-done.3 = bf16[32,20,2048]{2,1,0:T(8,128)(2,1)} async-done(((bf16[32,20,2048]{2,1,0:T(8,128)(2,1)}), bf16[32,20,2048]{2,1,0:T(8,128)(2,1)}, u32[]{:S(2)}, u32[]{:S(2)}) %all-to-all-start.3) | async-done | bytes 2621472 | tf_op jit(solution)/shard_map/all_to_all | solution.py:58
  240.5 5.8 %fusion.46 = bf16[128,2048]{1,0:T(8,128)(2,1)} fusion(f32[128,2048]{1,0:T(8,128)} %reduce-scatter.2.cloned.1.call-done, f32[128,2048]{1,0:T(8,128)S(1)} %get-tuple-element.10, f32[128,2048]{1,0:T(8,128)S(1)} %convolution_bitcast_fusion, bf16[32,20,2048]{2,1,0:T(8,128)(2,1)} %all-to-all-done.3, f32[32,36]{0,1:T(8,128)} %copy.29, s32[32,36]{0,1:T(8,128)} %copy.27), kind=kOutput, calls=%fused_computation.33 | convolution fusion | flops 2014609408 | bytes 6300672 | tf_op jit(solution)/shard_map/rec,ecd->rd/dot_general | solution.py:66
  (63 shorter events, 8.4 us)
Async XLA Ops:
  6.5 103.1 %copy-start = (bf16[2048,352]{0,1:T(8,128)(2,1)S(1)}, bf16[2048,352]{0,1:T(8,128)(2,1)}, u32[]{:S(2)}) copy-start(bf16[2048,352]{0,1:T(8,128)(2,1)} %param.23) | copy-start | bytes 4325380
  6.5 59.5 %all-gather.2.cloned.1.call-start = ((), (), s32[]{:S(2)}) async-start(), calls=%async_computation.5 | async-start | bytes 8650752 | tf_op jit(solution)/shard_map/all_gather | solution.py:35
  15.2 61.6 %copy-start.3 = (pred[32,36,128]{2,1,0:T(8,128)(4,1)}, pred[32,36,128]{2,1,0:T(8,128)(4,1)S(1)}, u32[]{:S(2)}) copy-start(pred[32,36,128]{2,1,0:T(8,128)(4,1)S(1)} %iota_compare_fusion) | copy-start | bytes 442372
  15.4 55.7 %copy-start.4 = (f32[2048]{0:T(1024)S(1)}, f32[2048]{0:T(1024)}, u32[]{:S(2)}) copy-start(f32[2048]{0:T(1024)} %param.15) | copy-start | bytes 24580
  71.2 18.6 %collective-permute-start.1 = (bf16[128,2048]{1,0:T(8,128)(2,1)S(1)}, bf16[128,2048]{1,0:T(8,128)(2,1)}, u32[]{:S(2)}, u32[]{:S(2)}) collective-permute-start(bf16[128,2048]{1,0:T(8,128)(2,1)S(1)} %multiply_convert_fusion), channel_id=1, source_target_pairs={{0,64},{32,96},{64,0},{96,32},{1,65},{33,97},{65,1},{97,33},{2,66}... | collective-permute-start | bytes 1572872 | tf_op jit(solution)/shard_map/ppermute | solution.py:79
  74.2 23.8 %collective-permute-start = (bf16[128,2048]{1,0:T(8,128)(2,1)S(1)}, bf16[128,2048]{1,0:T(8,128)(2,1)}, u32[]{:S(2)}, u32[]{:S(2)}) collective-permute-start(bf16[128,2048]{1,0:T(8,128)(2,1)S(1)} %multiply_convert_fusion), channel_id=1, source_target_pairs={{0,32},{32,64},{64,96},{96,0},{1,33},{33,65},{65,97},{97,1},{2,34}... | collective-permute-start | bytes 1572872 | tf_op jit(solution)/shard_map/ppermute | solution.py:79
  74.5 23.5 %collective-permute-start.2 = (bf16[128,2048]{1,0:T(8,128)(2,1)S(1)}, bf16[128,2048]{1,0:T(8,128)(2,1)}, u32[]{:S(2)}, u32[]{:S(2)}) collective-permute-start(bf16[128,2048]{1,0:T(8,128)(2,1)S(1)} %multiply_convert_fusion), channel_id=1, source_target_pairs={{0,96},{32,0},{64,32},{96,64},{1,97},{33,1},{65,33},{97,65},{2,98}... | collective-permute-start | bytes 1572872 | tf_op jit(solution)/shard_map/ppermute | solution.py:79
  78.9 6.7 %slice-start = ((pred[32,36,128]{2,1,0:T(8,128)(4,1)}), pred[32,20,128]{2,1,0:T(8,128)(4,1)S(1)}, s32[]{:S(2)}) async-start(pred[32,36,128]{2,1,0:T(8,128)(4,1)} %copy-done.3), calls=%async_computation.7 | async-start | bytes 196608 | tf_op jit(solution)/shard_map/slice | solution.py:49
  78.9 37.0 %all-to-all-start = ((bf16[32,16,2048]{2,1,0:T(8,128)(2,1)}), bf16[32,16,2048]{2,1,0:T(8,128)(2,1)}, u32[]{:S(2)}, u32[]{:S(2)}) async-start(bf16[32,16,2048]{2,1,0:T(8,128)(2,1)} %convolution_convert_fusion.1), calls=%async_computation | async-start | bytes 4194304 | tf_op jit(solution)/shard_map/all_to_all | solution.py:51
  85.4 155.1 %reduce-scatter.2.cloned.1.call-start = ((), (), s32[]{:S(2)}) async-start(), calls=%async_computation.6 | async-start | bytes 5242880 | tf_op jit(solution)/shard_map/reduce_scatter | solution.py:90
  104.5 3.3 %copy-start.6 = (bf16[2048,352]{0,1:T(8,128)(2,1)S(1)}, bf16[2048,352]{0,1:T(8,128)(2,1)}, u32[]{:S(2)}) copy-start(bf16[2048,352]{0,1:T(8,128)(2,1)} %param.21) | copy-start | bytes 4325380
  106.5 1.3 copy-start.2
  116.0 45.9 %all-to-all-start.2 = ((bf16[32,20,2048]{2,1,0:T(8,128)(2,1)}), bf16[32,20,2048]{2,1,0:T(8,128)(2,1)}, u32[]{:S(2)}, u32[]{:S(2)}) async-start(bf16[32,20,2048]{2,1,0:T(8,128)(2,1)} %copy.34), calls=%async_computation.2 | async-start | bytes 6291456 | tf_op jit(solution)/shard_map/all_to_all | solution.py:51
  122.1 14.0 %slice-start.1 = ((s8[5767168]{0:T(1024)(128)(4,1)}), s8[4194304]{0:T(1024)(128)(4,1)S(1)}, s32[]{:S(2)}) async-start(s8[5767168]{0:T(1024)(128)(4,1)} %bitcast.87), calls=%async_computation.8 | async-start | bytes 8388608
  129.1 7.0 %slice-start.2 = ((s8[5767168]{0:T(1024)(128)(4,1)}), s8[1572864]{0:T(1024)(128)(4,1)S(1)}, s32[]{:S(2)}) async-start(s8[5767168]{0:T(1024)(128)(4,1)} %bitcast.87), calls=%async_computation.9 | async-start | bytes 3145728
  161.9 33.4 %all-to-all-start.1 = ((bf16[32,16,2048]{2,1,0:T(8,128)(2,1)}), bf16[32,16,2048]{2,1,0:T(8,128)(2,1)}, u32[]{:S(2)}, u32[]{:S(2)}) async-start(bf16[32,16,2048]{2,1,0:T(8,128)(2,1)} %copy.31), calls=%async_computation.1 | async-start | bytes 4194304 | tf_op jit(solution)/shard_map/all_to_all | solution.py:58
  167.0 16.8 %slice-start.3 = ((s8[5767168]{0:T(1024)(128)(4,1)}), s8[4194304]{0:T(1024)(128)(4,1)S(1)}, s32[]{:S(2)}) async-start(s8[5767168]{0:T(1024)(128)(4,1)} %bitcast.89), calls=%async_computation.10 | async-start | bytes 8388608
  175.2 8.5 %slice-start.4 = ((s8[5767168]{0:T(1024)(128)(4,1)}), s8[1572864]{0:T(1024)(128)(4,1)S(1)}, s32[]{:S(2)}) async-start(s8[5767168]{0:T(1024)(128)(4,1)} %bitcast.89), calls=%async_computation.11 | async-start | bytes 3145728
  191.4 9.9 %copy-start.5 = (f32[128,6]{0,1:T(8,128)S(1)}, f32[128,6]{0,1:T(8,128)}, u32[]{:S(2)}) copy-start(f32[128,6]{0,1:T(8,128)} %param.17) | copy-start | bytes 9220
  195.3 45.2 %all-to-all-start.3 = ((bf16[32,20,2048]{2,1,0:T(8,128)(2,1)}), bf16[32,20,2048]{2,1,0:T(8,128)(2,1)}, u32[]{:S(2)}, u32[]{:S(2)}) async-start(bf16[32,20,2048]{2,1,0:T(8,128)(2,1)} %copy.37), calls=%async_computation.3 | async-start | bytes 6291456 | tf_op jit(solution)/shard_map/all_to_all | solution.py:58
  206.0 40.3 %copy-start.1 = (bf16[2048,352]{0,1:T(8,128)(2,1)S(1)}, bf16[2048,352]{0,1:T(8,128)(2,1)}, u32[]{:S(2)}) copy-start(bf16[2048,352]{0,1:T(8,128)(2,1)} %param.23) | copy-start | bytes 4325380
Sparse Core Ops, SparseCore 0:
  9.6 56.3 all-gather.1
  116.1 46.3 reduce-scatter.1

commit v12 on v8

--- a/solution.py
+++ b/solution.py
@@ -62,7 +62,7 @@
         slot_weight.reshape(experts, capacity)[None, :, :],
         0.0,
     )
-    routed = sum(
+    routed_parts = [
         jnp.einsum(
             "rec,ecd->rd",
             combine[:, :, lo:hi],
@@ -71,7 +71,7 @@
             preferred_element_type=jnp.float32,
         )
         for lo, hi, part in zip(bounds[:-1], bounds[1:], returned)
-    )
+    ]
 
     group_rows = lax.all_gather(normed, "req", axis=0, tiled=True)
     s_gate = jnp.dot(group_rows, shared_gate, preferred_element_type=jnp.float32)
@@ -81,7 +81,8 @@
         s_hidden, shared_down, (((1,), (1,)), ((), ())), preferred_element_type=jnp.float32
     )
     shared = lax.psum_scatter(s_partial, "req", scatter_dimension=0, tiled=True)
-    return (stream_f + routed + shared).astype(jnp.bfloat16)
+    ready = lax.optimization_barrier(stream_f + shared + sum(routed_parts[:-1]))
+    return (ready + routed_parts[-1]).astype(jnp.bfloat16)
 
 
 def solution(mesh):

time: 251 us -> 255 us (1.016)
  waiting for transfers between devices: 123 us -> 128 us
    all_gather x1, waiting for transfers between devices: 17.3 us -> 21.4 us  [body(): group_rows = lax.all_gather(normed, 'req', axis=0, tiled=True)]
  transfers between devices with their start and end apart: 7 -> 7, of which waited for: 5 -> 5; matrix products, arithmetic and copies ran while one was open for 32% -> 30% of each run, Pallas kernels for 0% -> 0%
where the time goes in v12:
time: 255 us
  waiting for transfers between devices  128 us (50%)
  matrix products  65.9 us (26%)
  starting transfers between devices  23.5 us (9%)
  local copies, waits for them, and re-layouts  20.3 us (8%)
  between operations  13.4 us (5%)
  other arithmetic  3.8 us (1%)
    all_gather x1, waiting for transfers between devices, body(): lax.all_gather(out_weight, 'exp', axis=0, tiled=True)  51.1 us
    all_to_all x2, waiting for transfers between devices, body(): lax.all_to_all(result, 'exp', split_axis=0, concat_axis=0, tiled=True)  34.4 us
    all_gather x1, waiting for transfers between devices, body(): group_rows = lax.all_gather(normed, 'req', axis=0, tiled=True)  21.4 us
    all_to_all x2, waiting for transfers between devices, body(): lax.all_to_all(outgoing, 'exp', split_axis=0, concat_axis=0, tiled=True)  20.2 us
    dot_general x2, matrix products, body(): jnp.einsum('scd,df->scf', joined, w_up, preferred_element_type=jnp.float32)  15.4 us
    dot_general x2, matrix products, body(): jnp.einsum('scd,df->scf', joined, w_gate, preferred_element_type=jnp.floa...  14.8 us
    all_to_all x2, starting transfers between devices, body(): lax.all_to_all(outgoing, 'exp', split_axis=0, concat_axis=0, tiled=True)  13.1 us
    all_to_all x2, starting transfers between devices, body(): lax.all_to_all(result, 'exp', split_axis=0, concat_axis=0, tiled=True)  10.3 us
  transfers between devices with their start and end apart: 7, of which 5 were waited for; matrix products, arithmetic and copies ran while one was open for 30% of the time, Pallas kernels for 0%

profile of v12, /device:TPU:1, one launch (start us, length us, event | category | flops | bytes accessed | tf_op | source)
XLA Modules:
  0.0 254.7 jit_solution(1136896516446890490)
XLA Ops:
  6.5 0.7 all-gather.3.cloned.1.call-update
  7.3 0.8 copy.24
  8.4 1.7 reduce-window.6
  11.5 3.4 %scatter_custom_fusion = s32[1152]{0:T(1024)S(1)} fusion(s32[768]{0:T(1024)S(1)} %fusion.78, s32[768]{0:T(1024)S(1)} %add_select_fusion, s32[]{:T(128)} %constant.13.clone.1), kind=kCustom, calls=%fused_computation.78 | custom fusion | bytes 4612 | tf_op jit(solution)/shard_map/scatter | solution.py:30
  14.9 51.1 %all-gather.3.cloned.1.call-done = bf16[2048,2048]{1,0:T(8,128)(2,1)} async-done(((bf16[64,2048]{1,0:T(8,128)(2,1)}), bf16[2048,2048]{1,0:T(8,128)(2,1)}) %all-gather.3.cloned.1.call-update) | async-done | bytes 8388624 | tf_op jit(solution)/shard_map/all_gather | solution.py:35
  66.1 5.0 %multiply_reduce_fusion = (f32[128]{0:T(128)S(1)}, f32[128,2048]{1,0:T(8,128)S(1)}) fusion(bf16[128,2048]{1,0:T(8,128)(2,1)} %param.12, bf16[2048,2048]{1,0:T(8,128)(2,1)} %all-gather.3.cloned.1.call-done, bf16[128,2048]{1,0:T(8,128)(2,1)} %param.13), kind=kOutput, calls=%fused_computation.40 | convolution fusion | flops 1075314560 | bytes 10486272 | tf_op jit(solution)/shard_map/dot_general | solution.py:33
  71.0 1.0 multiply_convert_fusion
  72.4 3.1 %convolution_convert_fusion.1 = bf16[32,16,2048]{2,1,0:T(8,128)(2,1)} fusion(bf16[128,2048]{1,0:T(8,128)(2,1)} %multiply_convert_fusion, pred[32,36,128]{2,1,0:T(8,128)(4,1)S(1)} %iota_compare_fusion), kind=kOutput, calls=%fused_computation.20 | convolution fusion | flops 269484032 | bytes 2686976 | tf_op jit(solution)/shard_map/ecr,rd->ecd/dot_general | solution.py:48
  75.5 5.5 %all-to-all-start = ((bf16[32,16,2048]{2,1,0:T(8,128)(2,1)}), bf16[32,16,2048]{2,1,0:T(8,128)(2,1)}, u32[]{:S(2)}, u32[]{:S(2)}) async-start(bf16[32,16,2048]{2,1,0:T(8,128)(2,1)} %convolution_convert_fusion.1), calls=%async_computation.1 | async-start | bytes 4194304 | tf_op jit(solution)/shard_map/all_to_all | solution.py:51
  81.1 21.4 %all-gather.5.cloned.1.call-done = bf16[512,2048]{1,0:T(8,128)(2,1)} async-done(((bf16[128,2048]{1,0:T(8,128)(2,1)}), bf16[512,2048]{1,0:T(8,128)(2,1)}) %all-gather.5.cloned.1.call-update) | async-done | bytes 2097168 | tf_op jit(solution)/shard_map/all_gather | solution.py:76
  102.4 2.9 %fusion.82 = f32[512,352]{0,1:T(8,128)S(1)} fusion(bf16[512,2048]{1,0:T(8,128)(2,1)} %all-gather.5.cloned.1.call-done, bf16[2048,352]{0,1:T(8,128)(2,1)} %param.21), kind=kOutput, calls=%fused_computation.88 | convolution fusion | flops 738197504 | bytes 4259840 | tf_op jit(solution)/shard_map/dot_general | solution.py:77
  105.4 6.2 %fusion.49 = f32[512,2048]{1,0:T(8,128)} fusion(bf16[2048,352]{0,1:T(8,128)(2,1)S(1)} %copy-done, bf16[512,2048]{1,0:T(8,128)(2,1)} %all-gather.5.cloned.1.call-done, bf16[2048,352]{0,1:T(8,128)(2,1)} %param.22, f32[512,352]{0,1:T(8,128)S(1)} %fusion.82), kind=kOutput, calls=%fused_computation.38 | convolution fusion | flops 1477476352 | bytes 9895936 | tf_op jit(solution)/shard_map/dot_general | solution.py:80
  111.6 1.0 copy-done.2
  112.6 0.8 convolution_convert_fusion
  113.5 3.2 %copy.34 = bf16[32,20,2048]{2,1,0:T(8,128)(2,1)} copy(bf16[32,20,2048]{2,0,1:T(8,128)(2,1)S(1)} %convolution_convert_fusion) | data formatting | bytes 5242880 | tf_op jit(solution)/shard_map/convert_element_type | solution.py:50
  116.6 7.6 %all-to-all-start.2 = ((bf16[32,20,2048]{2,1,0:T(8,128)(2,1)}), bf16[32,20,2048]{2,1,0:T(8,128)(2,1)}, u32[]{:S(2)}, u32[]{:S(2)}) async-start(bf16[32,20,2048]{2,1,0:T(8,128)(2,1)} %copy.34), calls=%async_computation.3 | async-start | bytes 6291456 | tf_op jit(solution)/shard_map/all_to_all | solution.py:51
  124.3 6.5 %fusion.10 = f32[32,16,1408]{2,1,0:T(8,128)S(1)} fusion(bf16[32,16,2048]{2,1,0:T(8,128)(2,1)} %all-to-all-done, bf16[1,2048,1408]{2,1,0:T(8,128)(2,1)} %param.18), kind=kOutput, calls=%fused_computation.12 | convolution fusion | flops 2952790016 | bytes 10747904 | tf_op jit(solution)/shard_map/scd,df->scf/dot_general | solution.py:52
  130.8 6.9 %fusion.24 = bf16[32,16,1408]{2,1,0:T(8,128)(2,1)S(1)} fusion(bf16[32,16,2048]{2,1,0:T(8,128)(2,1)} %all-to-all-done, bf16[1,2048,1408]{2,1,0:T(8,128)(2,1)} %param.19, f32[32,16,1408]{2,1,0:T(8,128)S(1)} %fusion.10), kind=kOutput, calls=%fused_computation.19 | convolution fusion | flops 2957115392 | bytes 12189696 | tf_op jit(solution)/shard_map/scd,df->scf/dot_general | solution.py:53
  137.8 3.6 %fusion.27 = bf16[32,16,2048]{2,0,1:T(8,128)(2,1)S(1)} fusion(bf16[1,1408,2048]{2,1,0:T(8,128)(2,1)S(1)} %bitcast.73, bf16[32,16,1408]{2,1,0:T(8,128)(2,1)S(1)} %fusion.24), kind=kOutput, calls=%fused_computation.21 | convolution fusion | flops 2953838592 | bytes 9306112 | tf_op jit(solution)/shard_map/scf,fd->scd/dot_general | solution.py:55
  141.4 2.5 copy.31
  143.9 20.2 %all-to-all-done.2 = bf16[32,20,2048]{2,1,0:T(8,128)(2,1)} async-done(((bf16[32,20,2048]{2,1,0:T(8,128)(2,1)}), bf16[32,20,2048]{2,1,0:T(8,128)(2,1)}, u32[]{:S(2)}, u32[]{:S(2)}) %all-to-all-start.2) | async-done | bytes 2621472 | tf_op jit(solution)/shard_map/all_to_all | solution.py:51
  164.1 5.1 %all-to-all-start.1 = ((bf16[32,16,2048]{2,1,0:T(8,128)(2,1)}), bf16[32,16,2048]{2,1,0:T(8,128)(2,1)}, u32[]{:S(2)}, u32[]{:S(2)}) async-start(bf16[32,16,2048]{2,1,0:T(8,128)(2,1)} %copy.31), calls=%async_computation.2 | async-start | bytes 4194304 | tf_op jit(solution)/shard_map/all_to_all | solution.py:58
  169.1 8.3 %fusion.8 = f32[32,20,1408]{2,0,1:T(8,128)S(1)} fusion(bf16[1,2048,1408]{2,1,0:T(8,128)(2,1)} %param.18, bf16[32,20,2048]{2,1,0:T(8,128)(2,1)} %all-to-all-done.2), kind=kOutput, calls=%fused_computation.10 | convolution fusion | flops 3690987520 | bytes 11993088 | tf_op jit(solution)/shard_map/scd,df->scf/dot_general | solution.py:52
  177.4 8.5 %fusion.18 = bf16[32,20,1408]{2,0,1:T(8,128)(2,1)S(1)} fusion(bf16[1,2048,1408]{2,1,0:T(8,128)(2,1)} %param.19, f32[32,20,1408]{2,0,1:T(8,128)S(1)} %fusion.8, bf16[32,20,2048]{2,1,0:T(8,128)(2,1)} %all-to-all-done.2), kind=kOutput, calls=%fused_computation.16 | convolution fusion | flops 3696394240 | bytes 13795328 | tf_op jit(solution)/shard_map/scd,df->scf/dot_general | solution.py:53
  185.9 4.4 %fusion.21 = bf16[32,20,2048]{2,0,1:T(8,128)(2,1)S(1)} fusion(bf16[32,20,1408]{2,0,1:T(8,128)(2,1)S(1)} %fusion.18, bf16[1,1408,2048]{2,1,0:T(8,128)(2,1)S(1)} %bitcast.75), kind=kOutput, calls=%fused_computation.17 | convolution fusion | flops 3692298240 | bytes 10190848 | tf_op jit(solution)/shard_map/scf,fd->scd/dot_general | solution.py:55
  190.4 3.1 %copy.37 = bf16[32,20,2048]{2,1,0:T(8,128)(2,1)} copy(bf16[32,20,2048]{2,0,1:T(8,128)(2,1)S(1)} %fusion.21) | data formatting | bytes 5242880 | tf_op jit(solution)/shard_map/convert_element_type | solution.py:57
  193.5 3.9 %all-to-all-done.1 = bf16[32,16,2048]{2,1,0:T(8,128)(2,1)} async-done(((bf16[32,16,2048]{2,1,0:T(8,128)(2,1)}), bf16[32,16,2048]{2,1,0:T(8,128)(2,1)}, u32[]{:S(2)}, u32[]{:S(2)}) %all-to-all-start.1) | async-done | bytes 2097184 | tf_op jit(solution)/shard_map/all_to_all | solution.py:58
  197.4 5.3 %all-to-all-start.3 = ((bf16[32,20,2048]{2,1,0:T(8,128)(2,1)}), bf16[32,20,2048]{2,1,0:T(8,128)(2,1)}, u32[]{:S(2)}, u32[]{:S(2)}) async-start(bf16[32,20,2048]{2,1,0:T(8,128)(2,1)} %copy.37), calls=%async_computation.4 | async-start | bytes 6291456 | tf_op jit(solution)/shard_map/all_to_all | solution.py:58
  203.7 3.6 %scatter_custom_fusion.1 = f32[1152]{0:T(1024)S(1)} fusion(s32[768]{0:T(1024)S(1)} %fusion.78, f32[768]{0:T(1024)S(1)} %reshape.80, f32[]{:T(128)} %constant.36.clone.1), kind=kCustom, calls=%fused_computation.76 | custom fusion | bytes 4612 | tf_op jit(solution)/shard_map/scatter | solution.py:59
  208.1 4.1 %fusion.38 = f32[128,2048]{1,0:T(8,128)S(1)} fusion(bf16[32,16,2048]{2,1,0:T(8,128)(2,1)} %all-to-all-done.1, f32[128,2048]{1,0:T(8,128)S(1)} %get-tuple-element.10, f32[128,2048]{1,0:T(8,128)} %reduce-scatter.2.cloned.1.call-done, f32[32,36]{0,1:T(8,128)} %copy.29, s32[32,36]{0,1:T(8,128)} %copy.27), kind=kOutput, calls=%fused_computation.27 | convolution fusion | flops 1611431936 | bytes 5252096 | tf_op jit(solution)/shard_map/rec,ecd->rd/dot_general | solution.py:66
  212.2 30.4 %all-to-all-done.3 = bf16[32,20,2048]{2,1,0:T(8,128)(2,1)} async-done(((bf16[32,20,2048]{2,1,0:T(8,128)(2,1)}), bf16[32,20,2048]{2,1,0:T(8,128)(2,1)}, u32[]{:S(2)}, u32[]{:S(2)}) %all-to-all-start.3) | async-done | bytes 2621472 | tf_op jit(solution)/shard_map/all_to_all | solution.py:58
  242.7 5.5 %fusion.39 = bf16[128,2048]{1,0:T(8,128)(2,1)} fusion(f32[128,2048]{1,0:T(8,128)S(1)} %fusion.38, bf16[32,20,2048]{2,1,0:T(8,128)(2,1)} %all-to-all-done.3, f32[32,36]{0,1:T(8,128)} %copy.29, s32[32,36]{0,1:T(8,128)} %copy.27), kind=kOutput, calls=%fused_computation.29 | convolution fusion | flops 2014085120 | bytes 4203520 | tf_op jit(solution)/shard_map/rec,ecd->rd/dot_general | solution.py:66
  (50 shorter events, 3.9 us)
Async XLA Ops:
  6.5 98.8 %copy-start = (bf16[2048,352]{0,1:T(8,128)(2,1)S(1)}, bf16[2048,352]{0,1:T(8,128)(2,1)}, u32[]{:S(2)}) copy-start(bf16[2048,352]{0,1:T(8,128)(2,1)} %param.23) | copy-start | bytes 4325380
  6.5 59.5 %all-gather.3.cloned.1.call-start = ((), (), s32[]{:S(2)}) async-start(), calls=%async_computation.5 | async-start | bytes 8650752 | tf_op jit(solution)/shard_map/all_gather | solution.py:35
  7.3 95.2 %all-gather.5.cloned.1.call-start = ((), (), s32[]{:S(2)}) async-start(), calls=%async_computation.6 | async-start | bytes 2621440 | tf_op jit(solution)/shard_map/all_gather | solution.py:76
  14.9 56.1 %copy-start.4 = (f32[2048]{0:T(1024)S(1)}, f32[2048]{0:T(1024)}, u32[]{:S(2)}) copy-start(f32[2048]{0:T(1024)} %param.15) | copy-start | bytes 24580
  72.4 8.7 %copy-start.3 = (pred[32,36,128]{2,1,0:T(8,128)(4,1)}, pred[32,36,128]{2,1,0:T(8,128)(4,1)S(1)}, u32[]{:S(2)}) copy-start(pred[32,36,128]{2,1,0:T(8,128)(4,1)S(1)} %iota_compare_fusion) | copy-start | bytes 442372
  75.5 41.1 %all-to-all-start = ((bf16[32,16,2048]{2,1,0:T(8,128)(2,1)}), bf16[32,16,2048]{2,1,0:T(8,128)(2,1)}, u32[]{:S(2)}, u32[]{:S(2)}) async-start(bf16[32,16,2048]{2,1,0:T(8,128)(2,1)} %convolution_convert_fusion.1), calls=%async_computation.1 | async-start | bytes 4194304 | tf_op jit(solution)/shard_map/all_to_all | solution.py:51
  81.0 127.1 %reduce-scatter.2.cloned.1.call-start = ((), (), s32[]{:S(2)}) async-start(), calls=%async_computation.7 | async-start | bytes 5242880 | tf_op jit(solution)/shard_map/reduce_scatter | solution.py:83
  111.6 1.0 copy-start.2
  111.6 1.0 slice-start
  116.6 47.4 %all-to-all-start.2 = ((bf16[32,20,2048]{2,1,0:T(8,128)(2,1)}), bf16[32,20,2048]{2,1,0:T(8,128)(2,1)}, u32[]{:S(2)}, u32[]{:S(2)}) async-start(bf16[32,20,2048]{2,1,0:T(8,128)(2,1)} %copy.34), calls=%async_computation.3 | async-start | bytes 6291456 | tf_op jit(solution)/shard_map/all_to_all | solution.py:51
  124.2 13.5 %slice-start.1 = ((s8[5767168]{0:T(1024)(128)(4,1)}), s8[4194304]{0:T(1024)(128)(4,1)S(1)}, s32[]{:S(2)}) async-start(s8[5767168]{0:T(1024)(128)(4,1)} %bitcast.72), calls=%async_computation.9 | async-start | bytes 8388608
  130.8 6.9 %slice-start.2 = ((s8[5767168]{0:T(1024)(128)(4,1)}), s8[1572864]{0:T(1024)(128)(4,1)S(1)}, s32[]{:S(2)}) async-start(s8[5767168]{0:T(1024)(128)(4,1)} %bitcast.72), calls=%async_computation.10 | async-start | bytes 3145728
  164.1 33.4 %all-to-all-start.1 = ((bf16[32,16,2048]{2,1,0:T(8,128)(2,1)}), bf16[32,16,2048]{2,1,0:T(8,128)(2,1)}, u32[]{:S(2)}, u32[]{:S(2)}) async-start(bf16[32,16,2048]{2,1,0:T(8,128)(2,1)} %copy.31), calls=%async_computation.2 | async-start | bytes 4194304 | tf_op jit(solution)/shard_map/all_to_all | solution.py:58
  169.1 16.8 %slice-start.3 = ((s8[5767168]{0:T(1024)(128)(4,1)}), s8[4194304]{0:T(1024)(128)(4,1)S(1)}, s32[]{:S(2)}) async-start(s8[5767168]{0:T(1024)(128)(4,1)} %bitcast.74), calls=%async_computation.11 | async-start | bytes 8388608
  177.4 8.5 %slice-start.4 = ((s8[5767168]{0:T(1024)(128)(4,1)}), s8[1572864]{0:T(1024)(128)(4,1)S(1)}, s32[]{:S(2)}) async-start(s8[5767168]{0:T(1024)(128)(4,1)} %bitcast.74), calls=%async_computation.12 | async-start | bytes 3145728
  193.5 9.9 %copy-start.5 = (f32[128,6]{0,1:T(8,128)S(1)}, f32[128,6]{0,1:T(8,128)}, u32[]{:S(2)}) copy-start(f32[128,6]{0,1:T(8,128)} %param.17) | copy-start | bytes 9220
  197.4 45.2 %all-to-all-start.3 = ((bf16[32,20,2048]{2,1,0:T(8,128)(2,1)}), bf16[32,20,2048]{2,1,0:T(8,128)(2,1)}, u32[]{:S(2)}, u32[]{:S(2)}) async-start(bf16[32,20,2048]{2,1,0:T(8,128)(2,1)} %copy.37), calls=%async_computation.4 | async-start | bytes 6291456 | tf_op jit(solution)/shard_map/all_to_all | solution.py:58
  208.1 40.1 %copy-start.1 = (bf16[2048,352]{0,1:T(8,128)(2,1)S(1)}, bf16[2048,352]{0,1:T(8,128)(2,1)}, u32[]{:S(2)}) copy-start(bf16[2048,352]{0,1:T(8,128)(2,1)} %param.23) | copy-start | bytes 4325380
Sparse Core Ops, SparseCore 0:
  9.6 56.3 all-gather.2
  72.1 30.2 all-gather.4
  111.7 46.9 reduce-scatter.1

commit v13 on v8

--- a/solution.py
+++ b/solution.py
@@ -67,7 +67,7 @@
             "rec,ecd->rd",
             combine[:, :, lo:hi],
             part.astype(jnp.float32),
-            precision=lax.Precision.HIGHEST,
+            precision=lax.Precision.HIGH,
             preferred_element_type=jnp.float32,
         )
         for lo, hi, part in zip(bounds[:-1], bounds[1:], returned)

time: 251 us -> 251 us (level)
  transfers between devices with their start and end apart: 7 -> 7, of which waited for: 5 -> 5; matrix products, arithmetic and copies ran while one was open for 32% -> 31% of each run, Pallas kernels for 0% -> 0%
where the time goes in v13:
time: 251 us
  waiting for transfers between devices  123 us (49%)
  matrix products  67.1 us (27%)
  starting transfers between devices  23.5 us (9%)
  local copies, waits for them, and re-layouts  19.3 us (8%)
  between operations  13.4 us (5%)
  other arithmetic  3.8 us (2%)
    all_gather x1, waiting for transfers between devices, body(): lax.all_gather(out_weight, 'exp', axis=0, tiled=True)  51.1 us
    all_to_all x2, waiting for transfers between devices, body(): lax.all_to_all(result, 'exp', split_axis=0, concat_axis=0, tiled=True)  34.9 us
    all_to_all x2, waiting for transfers between devices, body(): lax.all_to_all(outgoing, 'exp', split_axis=0, concat_axis=0, tiled=True)  19.4 us
    all_gather x1, waiting for transfers between devices, body(): group_rows = lax.all_gather(normed, 'req', axis=0, tiled=True)  17.3 us
    dot_general x2, matrix products, body(): jnp.einsum('scd,df->scf', joined, w_gate, preferred_element_type=jnp.floa...  15.6 us
    dot_general x2, matrix products, body(): jnp.einsum('scd,df->scf', joined, w_up, preferred_element_type=jnp.float32)  15.4 us
    all_to_all x2, starting transfers between devices, body(): lax.all_to_all(outgoing, 'exp', split_axis=0, concat_axis=0, tiled=True)  13.1 us
    all_to_all x2, starting transfers between devices, body(): lax.all_to_all(result, 'exp', split_axis=0, concat_axis=0, tiled=True)  10.3 us
  transfers between devices with their start and end apart: 7, of which 5 were waited for; matrix products, arithmetic and copies ran while one was open for 31% of the time, Pallas kernels for 0%

profile of v13, /device:TPU:1, one launch (start us, length us, event | category | flops | bytes accessed | tf_op | source)
XLA Modules:
  0.0 250.5 jit_solution(235817732331820948)
XLA Ops:
  6.5 0.7 all-gather.3.cloned.1.call-update
  7.3 0.8 copy.24
  9.3 1.7 reduce-window.6
  11.5 3.4 %scatter_custom_fusion = s32[1152]{0:T(1024)S(1)} fusion(s32[768]{0:T(1024)S(1)} %fusion.83, s32[768]{0:T(1024)S(1)} %add_select_fusion, s32[]{:T(128)} %constant.13.clone.1), kind=kCustom, calls=%fused_computation.79 | custom fusion | bytes 4612 | tf_op jit(solution)/shard_map/scatter | solution.py:30
  14.9 51.1 %all-gather.3.cloned.1.call-done = bf16[2048,2048]{1,0:T(8,128)(2,1)} async-done(((bf16[64,2048]{1,0:T(8,128)(2,1)}), bf16[2048,2048]{1,0:T(8,128)(2,1)}) %all-gather.3.cloned.1.call-update) | async-done | bytes 8388624 | tf_op jit(solution)/shard_map/all_gather | solution.py:35
  66.1 5.0 %multiply_reduce_fusion = (f32[128]{0:T(128)S(1)}, f32[128,2048]{1,0:T(8,128)S(1)}) fusion(bf16[128,2048]{1,0:T(8,128)(2,1)} %param.12, bf16[2048,2048]{1,0:T(8,128)(2,1)} %all-gather.3.cloned.1.call-done, bf16[128,2048]{1,0:T(8,128)(2,1)} %param.13), kind=kOutput, calls=%fused_computation.41 | convolution fusion | flops 1075314560 | bytes 10486272 | tf_op jit(solution)/shard_map/dot_general | solution.py:33
  71.0 1.0 multiply_convert_fusion
  72.4 3.2 %convolution_convert_fusion.1 = bf16[32,16,2048]{2,1,0:T(8,128)(2,1)} fusion(bf16[128,2048]{1,0:T(8,128)(2,1)} %multiply_convert_fusion, pred[32,36,128]{2,1,0:T(8,128)(4,1)S(1)} %iota_compare_fusion), kind=kOutput, calls=%fused_computation.20 | convolution fusion | flops 269484032 | bytes 2686976 | tf_op jit(solution)/shard_map/ecr,rd->ecd/dot_general | solution.py:48
  75.6 5.5 %all-to-all-start = ((bf16[32,16,2048]{2,1,0:T(8,128)(2,1)}), bf16[32,16,2048]{2,1,0:T(8,128)(2,1)}, u32[]{:S(2)}, u32[]{:S(2)}) async-start(bf16[32,16,2048]{2,1,0:T(8,128)(2,1)} %convolution_convert_fusion.1), calls=%async_computation | async-start | bytes 4194304 | tf_op jit(solution)/shard_map/all_to_all | solution.py:51
  81.2 0.8 convolution_convert_fusion
  82.0 3.2 %copy.34 = bf16[32,20,2048]{2,1,0:T(8,128)(2,1)} copy(bf16[32,20,2048]{2,0,1:T(8,128)(2,1)S(1)} %convolution_convert_fusion) | data formatting | bytes 5242880 | tf_op jit(solution)/shard_map/convert_element_type | solution.py:50
  85.2 17.3 %all-gather.5.cloned.1.call-done = bf16[512,2048]{1,0:T(8,128)(2,1)} async-done(((bf16[128,2048]{1,0:T(8,128)(2,1)}), bf16[512,2048]{1,0:T(8,128)(2,1)}) %all-gather.5.cloned.1.call-update) | async-done | bytes 2097168 | tf_op jit(solution)/shard_map/all_gather | solution.py:76
  102.4 3.8 %fusion.87 = f32[512,352]{0,1:T(8,128)} fusion(bf16[512,2048]{1,0:T(8,128)(2,1)} %all-gather.5.cloned.1.call-done, bf16[2048,352]{0,1:T(8,128)(2,1)} %param.21), kind=kOutput, calls=%fused_computation.89 | convolution fusion | flops 738197504 | bytes 4259840 | tf_op jit(solution)/shard_map/dot_general | solution.py:77
  106.2 6.3 %fusion.54 = f32[512,2048]{1,0:T(8,128)} fusion(bf16[2048,352]{0,1:T(8,128)(2,1)S(1)} %copy-done, bf16[512,2048]{1,0:T(8,128)(2,1)} %all-gather.5.cloned.1.call-done, bf16[2048,352]{0,1:T(8,128)(2,1)} %param.22, f32[512,352]{0,1:T(8,128)} %fusion.87), kind=kOutput, calls=%fused_computation.39 | convolution fusion | flops 1477476352 | bytes 9895936 | tf_op jit(solution)/shard_map/dot_general | solution.py:80
  112.6 7.6 %all-to-all-start.2 = ((bf16[32,20,2048]{2,1,0:T(8,128)(2,1)}), bf16[32,20,2048]{2,1,0:T(8,128)(2,1)}, u32[]{:S(2)}, u32[]{:S(2)}) async-start(bf16[32,20,2048]{2,1,0:T(8,128)(2,1)} %copy.34), calls=%async_computation.2 | async-start | bytes 6291456 | tf_op jit(solution)/shard_map/all_to_all | solution.py:51
  120.2 7.3 %fusion.10 = f32[32,16,1408]{2,1,0:T(8,128)S(1)} fusion(bf16[32,16,2048]{2,1,0:T(8,128)(2,1)} %all-to-all-done, bf16[1,2048,1408]{2,1,0:T(8,128)(2,1)} %param.18), kind=kOutput, calls=%fused_computation.12 | convolution fusion | flops 2952790016 | bytes 10747904 | tf_op jit(solution)/shard_map/scd,df->scf/dot_general | solution.py:52
  127.6 6.9 %fusion.24 = bf16[32,16,1408]{2,1,0:T(8,128)(2,1)S(1)} fusion(bf16[32,16,2048]{2,1,0:T(8,128)(2,1)} %all-to-all-done, bf16[1,2048,1408]{2,1,0:T(8,128)(2,1)} %param.19, f32[32,16,1408]{2,1,0:T(8,128)S(1)} %fusion.10), kind=kOutput, calls=%fused_computation.19 | convolution fusion | flops 2957115392 | bytes 12189696 | tf_op jit(solution)/shard_map/scd,df->scf/dot_general | solution.py:53
  134.5 3.6 %fusion.27 = bf16[32,16,2048]{2,0,1:T(8,128)(2,1)S(1)} fusion(bf16[1,1408,2048]{2,1,0:T(8,128)(2,1)S(1)} %bitcast.77, bf16[32,16,1408]{2,1,0:T(8,128)(2,1)S(1)} %fusion.24), kind=kOutput, calls=%fused_computation.21 | convolution fusion | flops 2953838592 | bytes 9306112 | tf_op jit(solution)/shard_map/scf,fd->scd/dot_general | solution.py:55
  138.2 2.5 copy.31
  140.6 19.4 %all-to-all-done.2 = bf16[32,20,2048]{2,1,0:T(8,128)(2,1)} async-done(((bf16[32,20,2048]{2,1,0:T(8,128)(2,1)}), bf16[32,20,2048]{2,1,0:T(8,128)(2,1)}, u32[]{:S(2)}, u32[]{:S(2)}) %all-to-all-start.2) | async-done | bytes 2621472 | tf_op jit(solution)/shard_map/all_to_all | solution.py:51
  160.0 5.0 %all-to-all-start.1 = ((bf16[32,16,2048]{2,1,0:T(8,128)(2,1)}), bf16[32,16,2048]{2,1,0:T(8,128)(2,1)}, u32[]{:S(2)}, u32[]{:S(2)}) async-start(bf16[32,16,2048]{2,1,0:T(8,128)(2,1)} %copy.31), calls=%async_computation.1 | async-start | bytes 4194304 | tf_op jit(solution)/shard_map/all_to_all | solution.py:58
  165.1 8.3 %fusion.8 = f32[32,20,1408]{2,0,1:T(8,128)S(1)} fusion(bf16[1,2048,1408]{2,1,0:T(8,128)(2,1)} %param.18, bf16[32,20,2048]{2,1,0:T(8,128)(2,1)} %all-to-all-done.2), kind=kOutput, calls=%fused_computation.10 | convolution fusion | flops 3690987520 | bytes 11993088 | tf_op jit(solution)/shard_map/scd,df->scf/dot_general | solution.py:52
  173.4 8.5 %fusion.18 = bf16[32,20,1408]{2,0,1:T(8,128)(2,1)S(1)} fusion(bf16[1,2048,1408]{2,1,0:T(8,128)(2,1)} %param.19, f32[32,20,1408]{2,0,1:T(8,128)S(1)} %fusion.8, bf16[32,20,2048]{2,1,0:T(8,128)(2,1)} %all-to-all-done.2), kind=kOutput, calls=%fused_computation.16 | convolution fusion | flops 3696394240 | bytes 13795328 | tf_op jit(solution)/shard_map/scd,df->scf/dot_general | solution.py:53
  181.9 4.4 %fusion.21 = bf16[32,20,2048]{2,0,1:T(8,128)(2,1)S(1)} fusion(bf16[32,20,1408]{2,0,1:T(8,128)(2,1)S(1)} %fusion.18, bf16[1,1408,2048]{2,1,0:T(8,128)(2,1)S(1)} %bitcast.79), kind=kOutput, calls=%fused_computation.17 | convolution fusion | flops 3692298240 | bytes 10190848 | tf_op jit(solution)/shard_map/scf,fd->scd/dot_general | solution.py:55
  186.4 3.2 %copy.37 = bf16[32,20,2048]{2,1,0:T(8,128)(2,1)} copy(bf16[32,20,2048]{2,0,1:T(8,128)(2,1)S(1)} %fusion.21) | data formatting | bytes 5242880 | tf_op jit(solution)/shard_map/convert_element_type | solution.py:57
  189.5 3.9 %all-to-all-done.1 = bf16[32,16,2048]{2,1,0:T(8,128)(2,1)} async-done(((bf16[32,16,2048]{2,1,0:T(8,128)(2,1)}), bf16[32,16,2048]{2,1,0:T(8,128)(2,1)}, u32[]{:S(2)}, u32[]{:S(2)}) %all-to-all-start.1) | async-done | bytes 2097184 | tf_op jit(solution)/shard_map/all_to_all | solution.py:58
  193.4 5.3 %all-to-all-start.3 = ((bf16[32,20,2048]{2,1,0:T(8,128)(2,1)}), bf16[32,20,2048]{2,1,0:T(8,128)(2,1)}, u32[]{:S(2)}, u32[]{:S(2)}) async-start(bf16[32,20,2048]{2,1,0:T(8,128)(2,1)} %copy.37), calls=%async_computation.3 | async-start | bytes 6291456 | tf_op jit(solution)/shard_map/all_to_all | solution.py:58
  198.7 0.7 copy.27
  199.6 3.6 %scatter_custom_fusion.1 = f32[1152]{0:T(1024)S(1)} fusion(s32[768]{0:T(1024)S(1)} %fusion.83, f32[768]{0:T(1024)S(1)} %reshape.80, f32[]{:T(128)} %constant.36.clone.1), kind=kCustom, calls=%fused_computation.77 | custom fusion | bytes 4612 | tf_op jit(solution)/shard_map/scatter | solution.py:59
  204.1 3.6 %convolution_bitcast_fusion = f32[128,2048]{1,0:T(8,128)S(1)} fusion(bf16[32,16,2048]{2,1,0:T(8,128)(2,1)} %all-to-all-done.1, f32[32,36]{0,1:T(8,128)} %copy.29, s32[32,36]{0,1:T(8,128)} %copy.27), kind=kOutput, calls=%fused_computation.25 | convolution fusion | flops 805601280 | bytes 3154944 | tf_op jit(solution)/shard_map/rec,ecd->rd/dot_general | solution.py:66
  207.6 31.0 %all-to-all-done.3 = bf16[32,20,2048]{2,1,0:T(8,128)(2,1)} async-done(((bf16[32,20,2048]{2,1,0:T(8,128)(2,1)}), bf16[32,20,2048]{2,1,0:T(8,128)(2,1)}, u32[]{:S(2)}, u32[]{:S(2)}) %all-to-all-start.3) | async-done | bytes 2621472 | tf_op jit(solution)/shard_map/all_to_all | solution.py:58
  238.6 5.4 %fusion.46 = bf16[128,2048]{1,0:T(8,128)(2,1)} fusion(f32[128,2048]{1,0:T(8,128)} %reduce-scatter.2.cloned.1.call-done, f32[128,2048]{1,0:T(8,128)S(1)} %get-tuple-element.10, f32[128,2048]{1,0:T(8,128)S(1)} %convolution_bitcast_fusion, bf16[32,20,2048]{2,1,0:T(8,128)(2,1)} %all-to-all-done.3, f32[32,36]{0,1:T(8,128)} %copy.29, s32[32,36]{0,1:T(8,128)} %copy.27), kind=kOutput, calls=%fused_computation.32 | convolution fusion | flops 1007976448 | bytes 6300672 | tf_op jit(solution)/shard_map/rec,ecd->rd/dot_general | solution.py:66
  (47 shorter events, 3.2 us)
Async XLA Ops:
  6.5 99.7 %copy-start = (bf16[2048,352]{0,1:T(8,128)(2,1)S(1)}, bf16[2048,352]{0,1:T(8,128)(2,1)}, u32[]{:S(2)}) copy-start(bf16[2048,352]{0,1:T(8,128)(2,1)} %param.23) | copy-start | bytes 4325380
  6.5 59.5 %all-gather.3.cloned.1.call-start = ((), (), s32[]{:S(2)}) async-start(), calls=%async_computation.5 | async-start | bytes 8650752 | tf_op jit(solution)/shard_map/all_gather | solution.py:35
  7.3 95.2 %all-gather.5.cloned.1.call-start = ((), (), s32[]{:S(2)}) async-start(), calls=%async_computation.6 | async-start | bytes 2621440 | tf_op jit(solution)/shard_map/all_gather | solution.py:76
  14.9 56.1 %copy-start.3 = (f32[2048]{0:T(1024)S(1)}, f32[2048]{0:T(1024)}, u32[]{:S(2)}) copy-start(f32[2048]{0:T(1024)} %param.15) | copy-start | bytes 24580
  72.4 8.8 %copy-start.2 = (bf16[128,2048]{1,0:T(8,128)(2,1)S(1)}, bf16[128,2048]{1,0:T(8,128)(2,1)}, u32[]{:S(2)}) copy-start(bf16[128,2048]{1,0:T(8,128)(2,1)} %multiply_convert_fusion) | copy-start | bytes 1572868
  75.6 37.0 %all-to-all-start = ((bf16[32,16,2048]{2,1,0:T(8,128)(2,1)}), bf16[32,16,2048]{2,1,0:T(8,128)(2,1)}, u32[]{:S(2)}, u32[]{:S(2)}) async-start(bf16[32,16,2048]{2,1,0:T(8,128)(2,1)} %convolution_convert_fusion.1), calls=%async_computation | async-start | bytes 4194304 | tf_op jit(solution)/shard_map/all_to_all | solution.py:51
  81.1 157.5 %reduce-scatter.2.cloned.1.call-start = ((), (), s32[]{:S(2)}) async-start(), calls=%async_computation.7 | async-start | bytes 5242880 | tf_op jit(solution)/shard_map/reduce_scatter | solution.py:83
  112.6 47.4 %all-to-all-start.2 = ((bf16[32,20,2048]{2,1,0:T(8,128)(2,1)}), bf16[32,20,2048]{2,1,0:T(8,128)(2,1)}, u32[]{:S(2)}, u32[]{:S(2)}) async-start(bf16[32,20,2048]{2,1,0:T(8,128)(2,1)} %copy.34), calls=%async_computation.2 | async-start | bytes 6291456 | tf_op jit(solution)/shard_map/all_to_all | solution.py:51
  120.2 14.3 %slice-start = ((s8[5767168]{0:T(1024)(128)(4,1)}), s8[4194304]{0:T(1024)(128)(4,1)S(1)}, s32[]{:S(2)}) async-start(s8[5767168]{0:T(1024)(128)(4,1)} %bitcast.76), calls=%async_computation.8 | async-start | bytes 8388608
  127.6 7.0 %slice-start.1 = ((s8[5767168]{0:T(1024)(128)(4,1)}), s8[1572864]{0:T(1024)(128)(4,1)S(1)}, s32[]{:S(2)}) async-start(s8[5767168]{0:T(1024)(128)(4,1)} %bitcast.76), calls=%async_computation.9 | async-start | bytes 3145728
  160.0 33.4 %all-to-all-start.1 = ((bf16[32,16,2048]{2,1,0:T(8,128)(2,1)}), bf16[32,16,2048]{2,1,0:T(8,128)(2,1)}, u32[]{:S(2)}, u32[]{:S(2)}) async-start(bf16[32,16,2048]{2,1,0:T(8,128)(2,1)} %copy.31), calls=%async_computation.1 | async-start | bytes 4194304 | tf_op jit(solution)/shard_map/all_to_all | solution.py:58
  165.1 16.8 %slice-start.2 = ((s8[5767168]{0:T(1024)(128)(4,1)}), s8[4194304]{0:T(1024)(128)(4,1)S(1)}, s32[]{:S(2)}) async-start(s8[5767168]{0:T(1024)(128)(4,1)} %bitcast.78), calls=%async_computation.10 | async-start | bytes 8388608
  173.4 8.6 %slice-start.3 = ((s8[5767168]{0:T(1024)(128)(4,1)}), s8[1572864]{0:T(1024)(128)(4,1)S(1)}, s32[]{:S(2)}) async-start(s8[5767168]{0:T(1024)(128)(4,1)} %bitcast.78), calls=%async_computation.11 | async-start | bytes 3145728
  189.5 9.8 %copy-start.4 = (f32[128,6]{0,1:T(8,128)S(1)}, f32[128,6]{0,1:T(8,128)}, u32[]{:S(2)}) copy-start(f32[128,6]{0,1:T(8,128)} %param.17) | copy-start | bytes 9220
  193.4 45.2 %all-to-all-start.3 = ((bf16[32,20,2048]{2,1,0:T(8,128)(2,1)}), bf16[32,20,2048]{2,1,0:T(8,128)(2,1)}, u32[]{:S(2)}, u32[]{:S(2)}) async-start(bf16[32,20,2048]{2,1,0:T(8,128)(2,1)} %copy.37), calls=%async_computation.3 | async-start | bytes 6291456 | tf_op jit(solution)/shard_map/all_to_all | solution.py:58
  204.1 39.9 %copy-start.1 = (bf16[2048,352]{0,1:T(8,128)(2,1)S(1)}, bf16[2048,352]{0,1:T(8,128)(2,1)}, u32[]{:S(2)}) copy-start(bf16[2048,352]{0,1:T(8,128)(2,1)} %param.23) | copy-start | bytes 4325380
Sparse Core Ops, SparseCore 0:
  9.6 56.3 all-gather.2
  72.1 30.2 all-gather.4
  112.7 46.9 reduce-scatter.1

commit v14 on v13

--- a/solution.py
+++ b/solution.py
@@ -35,6 +35,7 @@
         lax.all_gather(out_weight, "exp", axis=0, tiled=True),
         preferred_element_type=jnp.float32,
     )
+    proj = lax.optimization_barrier(proj)
     stream = (residual.astype(jnp.float32) + proj).astype(jnp.bfloat16)
     stream_f = stream.astype(jnp.float32)
     scale = lax.rsqrt(jnp.mean(stream_f * stream_f, axis=1, keepdims=True) + 1e-06)

time: 251 us -> 250 us (level)
  no operation moved by 1% of the time
where the time goes in v14:
time: 250 us
  waiting for transfers between devices  125 us (50%)
  matrix products  65.9 us (26%)
  starting transfers between devices  23.5 us (9%)
  local copies, waits for them, and re-layouts  18.1 us (7%)
  between operations  13.5 us (5%)
  other arithmetic  4.09 us (2%)
    all_gather x1, waiting for transfers between devices, body(): lax.all_gather(out_weight, 'exp', axis=0, tiled=True)  51.1 us
    all_to_all x2, waiting for transfers between devices, body(): lax.all_to_all(result, 'exp', split_axis=0, concat_axis=0, tiled=True)  36.1 us
    all_to_all x2, waiting for transfers between devices, body(): lax.all_to_all(outgoing, 'exp', split_axis=0, concat_axis=0, tiled=True)  19.4 us
    all_gather x1, waiting for transfers between devices, body(): group_rows = lax.all_gather(normed, 'req', axis=0, tiled=True)  17.3 us
    dot_general x2, matrix products, body(): jnp.einsum('scd,df->scf', joined, w_gate, preferred_element_type=jnp.floa...  15.6 us
    dot_general x2, matrix products, body(): jnp.einsum('scd,df->scf', joined, w_up, preferred_element_type=jnp.float32)  15.4 us
    all_to_all x2, starting transfers between devices, body(): lax.all_to_all(outgoing, 'exp', split_axis=0, concat_axis=0, tiled=True)  13.1 us
    all_to_all x2, starting transfers between devices, body(): lax.all_to_all(result, 'exp', split_axis=0, concat_axis=0, tiled=True)  10.3 us
  transfers between devices with their start and end apart: 7, of which 5 were waited for; matrix products, arithmetic and copies ran while one was open for 31% of the time, Pallas kernels for 0%

profile of v14, /device:TPU:1, one launch (start us, length us, event | category | flops | bytes accessed | tf_op | source)
XLA Modules:
  0.0 249.7 jit_solution(15222790256009578458)
XLA Ops:
  6.5 0.7 all-gather.3.cloned.1.call-update
  7.3 0.8 copy.24
  8.4 0.7 broadcast_multiply_fusion
  9.3 1.7 reduce-window.6
  11.5 3.4 %scatter_custom_fusion = s32[1152]{0:T(1024)S(1)} fusion(s32[768]{0:T(1024)S(1)} %fusion.84, s32[768]{0:T(1024)S(1)} %add_select_fusion, s32[]{:T(128)} %constant.13.clone.1), kind=kCustom, calls=%fused_computation.80 | custom fusion | bytes 4612 | tf_op jit(solution)/shard_map/scatter | solution.py:30
  15.0 51.1 %all-gather.3.cloned.1.call-done = bf16[2048,2048]{1,0:T(8,128)(2,1)} async-done(((bf16[64,2048]{1,0:T(8,128)(2,1)}), bf16[2048,2048]{1,0:T(8,128)(2,1)}) %all-gather.3.cloned.1.call-update) | async-done | bytes 8388624 | tf_op jit(solution)/shard_map/all_gather | solution.py:35
  66.1 4.8 %fusion.88 = f32[128,2048]{1,0:T(8,128)S(1)} fusion(bf16[128,2048]{1,0:T(8,128)(2,1)} %param.12, bf16[2048,2048]{1,0:T(8,128)(2,1)} %all-gather.3.cloned.1.call-done), kind=kOutput, calls=%fused_computation.90 | convolution fusion | flops 1073741824 | bytes 9961472 | tf_op jit(solution)/shard_map/dot_general | solution.py:33
  71.2 1.0 fusion.55
  72.5 3.2 %convolution_convert_fusion.1 = bf16[32,16,2048]{2,1,0:T(8,128)(2,1)} fusion(bf16[128,2048]{1,0:T(8,128)(2,1)} %fusion.55, pred[32,36,128]{2,1,0:T(8,128)(4,1)S(1)} %iota_compare_fusion), kind=kOutput, calls=%fused_computation.20 | convolution fusion | flops 269484032 | bytes 2686976 | tf_op jit(solution)/shard_map/ecr,rd->ecd/dot_general | solution.py:49
  75.7 5.5 %all-to-all-start = ((bf16[32,16,2048]{2,1,0:T(8,128)(2,1)}), bf16[32,16,2048]{2,1,0:T(8,128)(2,1)}, u32[]{:S(2)}, u32[]{:S(2)}) async-start(bf16[32,16,2048]{2,1,0:T(8,128)(2,1)} %convolution_convert_fusion.1), calls=%async_computation | async-start | bytes 4194304 | tf_op jit(solution)/shard_map/all_to_all | solution.py:52
  81.3 0.8 convolution_convert_fusion
  82.2 3.1 %copy.34 = bf16[32,20,2048]{2,1,0:T(8,128)(2,1)} copy(bf16[32,20,2048]{2,0,1:T(8,128)(2,1)S(1)} %convolution_convert_fusion) | data formatting | bytes 5242880 | tf_op jit(solution)/shard_map/convert_element_type | solution.py:51
  85.3 17.3 %all-gather.5.cloned.1.call-done = bf16[512,2048]{1,0:T(8,128)(2,1)} async-done(((bf16[128,2048]{1,0:T(8,128)(2,1)}), bf16[512,2048]{1,0:T(8,128)(2,1)}) %all-gather.5.cloned.1.call-update) | async-done | bytes 2097168 | tf_op jit(solution)/shard_map/all_gather | solution.py:77
  102.6 2.9 %fusion.89 = f32[512,352]{0,1:T(8,128)S(1)} fusion(bf16[512,2048]{1,0:T(8,128)(2,1)} %all-gather.5.cloned.1.call-done, bf16[2048,352]{0,1:T(8,128)(2,1)} %param.21), kind=kOutput, calls=%fused_computation.91 | convolution fusion | flops 738197504 | bytes 4259840 | tf_op jit(solution)/shard_map/dot_general | solution.py:78
  105.5 6.2 %fusion.52 = f32[512,2048]{1,0:T(8,128)} fusion(bf16[2048,352]{0,1:T(8,128)(2,1)S(1)} %copy-done, bf16[512,2048]{1,0:T(8,128)(2,1)} %all-gather.5.cloned.1.call-done, bf16[2048,352]{0,1:T(8,128)(2,1)} %param.22, f32[512,352]{0,1:T(8,128)S(1)} %fusion.89), kind=kOutput, calls=%fused_computation.38 | convolution fusion | flops 1477476352 | bytes 9895936 | tf_op jit(solution)/shard_map/dot_general | solution.py:81
  111.7 7.6 %all-to-all-start.2 = ((bf16[32,20,2048]{2,1,0:T(8,128)(2,1)}), bf16[32,20,2048]{2,1,0:T(8,128)(2,1)}, u32[]{:S(2)}, u32[]{:S(2)}) async-start(bf16[32,20,2048]{2,1,0:T(8,128)(2,1)} %copy.34), calls=%async_computation.2 | async-start | bytes 6291456 | tf_op jit(solution)/shard_map/all_to_all | solution.py:52
  119.4 7.3 %fusion.10 = f32[32,16,1408]{2,1,0:T(8,128)S(1)} fusion(bf16[32,16,2048]{2,1,0:T(8,128)(2,1)} %all-to-all-done, bf16[1,2048,1408]{2,1,0:T(8,128)(2,1)} %param.18), kind=kOutput, calls=%fused_computation.12 | convolution fusion | flops 2952790016 | bytes 10747904 | tf_op jit(solution)/shard_map/scd,df->scf/dot_general | solution.py:53
  126.7 6.9 %fusion.24 = bf16[32,16,1408]{2,1,0:T(8,128)(2,1)S(1)} fusion(bf16[32,16,2048]{2,1,0:T(8,128)(2,1)} %all-to-all-done, bf16[1,2048,1408]{2,1,0:T(8,128)(2,1)} %param.19, f32[32,16,1408]{2,1,0:T(8,128)S(1)} %fusion.10), kind=kOutput, calls=%fused_computation.19 | convolution fusion | flops 2957115392 | bytes 12189696 | tf_op jit(solution)/shard_map/scd,df->scf/dot_general | solution.py:54
  133.7 3.6 %fusion.27 = bf16[32,16,2048]{2,0,1:T(8,128)(2,1)S(1)} fusion(bf16[1,1408,2048]{2,1,0:T(8,128)(2,1)S(1)} %bitcast.77, bf16[32,16,1408]{2,1,0:T(8,128)(2,1)S(1)} %fusion.24), kind=kOutput, calls=%fused_computation.21 | convolution fusion | flops 2953838592 | bytes 9306112 | tf_op jit(solution)/shard_map/scf,fd->scd/dot_general | solution.py:56
  137.3 2.5 copy.31
  139.8 19.4 %all-to-all-done.2 = bf16[32,20,2048]{2,1,0:T(8,128)(2,1)} async-done(((bf16[32,20,2048]{2,1,0:T(8,128)(2,1)}), bf16[32,20,2048]{2,1,0:T(8,128)(2,1)}, u32[]{:S(2)}, u32[]{:S(2)}) %all-to-all-start.2) | async-done | bytes 2621472 | tf_op jit(solution)/shard_map/all_to_all | solution.py:52
  159.2 5.0 %all-to-all-start.1 = ((bf16[32,16,2048]{2,1,0:T(8,128)(2,1)}), bf16[32,16,2048]{2,1,0:T(8,128)(2,1)}, u32[]{:S(2)}, u32[]{:S(2)}) async-start(bf16[32,16,2048]{2,1,0:T(8,128)(2,1)} %copy.31), calls=%async_computation.1 | async-start | bytes 4194304 | tf_op jit(solution)/shard_map/all_to_all | solution.py:59
  164.2 8.3 %fusion.8 = f32[32,20,1408]{2,0,1:T(8,128)S(1)} fusion(bf16[1,2048,1408]{2,1,0:T(8,128)(2,1)} %param.18, bf16[32,20,2048]{2,1,0:T(8,128)(2,1)} %all-to-all-done.2), kind=kOutput, calls=%fused_computation.10 | convolution fusion | flops 3690987520 | bytes 11993088 | tf_op jit(solution)/shard_map/scd,df->scf/dot_general | solution.py:53
  172.5 8.5 %fusion.18 = bf16[32,20,1408]{2,0,1:T(8,128)(2,1)S(1)} fusion(bf16[1,2048,1408]{2,1,0:T(8,128)(2,1)} %param.19, f32[32,20,1408]{2,0,1:T(8,128)S(1)} %fusion.8, bf16[32,20,2048]{2,1,0:T(8,128)(2,1)} %all-to-all-done.2), kind=kOutput, calls=%fused_computation.16 | convolution fusion | flops 3696394240 | bytes 13795328 | tf_op jit(solution)/shard_map/scd,df->scf/dot_general | solution.py:54
  181.0 4.4 %fusion.21 = bf16[32,20,2048]{2,0,1:T(8,128)(2,1)S(1)} fusion(bf16[32,20,1408]{2,0,1:T(8,128)(2,1)S(1)} %fusion.18, bf16[1,1408,2048]{2,1,0:T(8,128)(2,1)S(1)} %bitcast.79), kind=kOutput, calls=%fused_computation.17 | convolution fusion | flops 3692298240 | bytes 10190848 | tf_op jit(solution)/shard_map/scf,fd->scd/dot_general | solution.py:56
  185.5 3.2 %copy.37 = bf16[32,20,2048]{2,1,0:T(8,128)(2,1)} copy(bf16[32,20,2048]{2,0,1:T(8,128)(2,1)S(1)} %fusion.21) | data formatting | bytes 5242880 | tf_op jit(solution)/shard_map/convert_element_type | solution.py:58
  188.6 3.9 %all-to-all-done.1 = bf16[32,16,2048]{2,1,0:T(8,128)(2,1)} async-done(((bf16[32,16,2048]{2,1,0:T(8,128)(2,1)}), bf16[32,16,2048]{2,1,0:T(8,128)(2,1)}, u32[]{:S(2)}, u32[]{:S(2)}) %all-to-all-start.1) | async-done | bytes 2097184 | tf_op jit(solution)/shard_map/all_to_all | solution.py:59
  192.5 5.3 %all-to-all-start.3 = ((bf16[32,20,2048]{2,1,0:T(8,128)(2,1)}), bf16[32,20,2048]{2,1,0:T(8,128)(2,1)}, u32[]{:S(2)}, u32[]{:S(2)}) async-start(bf16[32,20,2048]{2,1,0:T(8,128)(2,1)} %copy.37), calls=%async_computation.3 | async-start | bytes 6291456 | tf_op jit(solution)/shard_map/all_to_all | solution.py:59
  198.2 3.6 %scatter_custom_fusion.1 = f32[1152]{0:T(1024)S(1)} fusion(s32[768]{0:T(1024)S(1)} %fusion.84, f32[768]{0:T(1024)S(1)} %reshape.80, f32[]{:T(128)} %constant.36.clone.1), kind=kCustom, calls=%fused_computation.78 | custom fusion | bytes 4612 | tf_op jit(solution)/shard_map/scatter | solution.py:60
  202.0 3.5 %convolution_bitcast_fusion = f32[128,2048]{1,0:T(8,128)S(1)} fusion(bf16[32,16,2048]{2,1,0:T(8,128)(2,1)} %all-to-all-done.1, f32[32,36]{0,1:T(8,128)S(1)} %copy.29, s32[32,36]{0,1:T(8,128)S(1)} %copy.27), kind=kOutput, calls=%fused_computation.25 | convolution fusion | flops 805601280 | bytes 3154944 | tf_op jit(solution)/shard_map/rec,ecd->rd/dot_general | solution.py:67
  205.5 32.2 %all-to-all-done.3 = bf16[32,20,2048]{2,1,0:T(8,128)(2,1)} async-done(((bf16[32,20,2048]{2,1,0:T(8,128)(2,1)}), bf16[32,20,2048]{2,1,0:T(8,128)(2,1)}, u32[]{:S(2)}, u32[]{:S(2)}) %all-to-all-start.3) | async-done | bytes 2621472 | tf_op jit(solution)/shard_map/all_to_all | solution.py:59
  237.8 5.4 %fusion.44 = bf16[128,2048]{1,0:T(8,128)(2,1)} fusion(f32[128,2048]{1,0:T(8,128)} %reduce-scatter.2.cloned.1.call-done, f32[128,2048]{1,0:T(8,128)S(1)} %convolution_bitcast_fusion, bf16[32,20,2048]{2,1,0:T(8,128)(2,1)} %all-to-all-done.3, bf16[128,2048]{1,0:T(8,128)(2,1)S(1)} %get-tuple-element.10, f32[32,36]{0,1:T(8,128)S(1)} %copy.29, s32[32,36]{0,1:T(8,128)S(1)} %copy.27), kind=kOutput, calls=%fused_computation.29 | convolution fusion | flops 1008238592 | bytes 5776384 | tf_op jit(solution)/shard_map/rec,ecd->rd/dot_general | solution.py:67
  (50 shorter events, 2.3 us)
Async XLA Ops:
  6.5 99.0 %copy-start = (bf16[2048,352]{0,1:T(8,128)(2,1)S(1)}, bf16[2048,352]{0,1:T(8,128)(2,1)}, u32[]{:S(2)}) copy-start(bf16[2048,352]{0,1:T(8,128)(2,1)} %param.23) | copy-start | bytes 4325380
  6.5 59.5 %all-gather.3.cloned.1.call-start = ((), (), s32[]{:S(2)}) async-start(), calls=%async_computation.5 | async-start | bytes 8650752 | tf_op jit(solution)/shard_map/all_gather | solution.py:35
  7.3 95.3 %all-gather.5.cloned.1.call-start = ((), (), s32[]{:S(2)}) async-start(), calls=%async_computation.6 | async-start | bytes 2621440 | tf_op jit(solution)/shard_map/all_gather | solution.py:77
  14.9 55.9 %copy-start.3 = (bf16[128,2048]{1,0:T(8,128)(2,1)S(1)}, bf16[128,2048]{1,0:T(8,128)(2,1)}, u32[]{:S(2)}) copy-start(bf16[128,2048]{1,0:T(8,128)(2,1)} %param.13) | copy-start | bytes 1572868
  14.9 56.2 %copy-start.4 = (f32[2048]{0:T(1024)S(1)}, f32[2048]{0:T(1024)}, u32[]{:S(2)}) copy-start(f32[2048]{0:T(1024)} %param.15) | copy-start | bytes 24580
  72.5 8.8 %copy-start.2 = (bf16[128,2048]{1,0:T(8,128)(2,1)S(1)}, bf16[128,2048]{1,0:T(8,128)(2,1)}, u32[]{:S(2)}) copy-start(bf16[128,2048]{1,0:T(8,128)(2,1)} %fusion.55) | copy-start | bytes 1572868
  75.7 36.0 %all-to-all-start = ((bf16[32,16,2048]{2,1,0:T(8,128)(2,1)}), bf16[32,16,2048]{2,1,0:T(8,128)(2,1)}, u32[]{:S(2)}, u32[]{:S(2)}) async-start(bf16[32,16,2048]{2,1,0:T(8,128)(2,1)} %convolution_convert_fusion.1), calls=%async_computation | async-start | bytes 4194304 | tf_op jit(solution)/shard_map/all_to_all | solution.py:52
  81.2 156.5 %reduce-scatter.2.cloned.1.call-start = ((), (), s32[]{:S(2)}) async-start(), calls=%async_computation.7 | async-start | bytes 5242880 | tf_op jit(solution)/shard_map/reduce_scatter | solution.py:84
  111.7 47.4 %all-to-all-start.2 = ((bf16[32,20,2048]{2,1,0:T(8,128)(2,1)}), bf16[32,20,2048]{2,1,0:T(8,128)(2,1)}, u32[]{:S(2)}, u32[]{:S(2)}) async-start(bf16[32,20,2048]{2,1,0:T(8,128)(2,1)} %copy.34), calls=%async_computation.2 | async-start | bytes 6291456 | tf_op jit(solution)/shard_map/all_to_all | solution.py:52
  119.3 14.3 %slice-start = ((s8[5767168]{0:T(1024)(128)(4,1)}), s8[4194304]{0:T(1024)(128)(4,1)S(1)}, s32[]{:S(2)}) async-start(s8[5767168]{0:T(1024)(128)(4,1)} %bitcast.76), calls=%async_computation.8 | async-start | bytes 8388608
  126.7 7.0 %slice-start.1 = ((s8[5767168]{0:T(1024)(128)(4,1)}), s8[1572864]{0:T(1024)(128)(4,1)S(1)}, s32[]{:S(2)}) async-start(s8[5767168]{0:T(1024)(128)(4,1)} %bitcast.76), calls=%async_computation.9 | async-start | bytes 3145728
  159.2 33.4 %all-to-all-start.1 = ((bf16[32,16,2048]{2,1,0:T(8,128)(2,1)}), bf16[32,16,2048]{2,1,0:T(8,128)(2,1)}, u32[]{:S(2)}, u32[]{:S(2)}) async-start(bf16[32,16,2048]{2,1,0:T(8,128)(2,1)} %copy.31), calls=%async_computation.1 | async-start | bytes 4194304 | tf_op jit(solution)/shard_map/all_to_all | solution.py:59
  164.2 16.8 %slice-start.2 = ((s8[5767168]{0:T(1024)(128)(4,1)}), s8[4194304]{0:T(1024)(128)(4,1)S(1)}, s32[]{:S(2)}) async-start(s8[5767168]{0:T(1024)(128)(4,1)} %bitcast.78), calls=%async_computation.10 | async-start | bytes 8388608
  172.5 8.5 %slice-start.3 = ((s8[5767168]{0:T(1024)(128)(4,1)}), s8[1572864]{0:T(1024)(128)(4,1)S(1)}, s32[]{:S(2)}) async-start(s8[5767168]{0:T(1024)(128)(4,1)} %bitcast.78), calls=%async_computation.11 | async-start | bytes 3145728
  188.6 9.3 %copy-start.5 = (f32[128,6]{0,1:T(8,128)S(1)}, f32[128,6]{0,1:T(8,128)}, u32[]{:S(2)}) copy-start(f32[128,6]{0,1:T(8,128)} %param.17) | copy-start | bytes 9220
  192.5 45.2 %all-to-all-start.3 = ((bf16[32,20,2048]{2,1,0:T(8,128)(2,1)}), bf16[32,20,2048]{2,1,0:T(8,128)(2,1)}, u32[]{:S(2)}, u32[]{:S(2)}) async-start(bf16[32,20,2048]{2,1,0:T(8,128)(2,1)} %copy.37), calls=%async_computation.3 | async-start | bytes 6291456 | tf_op jit(solution)/shard_map/all_to_all | solution.py:59
  202.0 41.1 %copy-start.1 = (bf16[2048,352]{0,1:T(8,128)(2,1)S(1)}, bf16[2048,352]{0,1:T(8,128)(2,1)}, u32[]{:S(2)}) copy-start(bf16[2048,352]{0,1:T(8,128)(2,1)} %param.23) | copy-start | bytes 4325380
Sparse Core Ops, SparseCore 0:
  9.6 56.3 all-gather.2
  72.3 30.2 all-gather.4
  111.8 46.9 reduce-scatter.1

commit v15 on v14

--- a/solution.py
+++ b/solution.py
@@ -46,9 +46,8 @@
     bounds = [0, min(16, capacity), capacity] if capacity > 16 else [0, capacity]
     returned = []
     for lo, hi in zip(bounds[:-1], bounds[1:]):
-        outgoing = jnp.einsum(
-            "ecr,rd->ecd", pick[:, lo:hi], normed, preferred_element_type=jnp.float32
-        ).astype(jnp.bfloat16)
+        padded = jnp.concatenate([normed, jnp.zeros((1, width), jnp.bfloat16)], axis=0)
+        outgoing = padded[table.reshape(experts, capacity)[:, lo:hi]]
         joined = lax.all_to_all(outgoing, "exp", split_axis=0, concat_axis=0, tiled=True)
         gate_part = jnp.einsum("scd,df->scf", joined, w_gate, preferred_element_type=jnp.float32)
         up_part = jnp.einsum("scd,df->scf", joined, w_up, preferred_element_type=jnp.float32)
@@ -57,12 +56,12 @@
             "scf,fd->scd", hidden, w_down, preferred_element_type=jnp.float32
         ).astype(jnp.bfloat16)
         returned.append(lax.all_to_all(result, "exp", split_axis=0, concat_axis=0, tiled=True))
-    slot_weight = jnp.zeros((experts * capacity,), jnp.float32).at[slot].set(gate_weights.reshape(-1))
-    combine = jnp.where(
-        table.reshape(experts, capacity)[None, :, :] == rows[:, None, None],
-        slot_weight.reshape(experts, capacity)[None, :, :],
-        0.0,
-    )
+    slots = jnp.arange(experts * capacity, dtype=jnp.int32)
+    row_slots = slot.reshape(row_count, topk)
+    combine = jnp.sum(
+        jnp.where(row_slots[:, :, None] == slots[None, None, :], gate_weights[:, :, None], 0.0),
+        axis=1,
+    ).reshape(row_count, experts, capacity)
     routed = sum(
         jnp.einsum(
             "rec,ecd->rd",

time: 250 us -> 252 us (level)
  local copies, waits for them, and re-layouts: 18.1 us -> 26.6 us
  matrix products: 65.9 us -> 60.4 us
    gather x0 -> x3, local copies, waits for them, and re-layouts: none -> 12.6 us  [body(): outgoing = padded[table.reshape(experts, capacity)[:, lo:hi]]]
    all_gather x1, waiting for transfers between devices: 17.3 us -> 10.7 us  [body(): group_rows = lax.all_gather(normed, 'req', axis=0, tiled=True)]
    dot_general x2 -> x0, matrix products: 4.01 us -> none  [body(): jnp.einsum('ecr,rd->ecd', pick[:, lo:hi], normed, preferred_element_type=...]
    scatter x1 -> x0, local copies, waits for them, and re-layouts: 3.64 us -> none  [body(): jnp.zeros((experts * capacity,), jnp.float32).at[slot]]
    all_to_all x2, waiting for transfers between devices: 36.1 us -> 39.3 us  [body(): lax.all_to_all(result, 'exp', split_axis=0, concat_axis=0, tiled=True)]
    convert_element_type x1 -> x0, local copies, waits for them, and re-layouts: 3.15 us -> none  [body(): outgoing = jnp.einsum('ecr,rd->ecd', pick[:, lo:hi], normed, preferred_el...]
where the time goes in v15:
time: 252 us
  waiting for transfers between devices  123 us (49%)
  matrix products  60.4 us (24%)
  local copies, waits for them, and re-layouts  26.6 us (11%)
  starting transfers between devices  23.6 us (9%)
  between operations  13.5 us (5%)
  other arithmetic  4.38 us (2%)
    all_gather x1, waiting for transfers between devices, body(): lax.all_gather(out_weight, 'exp', axis=0, tiled=True)  51.1 us
    all_to_all x2, waiting for transfers between devices, body(): lax.all_to_all(result, 'exp', split_axis=0, concat_axis=0, tiled=True)  39.3 us
    all_to_all x2, waiting for transfers between devices, body(): lax.all_to_all(outgoing, 'exp', split_axis=0, concat_axis=0, tiled=True)  21.1 us
    dot_general x2, matrix products, body(): jnp.einsum('scd,df->scf', joined, w_gate, preferred_element_type=jnp.floa...  15.6 us
    dot_general x2, matrix products, body(): jnp.einsum('scd,df->scf', joined, w_up, preferred_element_type=jnp.float32)  13.7 us
    all_to_all x2, starting transfers between devices, body(): lax.all_to_all(outgoing, 'exp', split_axis=0, concat_axis=0, tiled=True)  13.3 us
    gather x3, local copies, waits for them, and re-layouts, body(): outgoing = padded[table.reshape(experts, capacity)[:, lo:hi]]  12.6 us
    all_gather x1, waiting for transfers between devices, body(): group_rows = lax.all_gather(normed, 'req', axis=0, tiled=True)  10.7 us
  transfers between devices with their start and end apart: 7, of which 5 were waited for; matrix products, arithmetic and copies ran while one was open for 31% of the time, Pallas kernels for 0%

profile of v15, /device:TPU:1, one launch (start us, length us, event | category | flops | bytes accessed | tf_op | source)
XLA Modules:
  0.0 251.5 jit_solution(10835718608701939738)
XLA Ops:
  7.3 0.8 copy.37
  8.4 1.7 reduce-window.6
  11.5 3.4 %scatter_custom_fusion = s32[1152]{0:T(1024)S(1)} fusion(s32[768]{0:T(1024)S(1)} %fusion.72, s32[768]{0:T(1024)S(1)} %add_select_fusion, s32[]{:T(128)} %constant.13.clone.1), kind=kCustom, calls=%fused_computation.72 | custom fusion | bytes 4612 | tf_op jit(solution)/shard_map/scatter | solution.py:30
  14.9 51.1 %all-gather.3.cloned.1.call-done = bf16[2048,2048]{1,0:T(8,128)(2,1)} async-done(((bf16[64,2048]{1,0:T(8,128)(2,1)}), bf16[2048,2048]{1,0:T(8,128)(2,1)}) %all-gather.3.cloned.1.call-update) | async-done | bytes 8388624 | tf_op jit(solution)/shard_map/all_gather | solution.py:35
  66.1 4.8 %fusion.75 = f32[128,2048]{1,0:T(8,128)S(1)} fusion(bf16[128,2048]{1,0:T(8,128)(2,1)} %param.12, bf16[2048,2048]{1,0:T(8,128)(2,1)} %all-gather.3.cloned.1.call-done), kind=kOutput, calls=%fused_computation.80 | convolution fusion | flops 1073741824 | bytes 9961472 | tf_op jit(solution)/shard_map/dot_general | solution.py:33
  71.2 0.8 copy-done.2
  71.9 1.0 fusion.55
  73.1 1.1 concatenate.4
  74.2 3.4 %gather_fusion = bf16[512,2048]{1,0:T(8,128)(2,1)} fusion(bf16[129,2048]{1,0:T(8,128)(2,1)S(1)} %concatenate.4, s32[1024]{0:T(1024)S(1)} %pad_clamp_fusion.1), kind=kCustom, calls=%fused_computation | custom fusion | bytes 4196352 | tf_op jit(solution)/shard_map/gather | solution.py:50
  77.6 5.5 %all-to-all-start = ((bf16[32,16,2048]{2,1,0:T(8,128)(2,1)}), bf16[32,16,2048]{2,1,0:T(8,128)(2,1)}, u32[]{:S(2)}, u32[]{:S(2)}) async-start(bf16[32,16,2048]{2,1,0:T(8,128)(2,1)} %bitcast.72), calls=%async_computation | async-start | bytes 4194304 | tf_op jit(solution)/shard_map/all_to_all | solution.py:51
  83.4 4.1 %gather_fusion.1 = bf16[640,2048]{1,0:T(8,128)(2,1)} fusion(bf16[129,2048]{1,0:T(8,128)(2,1)S(1)} %concatenate.4, s32[1024]{0:T(1024)S(1)} %pad_clamp_fusion), kind=kCustom, calls=%fused_computation.1 | custom fusion | bytes 5245440 | tf_op jit(solution)/shard_map/gather | solution.py:50
  87.5 5.1 %reshape.89 = bf16[32,20,2048]{2,1,0:T(8,128)(2,1)} reshape(bf16[640,2048]{1,0:T(8,128)(2,1)} %gather_fusion.1) | data formatting | bytes 5242880 | tf_op jit(solution)/shard_map/gather | solution.py:50
  92.6 10.7 %all-gather.5.cloned.1.call-done = bf16[512,2048]{1,0:T(8,128)(2,1)} async-done(((bf16[128,2048]{1,0:T(8,128)(2,1)}), bf16[512,2048]{1,0:T(8,128)(2,1)}) %all-gather.5.cloned.1.call-update) | async-done | bytes 2097168 | tf_op jit(solution)/shard_map/all_gather | solution.py:76
  103.4 3.9 %fusion.76 = f32[512,352]{0,1:T(8,128)} fusion(bf16[512,2048]{1,0:T(8,128)(2,1)} %all-gather.5.cloned.1.call-done, bf16[2048,352]{0,1:T(8,128)(2,1)} %param.21), kind=kOutput, calls=%fused_computation.81 | convolution fusion | flops 738197504 | bytes 4259840 | tf_op jit(solution)/shard_map/dot_general | solution.py:77
  107.3 5.7 %fusion.52 = f32[512,2048]{1,0:T(8,128)} fusion(bf16[2048,352]{0,1:T(8,128)(2,1)S(1)} %copy-done, bf16[512,2048]{1,0:T(8,128)(2,1)S(1)} %copy-done.7, bf16[2048,352]{0,1:T(8,128)(2,1)} %param.22, f32[512,352]{0,1:T(8,128)} %fusion.76), kind=kOutput, calls=%fused_computation.39 | convolution fusion | flops 1477476352 | bytes 9895936 | tf_op jit(solution)/shard_map/dot_general | solution.py:80
  113.1 7.7 %all-to-all-start.2 = ((bf16[32,20,2048]{2,1,0:T(8,128)(2,1)}), bf16[32,20,2048]{2,1,0:T(8,128)(2,1)}, u32[]{:S(2)}, u32[]{:S(2)}) async-start(bf16[32,20,2048]{2,1,0:T(8,128)(2,1)} %reshape.89), calls=%async_computation.2 | async-start | bytes 6291456 | tf_op jit(solution)/shard_map/all_to_all | solution.py:51
  120.8 7.3 %fusion.10 = f32[32,16,1408]{2,1,0:T(8,128)S(1)} fusion(bf16[32,16,2048]{2,1,0:T(8,128)(2,1)} %all-to-all-done, bf16[1,2048,1408]{2,1,0:T(8,128)(2,1)} %param.18), kind=kOutput, calls=%fused_computation.13 | convolution fusion | flops 2952790016 | bytes 10747904 | tf_op jit(solution)/shard_map/scd,df->scf/dot_general | solution.py:52
  128.2 5.2 %fusion.24 = bf16[32,16,1408]{2,1,0:T(8,128)(2,1)S(1)} fusion(bf16[32,16,2048]{2,1,0:T(8,128)(2,1)} %all-to-all-done, bf16[1,2048,1408]{2,1,0:T(8,128)(2,1)S(1)} %bitcast.75, f32[32,16,1408]{2,1,0:T(8,128)S(1)} %fusion.10), kind=kOutput, calls=%fused_computation.21 | convolution fusion | flops 2957115392 | bytes 12189696 | tf_op jit(solution)/shard_map/scd,df->scf/dot_general | solution.py:53
  133.4 3.6 %fusion.27 = bf16[32,16,2048]{2,0,1:T(8,128)(2,1)S(1)} fusion(bf16[1,1408,2048]{2,1,0:T(8,128)(2,1)S(1)} %bitcast.77, bf16[32,16,1408]{2,1,0:T(8,128)(2,1)S(1)} %fusion.24), kind=kOutput, calls=%fused_computation.22 | convolution fusion | flops 2953838592 | bytes 9306112 | tf_op jit(solution)/shard_map/scf,fd->scd/dot_general | solution.py:55
  137.1 2.5 copy.45
  139.5 21.1 %all-to-all-done.2 = bf16[32,20,2048]{2,1,0:T(8,128)(2,1)} async-done(((bf16[32,20,2048]{2,1,0:T(8,128)(2,1)}), bf16[32,20,2048]{2,1,0:T(8,128)(2,1)}, u32[]{:S(2)}, u32[]{:S(2)}) %all-to-all-start.2) | async-done | bytes 2621472 | tf_op jit(solution)/shard_map/all_to_all | solution.py:51
  160.6 5.0 %all-to-all-start.1 = ((bf16[32,16,2048]{2,1,0:T(8,128)(2,1)}), bf16[32,16,2048]{2,1,0:T(8,128)(2,1)S(1)}, u32[]{:S(2)}, u32[]{:S(2)}) async-start(bf16[32,16,2048]{2,1,0:T(8,128)(2,1)} %copy.45), calls=%async_computation.1 | async-start | bytes 4194304 | tf_op jit(solution)/shard_map/all_to_all | solution.py:58
  165.6 8.3 %fusion.8 = f32[32,20,1408]{2,0,1:T(8,128)S(1)} fusion(bf16[1,2048,1408]{2,1,0:T(8,128)(2,1)} %param.18, bf16[32,20,2048]{2,1,0:T(8,128)(2,1)} %all-to-all-done.2), kind=kOutput, calls=%fused_computation.11 | convolution fusion | flops 3690987520 | bytes 11993088 | tf_op jit(solution)/shard_map/scd,df->scf/dot_general | solution.py:52
  173.9 8.5 %fusion.18 = bf16[32,20,1408]{2,0,1:T(8,128)(2,1)S(1)} fusion(bf16[1,2048,1408]{2,1,0:T(8,128)(2,1)} %param.19, f32[32,20,1408]{2,0,1:T(8,128)S(1)} %fusion.8, bf16[32,20,2048]{2,1,0:T(8,128)(2,1)} %all-to-all-done.2), kind=kOutput, calls=%fused_computation.19 | convolution fusion | flops 3696394240 | bytes 13795328 | tf_op jit(solution)/shard_map/scd,df->scf/dot_general | solution.py:53
  182.4 4.4 %fusion.21 = bf16[32,20,2048]{2,0,1:T(8,128)(2,1)S(1)} fusion(bf16[32,20,1408]{2,0,1:T(8,128)(2,1)S(1)} %fusion.18, bf16[1,1408,2048]{2,1,0:T(8,128)(2,1)S(1)} %bitcast.79), kind=kOutput, calls=%fused_computation.20 | convolution fusion | flops 3692298240 | bytes 10190848 | tf_op jit(solution)/shard_map/scf,fd->scd/dot_general | solution.py:55
  186.9 3.2 %copy.50 = bf16[32,20,2048]{2,1,0:T(8,128)(2,1)} copy(bf16[32,20,2048]{2,0,1:T(8,128)(2,1)S(1)} %fusion.21) | data formatting | bytes 5242880 | tf_op jit(solution)/shard_map/convert_element_type | solution.py:57
  190.0 3.8 %all-to-all-done.1 = bf16[32,16,2048]{2,1,0:T(8,128)(2,1)S(1)} async-done(((bf16[32,16,2048]{2,1,0:T(8,128)(2,1)}), bf16[32,16,2048]{2,1,0:T(8,128)(2,1)S(1)}, u32[]{:S(2)}, u32[]{:S(2)}) %all-to-all-start.1) | async-done | bytes 2097184 | tf_op jit(solution)/shard_map/all_to_all | solution.py:58
  193.9 5.3 %all-to-all-start.3 = ((bf16[32,20,2048]{2,1,0:T(8,128)(2,1)}), bf16[32,20,2048]{2,1,0:T(8,128)(2,1)}, u32[]{:S(2)}, u32[]{:S(2)}) async-start(bf16[32,20,2048]{2,1,0:T(8,128)(2,1)} %copy.50), calls=%async_computation.3 | async-start | bytes 6291456 | tf_op jit(solution)/shard_map/all_to_all | solution.py:58
  200.1 0.8 slice.31
  200.8 2.8 %convolution_bitcast_fusion = f32[128,2048]{1,0:T(8,128)} fusion(bf16[32,16,2048]{2,1,0:T(8,128)(2,1)S(1)} %all-to-all-done.1, f32[128,32,16]{0,2,1:T(8,128)S(1)} %slice.29), kind=kOutput, calls=%fused_computation.26 | convolution fusion | flops 805306368 | bytes 3407872 | tf_op jit(solution)/shard_map/rec,ecd->rd/dot_general | solution.py:66
  203.6 35.5 %all-to-all-done.3 = bf16[32,20,2048]{2,1,0:T(8,128)(2,1)} async-done(((bf16[32,20,2048]{2,1,0:T(8,128)(2,1)}), bf16[32,20,2048]{2,1,0:T(8,128)(2,1)}, u32[]{:S(2)}, u32[]{:S(2)}) %all-to-all-start.3) | async-done | bytes 2621472 | tf_op jit(solution)/shard_map/all_to_all | solution.py:58
  239.1 5.9 %fusion.44 = bf16[128,2048]{1,0:T(8,128)(2,1)} fusion(f32[128,2048]{1,0:T(8,128)} %reduce-scatter.2.cloned.1.call-done, f32[128,2048]{1,0:T(8,128)} %convolution_bitcast_fusion, bf16[32,20,2048]{2,1,0:T(8,128)(2,1)} %all-to-all-done.3, bf16[128,2048]{1,0:T(8,128)(2,1)} %copy-done.2, f32[128,32,20]{0,2,1:T(8,128)} %slice.31), kind=kOutput, calls=%fused_computation.30 | convolution fusion | flops 1007943680 | bytes 6094848 | tf_op jit(solution)/shard_map/rec,ecd->rd/dot_general | solution.py:66
  (64 shorter events, 4.0 us)
Async XLA Ops:
  6.5 100.8 %copy-start = (bf16[2048,352]{0,1:T(8,128)(2,1)S(1)}, bf16[2048,352]{0,1:T(8,128)(2,1)}, u32[]{:S(2)}) copy-start(bf16[2048,352]{0,1:T(8,128)(2,1)} %param.23) | copy-start | bytes 4325380
  6.5 59.5 %all-gather.3.cloned.1.call-start = ((), (), s32[]{:S(2)}) async-start(), calls=%async_computation.5 | async-start | bytes 8650752 | tf_op jit(solution)/shard_map/all_gather | solution.py:35
  7.3 96.1 %all-gather.5.cloned.1.call-start = ((), (), s32[]{:S(2)}) async-start(), calls=%async_computation.6 | async-start | bytes 2621440 | tf_op jit(solution)/shard_map/all_gather | solution.py:76
  14.9 56.0 %copy-start.3 = (bf16[128,2048]{1,0:T(8,128)(2,1)S(1)}, bf16[128,2048]{1,0:T(8,128)(2,1)}, u32[]{:S(2)}) copy-start(bf16[128,2048]{1,0:T(8,128)(2,1)} %param.13) | copy-start | bytes 1572868
  14.9 57.0 %copy-start.5 = (f32[2048]{0:T(1024)S(1)}, f32[2048]{0:T(1024)}, u32[]{:S(2)}) copy-start(f32[2048]{0:T(1024)} %param.15) | copy-start | bytes 24580
  71.1 0.8 copy-start.2
  77.6 35.4 %all-to-all-start = ((bf16[32,16,2048]{2,1,0:T(8,128)(2,1)}), bf16[32,16,2048]{2,1,0:T(8,128)(2,1)}, u32[]{:S(2)}, u32[]{:S(2)}) async-start(bf16[32,16,2048]{2,1,0:T(8,128)(2,1)} %bitcast.72), calls=%async_computation | async-start | bytes 4194304 | tf_op jit(solution)/shard_map/all_to_all | solution.py:51
  83.2 156.0 %reduce-scatter.2.cloned.1.call-start = ((), (), s32[]{:S(2)}) async-start(), calls=%async_computation.7 | async-start | bytes 5242880 | tf_op jit(solution)/shard_map/reduce_scatter | solution.py:83
  103.4 4.0 %copy-start.7 = (bf16[512,2048]{1,0:T(8,128)(2,1)S(1)}, bf16[512,2048]{1,0:T(8,128)(2,1)}, u32[]{:S(2)}) copy-start(bf16[512,2048]{1,0:T(8,128)(2,1)} %all-gather.5.cloned.1.call-done) | copy-start | bytes 6291460
  113.0 15.1 %slice-start = ((s8[5767168]{0:T(1024)(128)(4,1)}), s8[1572864]{0:T(1024)(128)(4,1)S(1)}, s32[]{:S(2)}) async-start(s8[5767168]{0:T(1024)(128)(4,1)} %bitcast.74), calls=%async_computation.8 | async-start | bytes 3145728
  113.1 47.6 %all-to-all-start.2 = ((bf16[32,20,2048]{2,1,0:T(8,128)(2,1)}), bf16[32,20,2048]{2,1,0:T(8,128)(2,1)}, u32[]{:S(2)}, u32[]{:S(2)}) async-start(bf16[32,20,2048]{2,1,0:T(8,128)(2,1)} %reshape.89), calls=%async_computation.2 | async-start | bytes 6291456 | tf_op jit(solution)/shard_map/all_to_all | solution.py:51
  120.8 7.3 %slice-start.1 = ((s8[5767168]{0:T(1024)(128)(4,1)}), s8[4194304]{0:T(1024)(128)(4,1)S(1)}, s32[]{:S(2)}) async-start(s8[5767168]{0:T(1024)(128)(4,1)} %bitcast.74), calls=%async_computation.9 | async-start | bytes 8388608
  120.8 12.6 %slice-start.2 = ((s8[5767168]{0:T(1024)(128)(4,1)}), s8[4194304]{0:T(1024)(128)(4,1)S(1)}, s32[]{:S(2)}) async-start(s8[5767168]{0:T(1024)(128)(4,1)} %bitcast.76), calls=%async_computation.10 | async-start | bytes 8388608
  128.2 5.3 %slice-start.3 = ((s8[5767168]{0:T(1024)(128)(4,1)}), s8[1572864]{0:T(1024)(128)(4,1)S(1)}, s32[]{:S(2)}) async-start(s8[5767168]{0:T(1024)(128)(4,1)} %bitcast.76), calls=%async_computation.11 | async-start | bytes 3145728
  160.6 33.3 %all-to-all-start.1 = ((bf16[32,16,2048]{2,1,0:T(8,128)(2,1)}), bf16[32,16,2048]{2,1,0:T(8,128)(2,1)S(1)}, u32[]{:S(2)}, u32[]{:S(2)}) async-start(bf16[32,16,2048]{2,1,0:T(8,128)(2,1)} %copy.45), calls=%async_computation.1 | async-start | bytes 4194304 | tf_op jit(solution)/shard_map/all_to_all | solution.py:58
  165.6 16.8 %slice-start.4 = ((s8[5767168]{0:T(1024)(128)(4,1)}), s8[4194304]{0:T(1024)(128)(4,1)S(1)}, s32[]{:S(2)}) async-start(s8[5767168]{0:T(1024)(128)(4,1)} %bitcast.78), calls=%async_computation.12 | async-start | bytes 8388608
  173.9 8.5 %slice-start.5 = ((s8[5767168]{0:T(1024)(128)(4,1)}), s8[1572864]{0:T(1024)(128)(4,1)S(1)}, s32[]{:S(2)}) async-start(s8[5767168]{0:T(1024)(128)(4,1)} %bitcast.78), calls=%async_computation.13 | async-start | bytes 3145728
  190.0 9.1 %copy-start.4 = (s32[128,6]{1,0:T(8,128)S(1)}, s32[128,6]{1,0:T(8,128)}, u32[]{:S(2)}) copy-start(s32[128,6]{1,0:T(8,128)} %get-tuple-element.11) | copy-start | bytes 9220
  190.0 9.2 %copy-start.6 = (f32[128,6]{0,1:T(8,128)S(1)}, f32[128,6]{0,1:T(8,128)}, u32[]{:S(2)}) copy-start(f32[128,6]{0,1:T(8,128)} %param.17) | copy-start | bytes 9220
  193.9 45.2 %all-to-all-start.3 = ((bf16[32,20,2048]{2,1,0:T(8,128)(2,1)}), bf16[32,20,2048]{2,1,0:T(8,128)(2,1)}, u32[]{:S(2)}, u32[]{:S(2)}) async-start(bf16[32,20,2048]{2,1,0:T(8,128)(2,1)} %copy.50), calls=%async_computation.3 | async-start | bytes 6291456 | tf_op jit(solution)/shard_map/all_to_all | solution.py:58
  200.8 44.1 %copy-start.1 = (bf16[2048,352]{0,1:T(8,128)(2,1)S(1)}, bf16[2048,352]{0,1:T(8,128)(2,1)}, u32[]{:S(2)}) copy-start(bf16[2048,352]{0,1:T(8,128)(2,1)} %param.23) | copy-start | bytes 4325380
Sparse Core Ops, SparseCore 0:
  9.6 56.3 all-gather.2
  73.1 30.2 all-gather.4
  113.2 46.9 reduce-scatter.1

commit v16 on v14

--- a/solution.py
+++ b/solution.py
@@ -50,6 +50,8 @@
             "ecr,rd->ecd", pick[:, lo:hi], normed, preferred_element_type=jnp.float32
         ).astype(jnp.bfloat16)
         joined = lax.all_to_all(outgoing, "exp", split_axis=0, concat_axis=0, tiled=True)
+        if lo == 0:
+            first_landed = joined
         gate_part = jnp.einsum("scd,df->scf", joined, w_gate, preferred_element_type=jnp.float32)
         up_part = jnp.einsum("scd,df->scf", joined, w_up, preferred_element_type=jnp.float32)
         hidden = (jax.nn.silu(gate_part) * up_part).astype(jnp.bfloat16)
@@ -75,6 +77,7 @@
     )
 
     group_rows = lax.all_gather(normed, "req", axis=0, tiled=True)
+    group_rows, _ = lax.optimization_barrier((group_rows, first_landed))
     s_gate = jnp.dot(group_rows, shared_gate, preferred_element_type=jnp.float32)
     s_up = jnp.dot(group_rows, shared_up, preferred_element_type=jnp.float32)
     s_hidden = (jax.nn.silu(s_gate) * s_up).astype(jnp.bfloat16)

time: 250 us -> 246 us (0.984)
    all_gather x1, waiting for transfers between devices: 17.3 us -> 0.02 us  [body(): group_rows = lax.all_gather(normed, 'req', axis=0, tiled=True)]
    all_to_all x2, waiting for transfers between devices: 19.4 us -> 35.3 us  [body(): lax.all_to_all(outgoing, 'exp', split_axis=0, concat_axis=0, tiled=True)]
where the time goes in v16:
time: 246 us; the launch traced here: 245 us
  waiting for transfers between devices  123 us (50%)
  matrix products  65.1 us (26%)
  starting transfers between devices  21.3 us (9%)
  local copies, waits for them, and re-layouts  18.1 us (7%)
  between operations  13.5 us (5%)
  other arithmetic  4.09 us (2%)
    all_gather x1, waiting for transfers between devices, body(): lax.all_gather(out_weight, 'exp', axis=0, tiled=True)  51.1 us
    all_to_all x2, waiting for transfers between devices, body(): lax.all_to_all(result, 'exp', split_axis=0, concat_axis=0, tiled=True)  36 us
    all_to_all x2, waiting for transfers between devices, body(): lax.all_to_all(outgoing, 'exp', split_axis=0, concat_axis=0, tiled=True)  35.3 us
    dot_general x2, matrix products, body(): jnp.einsum('scd,df->scf', joined, w_up, preferred_element_type=jnp.float32)  15.4 us
    dot_general x2, matrix products, body(): jnp.einsum('scd,df->scf', joined, w_gate, preferred_element_type=jnp.floa...  14.8 us
    all_to_all x2, starting transfers between devices, body(): lax.all_to_all(outgoing, 'exp', split_axis=0, concat_axis=0, tiled=True)  10.8 us
    all_to_all x2, starting transfers between devices, body(): lax.all_to_all(result, 'exp', split_axis=0, concat_axis=0, tiled=True)  10.2 us
    dot_general x2, matrix products, body(): jnp.einsum('rec,ecd->rd', combine[:, :, lo:hi], part.astype(jnp.float32),...  8.91 us
  transfers between devices with their start and end apart: 7, of which 5 were waited for; matrix products, arithmetic and copies ran while one was open for 31% of the time, Pallas kernels for 0%

profile of v16, /device:TPU:1, one launch (start us, length us, event | category | flops | bytes accessed | tf_op | source)
XLA Modules:
  0.0 245.2 jit_solution(8125029657732040871)
XLA Ops:
  6.5 0.7 all-gather.3.cloned.1.call-update
  7.3 0.8 copy.24
  8.4 0.7 broadcast_multiply_fusion
  9.3 1.7 reduce-window.6
  11.5 3.4 %scatter_custom_fusion = s32[1152]{0:T(1024)S(1)} fusion(s32[768]{0:T(1024)S(1)} %fusion.84, s32[768]{0:T(1024)S(1)} %add_select_fusion, s32[]{:T(128)} %constant.13.clone.1), kind=kCustom, calls=%fused_computation.80 | custom fusion | bytes 4612 | tf_op jit(solution)/shard_map/scatter | solution.py:30
  15.0 51.1 %all-gather.3.cloned.1.call-done = bf16[2048,2048]{1,0:T(8,128)(2,1)} async-done(((bf16[64,2048]{1,0:T(8,128)(2,1)}), bf16[2048,2048]{1,0:T(8,128)(2,1)}) %all-gather.3.cloned.1.call-update) | async-done | bytes 8388624 | tf_op jit(solution)/shard_map/all_gather | solution.py:35
  66.1 4.8 %fusion.88 = f32[128,2048]{1,0:T(8,128)S(1)} fusion(bf16[128,2048]{1,0:T(8,128)(2,1)} %param.12, bf16[2048,2048]{1,0:T(8,128)(2,1)} %all-gather.3.cloned.1.call-done), kind=kOutput, calls=%fused_computation.90 | convolution fusion | flops 1073741824 | bytes 9961472 | tf_op jit(solution)/shard_map/dot_general | solution.py:33
  71.2 1.0 fusion.55
  72.5 3.2 %convolution_convert_fusion.1 = bf16[32,16,2048]{2,1,0:T(8,128)(2,1)} fusion(bf16[128,2048]{1,0:T(8,128)(2,1)} %fusion.55, pred[32,36,128]{2,1,0:T(8,128)(4,1)S(1)} %iota_compare_fusion), kind=kOutput, calls=%fused_computation.20 | convolution fusion | flops 269484032 | bytes 2686976 | tf_op jit(solution)/shard_map/ecr,rd->ecd/dot_general | solution.py:49
  75.7 5.5 %all-to-all-start = ((bf16[32,16,2048]{2,1,0:T(8,128)(2,1)}), bf16[32,16,2048]{2,1,0:T(8,128)(2,1)}, u32[]{:S(2)}, u32[]{:S(2)}) async-start(bf16[32,16,2048]{2,1,0:T(8,128)(2,1)} %convolution_convert_fusion.1), calls=%async_computation | async-start | bytes 4194304 | tf_op jit(solution)/shard_map/all_to_all | solution.py:52
  81.3 0.8 convolution_convert_fusion
  82.1 3.2 %copy.34 = bf16[32,20,2048]{2,1,0:T(8,128)(2,1)} copy(bf16[32,20,2048]{2,0,1:T(8,128)(2,1)S(1)} %convolution_convert_fusion) | data formatting | bytes 5242880 | tf_op jit(solution)/shard_map/convert_element_type | solution.py:51
  85.3 24.3 %all-to-all-done = bf16[32,16,2048]{2,1,0:T(8,128)(2,1)} async-done(((bf16[32,16,2048]{2,1,0:T(8,128)(2,1)}), bf16[32,16,2048]{2,1,0:T(8,128)(2,1)}, u32[]{:S(2)}, u32[]{:S(2)}) %all-to-all-start) | async-done | bytes 2097184 | tf_op jit(solution)/shard_map/all_to_all | solution.py:52
  109.6 5.3 %all-to-all-start.2 = ((bf16[32,20,2048]{2,1,0:T(8,128)(2,1)}), bf16[32,20,2048]{2,1,0:T(8,128)(2,1)}, u32[]{:S(2)}, u32[]{:S(2)}) async-start(bf16[32,20,2048]{2,1,0:T(8,128)(2,1)} %copy.34), calls=%async_computation.2 | async-start | bytes 6291456 | tf_op jit(solution)/shard_map/all_to_all | solution.py:52
  115.1 2.9 %fusion.89 = f32[512,352]{0,1:T(8,128)S(1)} fusion(bf16[512,2048]{1,0:T(8,128)(2,1)} %all-gather.5.cloned.1.call-done, bf16[2048,352]{0,1:T(8,128)(2,1)} %param.21), kind=kOutput, calls=%fused_computation.91 | convolution fusion | flops 738197504 | bytes 4259840 | tf_op jit(solution)/shard_map/dot_general | solution.py:81
  118.0 6.2 %fusion.52 = f32[512,2048]{1,0:T(8,128)} fusion(bf16[2048,352]{0,1:T(8,128)(2,1)S(1)} %copy-done, bf16[512,2048]{1,0:T(8,128)(2,1)} %all-gather.5.cloned.1.call-done, bf16[2048,352]{0,1:T(8,128)(2,1)} %param.22, f32[512,352]{0,1:T(8,128)S(1)} %fusion.89), kind=kOutput, calls=%fused_computation.38 | convolution fusion | flops 1477476352 | bytes 9895936 | tf_op jit(solution)/shard_map/dot_general | solution.py:84
  124.2 6.5 %fusion.10 = f32[32,16,1408]{2,1,0:T(8,128)S(1)} fusion(bf16[32,16,2048]{2,1,0:T(8,128)(2,1)} %all-to-all-done, bf16[1,2048,1408]{2,1,0:T(8,128)(2,1)} %param.18), kind=kOutput, calls=%fused_computation.12 | convolution fusion | flops 2952790016 | bytes 10747904 | tf_op jit(solution)/shard_map/scd,df->scf/dot_general | solution.py:55
  130.8 6.8 %fusion.24 = bf16[32,16,1408]{2,1,0:T(8,128)(2,1)S(1)} fusion(bf16[32,16,2048]{2,1,0:T(8,128)(2,1)} %all-to-all-done, bf16[1,2048,1408]{2,1,0:T(8,128)(2,1)} %param.19, f32[32,16,1408]{2,1,0:T(8,128)S(1)} %fusion.10), kind=kOutput, calls=%fused_computation.19 | convolution fusion | flops 2957115392 | bytes 12189696 | tf_op jit(solution)/shard_map/scd,df->scf/dot_general | solution.py:56
  137.7 3.6 %fusion.27 = bf16[32,16,2048]{2,0,1:T(8,128)(2,1)S(1)} fusion(bf16[1,1408,2048]{2,1,0:T(8,128)(2,1)S(1)} %bitcast.77, bf16[32,16,1408]{2,1,0:T(8,128)(2,1)S(1)} %fusion.24), kind=kOutput, calls=%fused_computation.21 | convolution fusion | flops 2953838592 | bytes 9306112 | tf_op jit(solution)/shard_map/scf,fd->scd/dot_general | solution.py:58
  141.3 2.5 %copy.31 = bf16[32,16,2048]{2,1,0:T(8,128)(2,1)} copy(bf16[32,16,2048]{2,0,1:T(8,128)(2,1)S(1)} %fusion.27) | data formatting | bytes 4194304 | tf_op jit(solution)/shard_map/convert_element_type | solution.py:60
  143.8 11.0 %all-to-all-done.2 = bf16[32,20,2048]{2,1,0:T(8,128)(2,1)} async-done(((bf16[32,20,2048]{2,1,0:T(8,128)(2,1)}), bf16[32,20,2048]{2,1,0:T(8,128)(2,1)}, u32[]{:S(2)}, u32[]{:S(2)}) %all-to-all-start.2) | async-done | bytes 2621472 | tf_op jit(solution)/shard_map/all_to_all | solution.py:52
  154.8 5.0 %all-to-all-start.1 = ((bf16[32,16,2048]{2,1,0:T(8,128)(2,1)}), bf16[32,16,2048]{2,1,0:T(8,128)(2,1)}, u32[]{:S(2)}, u32[]{:S(2)}) async-start(bf16[32,16,2048]{2,1,0:T(8,128)(2,1)} %copy.31), calls=%async_computation.1 | async-start | bytes 4194304 | tf_op jit(solution)/shard_map/all_to_all | solution.py:61
  159.8 8.3 %fusion.8 = f32[32,20,1408]{2,0,1:T(8,128)S(1)} fusion(bf16[1,2048,1408]{2,1,0:T(8,128)(2,1)} %param.18, bf16[32,20,2048]{2,1,0:T(8,128)(2,1)} %all-to-all-done.2), kind=kOutput, calls=%fused_computation.10 | convolution fusion | flops 3690987520 | bytes 11993088 | tf_op jit(solution)/shard_map/scd,df->scf/dot_general | solution.py:55
  168.0 8.6 %fusion.18 = bf16[32,20,1408]{2,0,1:T(8,128)(2,1)S(1)} fusion(bf16[1,2048,1408]{2,1,0:T(8,128)(2,1)} %param.19, f32[32,20,1408]{2,0,1:T(8,128)S(1)} %fusion.8, bf16[32,20,2048]{2,1,0:T(8,128)(2,1)} %all-to-all-done.2), kind=kOutput, calls=%fused_computation.16 | convolution fusion | flops 3696394240 | bytes 13795328 | tf_op jit(solution)/shard_map/scd,df->scf/dot_general | solution.py:56
  176.7 4.4 %fusion.21 = bf16[32,20,2048]{2,0,1:T(8,128)(2,1)S(1)} fusion(bf16[32,20,1408]{2,0,1:T(8,128)(2,1)S(1)} %fusion.18, bf16[1,1408,2048]{2,1,0:T(8,128)(2,1)S(1)} %bitcast.79), kind=kOutput, calls=%fused_computation.17 | convolution fusion | flops 3692298240 | bytes 10190848 | tf_op jit(solution)/shard_map/scf,fd->scd/dot_general | solution.py:58
  181.1 3.2 %copy.37 = bf16[32,20,2048]{2,1,0:T(8,128)(2,1)} copy(bf16[32,20,2048]{2,0,1:T(8,128)(2,1)S(1)} %fusion.21) | data formatting | bytes 5242880 | tf_op jit(solution)/shard_map/convert_element_type | solution.py:60
  184.3 3.8 %all-to-all-done.1 = bf16[32,16,2048]{2,1,0:T(8,128)(2,1)} async-done(((bf16[32,16,2048]{2,1,0:T(8,128)(2,1)}), bf16[32,16,2048]{2,1,0:T(8,128)(2,1)}, u32[]{:S(2)}, u32[]{:S(2)}) %all-to-all-start.1) | async-done | bytes 2097184 | tf_op jit(solution)/shard_map/all_to_all | solution.py:61
  188.1 5.3 %all-to-all-start.3 = ((bf16[32,20,2048]{2,1,0:T(8,128)(2,1)}), bf16[32,20,2048]{2,1,0:T(8,128)(2,1)}, u32[]{:S(2)}, u32[]{:S(2)}) async-start(bf16[32,20,2048]{2,1,0:T(8,128)(2,1)} %copy.37), calls=%async_computation.3 | async-start | bytes 6291456 | tf_op jit(solution)/shard_map/all_to_all | solution.py:61
  193.7 3.6 %scatter_custom_fusion.1 = f32[1152]{0:T(1024)S(1)} fusion(s32[768]{0:T(1024)S(1)} %fusion.84, f32[768]{0:T(1024)S(1)} %reshape.80, f32[]{:T(128)} %constant.36.clone.1), kind=kCustom, calls=%fused_computation.78 | custom fusion | bytes 4612 | tf_op jit(solution)/shard_map/scatter | solution.py:62
  197.5 3.5 %convolution_bitcast_fusion = f32[128,2048]{1,0:T(8,128)S(1)} fusion(bf16[32,16,2048]{2,1,0:T(8,128)(2,1)} %all-to-all-done.1, f32[32,36]{0,1:T(8,128)S(1)} %copy.29, s32[32,36]{0,1:T(8,128)S(1)} %copy.27), kind=kOutput, calls=%fused_computation.25 | convolution fusion | flops 805601280 | bytes 3154944 | tf_op jit(solution)/shard_map/rec,ecd->rd/dot_general | solution.py:69
  201.1 32.2 %all-to-all-done.3 = bf16[32,20,2048]{2,1,0:T(8,128)(2,1)} async-done(((bf16[32,20,2048]{2,1,0:T(8,128)(2,1)}), bf16[32,20,2048]{2,1,0:T(8,128)(2,1)}, u32[]{:S(2)}, u32[]{:S(2)}) %all-to-all-start.3) | async-done | bytes 2621472 | tf_op jit(solution)/shard_map/all_to_all | solution.py:61
  233.3 5.4 %fusion.44 = bf16[128,2048]{1,0:T(8,128)(2,1)} fusion(f32[128,2048]{1,0:T(8,128)} %reduce-scatter.2.cloned.1.call-done, f32[128,2048]{1,0:T(8,128)S(1)} %convolution_bitcast_fusion, bf16[32,20,2048]{2,1,0:T(8,128)(2,1)} %all-to-all-done.3, bf16[128,2048]{1,0:T(8,128)(2,1)S(1)} %get-tuple-element.12, f32[32,36]{0,1:T(8,128)S(1)} %copy.29, s32[32,36]{0,1:T(8,128)S(1)} %copy.27), kind=kOutput, calls=%fused_computation.29 | convolution fusion | flops 1008238592 | bytes 5776384 | tf_op jit(solution)/shard_map/rec,ecd->rd/dot_general | solution.py:69
  (50 shorter events, 2.5 us)
Async XLA Ops:
  6.5 111.5 %copy-start = (bf16[2048,352]{0,1:T(8,128)(2,1)S(1)}, bf16[2048,352]{0,1:T(8,128)(2,1)}, u32[]{:S(2)}) copy-start(bf16[2048,352]{0,1:T(8,128)(2,1)} %param.23) | copy-start | bytes 4325380
  6.5 59.5 %all-gather.3.cloned.1.call-start = ((), (), s32[]{:S(2)}) async-start(), calls=%async_computation.5 | async-start | bytes 8650752 | tf_op jit(solution)/shard_map/all_gather | solution.py:35
  7.3 107.8 %all-gather.5.cloned.1.call-start = ((), (), s32[]{:S(2)}) async-start(), calls=%async_computation.6 | async-start | bytes 2621440 | tf_op jit(solution)/shard_map/all_gather | solution.py:79
  14.9 55.9 %copy-start.3 = (bf16[128,2048]{1,0:T(8,128)(2,1)S(1)}, bf16[128,2048]{1,0:T(8,128)(2,1)}, u32[]{:S(2)}) copy-start(bf16[128,2048]{1,0:T(8,128)(2,1)} %param.13) | copy-start | bytes 1572868
  14.9 56.2 %copy-start.4 = (f32[2048]{0:T(1024)S(1)}, f32[2048]{0:T(1024)}, u32[]{:S(2)}) copy-start(f32[2048]{0:T(1024)} %param.15) | copy-start | bytes 24580
  72.5 8.7 %copy-start.2 = (bf16[128,2048]{1,0:T(8,128)(2,1)S(1)}, bf16[128,2048]{1,0:T(8,128)(2,1)}, u32[]{:S(2)}) copy-start(bf16[128,2048]{1,0:T(8,128)(2,1)} %fusion.55) | copy-start | bytes 1572868
  75.7 33.9 %all-to-all-start = ((bf16[32,16,2048]{2,1,0:T(8,128)(2,1)}), bf16[32,16,2048]{2,1,0:T(8,128)(2,1)}, u32[]{:S(2)}, u32[]{:S(2)}) async-start(bf16[32,16,2048]{2,1,0:T(8,128)(2,1)} %convolution_convert_fusion.1), calls=%async_computation | async-start | bytes 4194304 | tf_op jit(solution)/shard_map/all_to_all | solution.py:52
  109.6 45.2 %all-to-all-start.2 = ((bf16[32,20,2048]{2,1,0:T(8,128)(2,1)}), bf16[32,20,2048]{2,1,0:T(8,128)(2,1)}, u32[]{:S(2)}, u32[]{:S(2)}) async-start(bf16[32,20,2048]{2,1,0:T(8,128)(2,1)} %copy.34), calls=%async_computation.2 | async-start | bytes 6291456 | tf_op jit(solution)/shard_map/all_to_all | solution.py:52
  114.8 118.5 %reduce-scatter.2.cloned.1.call-start = ((), (), s32[]{:S(2)}) async-start(), calls=%async_computation.7 | async-start | bytes 5242880 | tf_op jit(solution)/shard_map/reduce_scatter | solution.py:87
  124.2 13.4 %slice-start = ((s8[5767168]{0:T(1024)(128)(4,1)}), s8[4194304]{0:T(1024)(128)(4,1)S(1)}, s32[]{:S(2)}) async-start(s8[5767168]{0:T(1024)(128)(4,1)} %bitcast.76), calls=%async_computation.8 | async-start | bytes 8388608
  130.8 6.9 %slice-start.1 = ((s8[5767168]{0:T(1024)(128)(4,1)}), s8[1572864]{0:T(1024)(128)(4,1)S(1)}, s32[]{:S(2)}) async-start(s8[5767168]{0:T(1024)(128)(4,1)} %bitcast.76), calls=%async_computation.9 | async-start | bytes 3145728
  154.8 33.3 %all-to-all-start.1 = ((bf16[32,16,2048]{2,1,0:T(8,128)(2,1)}), bf16[32,16,2048]{2,1,0:T(8,128)(2,1)}, u32[]{:S(2)}, u32[]{:S(2)}) async-start(bf16[32,16,2048]{2,1,0:T(8,128)(2,1)} %copy.31), calls=%async_computation.1 | async-start | bytes 4194304 | tf_op jit(solution)/shard_map/all_to_all | solution.py:61
  159.7 16.9 %slice-start.2 = ((s8[5767168]{0:T(1024)(128)(4,1)}), s8[4194304]{0:T(1024)(128)(4,1)S(1)}, s32[]{:S(2)}) async-start(s8[5767168]{0:T(1024)(128)(4,1)} %bitcast.78), calls=%async_computation.10 | async-start | bytes 8388608
  168.0 8.6 %slice-start.3 = ((s8[5767168]{0:T(1024)(128)(4,1)}), s8[1572864]{0:T(1024)(128)(4,1)S(1)}, s32[]{:S(2)}) async-start(s8[5767168]{0:T(1024)(128)(4,1)} %bitcast.78), calls=%async_computation.11 | async-start | bytes 3145728
  184.3 9.1 %copy-start.5 = (f32[128,6]{0,1:T(8,128)S(1)}, f32[128,6]{0,1:T(8,128)}, u32[]{:S(2)}) copy-start(f32[128,6]{0,1:T(8,128)} %param.17) | copy-start | bytes 9220
  188.1 45.2 %all-to-all-start.3 = ((bf16[32,20,2048]{2,1,0:T(8,128)(2,1)}), bf16[32,20,2048]{2,1,0:T(8,128)(2,1)}, u32[]{:S(2)}, u32[]{:S(2)}) async-start(bf16[32,20,2048]{2,1,0:T(8,128)(2,1)} %copy.37), calls=%async_computation.3 | async-start | bytes 6291456 | tf_op jit(solution)/shard_map/all_to_all | solution.py:61
  197.5 41.1 %copy-start.1 = (bf16[2048,352]{0,1:T(8,128)(2,1)S(1)}, bf16[2048,352]{0,1:T(8,128)(2,1)}, u32[]{:S(2)}) copy-start(bf16[2048,352]{0,1:T(8,128)(2,1)} %param.23) | copy-start | bytes 4325380
Sparse Core Ops, SparseCore 0:
  9.6 56.3 all-gather.2
  72.3 30.2 all-gather.4
  124.3 48.3 reduce-scatter.1
